TPU v7x, 32 devices: a whole 2x2x4 slice. The times are simulated.
32 devices in a mesh: dp: 8 (over y, x, core), mp: 4 (over z).
Axes of the slice: x: 2, y: 2, z: 4, core: 2. Of those that a mesh axis runs over, the one named last changes fastest.
Arguments:
- tokens: bfloat16 [512, 32, 1024], P('mp', 'dp'), may hold values from -6 to 6
- timesteps: int32 [32], P('dp'), may hold values from 0 to 4999
- buckets: int32 [32], P('dp'), may hold values from 0 to 31
- counts: int32 [8], replicated, may hold values from 1 to 4, as said below
- w_time: bfloat16 [1024, 1024], replicated, may hold values from -0.1875 to 0.1875
- table: float32 [32, 1024], replicated, may hold values from -3 to 3
- w_qkv: bfloat16 [3, 1024, 1024], P(None, None, 'mp'), may hold values from -0.1875 to 0.1875
- b_qv: float32 [2, 1024], P(None, 'mp'), may hold values from -0.6 to 0.6
- w_out: bfloat16 [1024, 1024], P('mp'), may hold values from -0.5 to 0.5
- b_out: float32 [1024], replicated, may hold values from -2 to 2
- gain1: float32 [1024], replicated, may hold values from 0.5 to 1.5
- shift1: float32 [1024], replicated, may hold values from -1.2 to 1.2
- w_up: bfloat16 [1024, 4096], P(None, 'mp'), may hold values from -0.1875 to 0.1875
- b_up: float32 [4096], P('mp'), may hold values from -3 to 3
- w_down: bfloat16 [4096, 1024], P('mp'), may hold values from -0.09375 to 0.09375
- b_down: float32 [1024], replicated, may hold values from -2 to 2
- gain2: float32 [1024], replicated, may hold values from 0.5 to 1.5
- shift2: float32 [1024], replicated, may hold values from -1.2 to 1.2
- cotangent: bfloat16 [512, 32, 1024], P('mp', 'dp'), may hold values from -6 to 6
Outputs:
- output: bfloat16 [512, 32, 1024], P('mp', 'dp')
- grad_tokens: float32 [512, 32, 1024], P('mp', 'dp')
- grad_w_time: float32 [1024, 1024], P(None, ('dp', 'mp'))
- grad_table: float32 [32, 1024], P(None, ('dp', 'mp'))
- grad_w_qkv: float32 [3, 1024, 1024], P(None, 'dp', 'mp')
- grad_b_qv: float32 [2, 1024], P(None, ('dp', 'mp'))
- grad_w_out: float32 [1024, 1024], P('mp', 'dp')
- grad_b_out: float32 [1024], P(('dp', 'mp'))
- grad_gain1: float32 [1024], P(('dp', 'mp'))
- grad_shift1: float32 [1024], P(('dp', 'mp'))
- grad_w_up: float32 [1024, 4096], P('dp', 'mp')
- grad_b_up: float32 [4096], P(('dp', 'mp'))
- grad_w_down: float32 [4096, 1024], P('mp', 'dp')
- grad_b_down: float32 [1024], P(('dp', 'mp'))
- grad_gain2: float32 [1024], P(('dp', 'mp'))
- grad_shift2: float32 [1024], P(('dp', 'mp'))
Inputs may be any that keep to these rules, and one draw needn't show every extreme that they name: Slot s of group g holds a live item iff s < counts[g]; in every draw some group has all 4 slots live.
All inputs are finite; a program needn't handle non-finite values.
Results may differ from a plain program's by a relative error of at most 0.025.
Values may be sent and summed in bfloat16 or wider, within the bound.
No kernel may reach another device: no remote copies, remote signals or barrier semaphores. Data moves between devices by JAX's collectives and lax.ppermute only.
A program may use at most 192 MiB of HBM per device.

v0:
```python
import math

import jax
import jax.numpy as jnp
from jax import lax
from jax.sharding import PartitionSpec as P

HD = 64
MB = 2


def layer_norm(values, gain, shift):
    center = values - jnp.mean(values, axis=-1, keepdims=True)
    spread = jnp.mean(center * center, axis=-1, keepdims=True)
    return center * lax.rsqrt(spread + 1e-05) * gain + shift


def exact_gelu(values):
    return jax.nn.gelu(values, approximate=False)


def sinusoid(steps, model_width):
    half_width = model_width // 2
    freqs = jnp.exp(-math.log(10000.0) * jnp.arange(half_width, dtype=jnp.float32) / half_width)
    angles = steps.astype(jnp.float32)[:, None] * freqs[None, :]
    return jnp.concatenate([jnp.sin(angles), jnp.cos(angles)], axis=-1)


def on_device(
    tokens,
    timesteps,
    buckets,
    counts,
    w_time,
    table,
    w_qkv,
    b_qv,
    w_out,
    b_out,
    gain1,
    shift1,
    w_up,
    b_up,
    w_down,
    b_down,
    gain2,
    shift2,
    cotangent,
):
    high = lax.Precision.HIGHEST
    f32 = jnp.float32
    bf16 = jnp.bfloat16
    split_count = lax.axis_size("mp")
    groups = lax.axis_size("dp")
    model_width = w_time.shape[0]
    head_cols = w_qkv.shape[2]
    unit_cols = w_up.shape[1]
    slot_count = tokens.shape[1]
    per_micro = slot_count // MB
    heads_here = head_cols // HD
    group_here = lax.axis_index("dp")
    block_here = lax.axis_index("mp")
    count_here = jnp.sum(jnp.where(jnp.arange(groups) == group_here, counts, 0))
    total_live = jnp.sum(counts).astype(f32)
    weighting = 1.0 / total_live
    live_all = (jnp.arange(slot_count) < count_here).astype(f32)
    sinus_all = sinusoid(timesteps, model_width).astype(bf16)
    onehot_all = (buckets[:, None] == jnp.arange(table.shape[0])[None, :]).astype(f32)
    proj_bias = jnp.stack([b_qv[0], jnp.zeros_like(b_qv[0]), b_qv[1]])
    acc_w_time = jnp.zeros((model_width, model_width), f32)
    acc_table = jnp.zeros(table.shape, f32)
    acc_w_qkv = jnp.zeros(w_qkv.shape, f32)
    acc_b_qv = jnp.zeros(b_qv.shape, f32)
    acc_w_out = jnp.zeros(w_out.shape, f32)
    acc_w_up = jnp.zeros(w_up.shape, f32)
    acc_b_up = jnp.zeros(b_up.shape, f32)
    acc_w_down = jnp.zeros(w_down.shape, f32)
    acc_vectors = jnp.zeros((6, model_width), f32)
    outputs = []
    input_grads = []
    for micro_step in range(MB):
        offset = micro_step * per_micro
        token_part = tokens[:, offset : offset + per_micro].astype(f32)
        sinus_part = sinus_all[offset : offset + per_micro]
        onehot_part = onehot_all[offset : offset + per_micro]
        live_mask = live_all[offset : offset + per_micro]
        time_embed = jnp.dot(sinus_part, w_time, preferred_element_type=f32)
        time_embed = time_embed + jnp.dot(onehot_part, table, precision=high)
        start_rows = token_part + time_embed[None]
        hidden = lax.all_gather(start_rows.astype(bf16), "mp", axis=0, tiled=True)
        length = hidden.shape[0]
        projected = jnp.einsum("lnd,cde->clne", hidden, w_qkv, preferred_element_type=f32)
        projected = (projected + proj_bias[:, None, None, :]).astype(bf16)
        split_heads = projected.reshape(3, length, per_micro, heads_here, HD)
        queries = split_heads[0]
        key_rows = split_heads[1]
        values = split_heads[2]
        scores = (
            jnp.einsum("qnhe,knhe->nhqk", queries, key_rows, preferred_element_type=f32) * 0.125
        )
        row_max = jnp.max(scores, axis=-1, keepdims=True)
        expos = jnp.exp(scores - row_max)
        summed = jnp.sum(expos, axis=-1, keepdims=True)
        log_total = row_max + jnp.log(summed)
        attend = expos / summed
        context = jnp.einsum(
            "nhqk,knhe->qnhe", attend.astype(bf16), values, preferred_element_type=f32
        )
        context = context.reshape(length, per_micro, head_cols).astype(bf16)
        mixing = (
            lax.psum_scatter(
                jnp.einsum("lnh,hd->lnd", context, w_out, preferred_element_type=f32).astype(
                    jnp.bfloat16
                ),
                "mp",
                scatter_dimension=0,
                tiled=True,
            ).astype(jnp.float32)
            + b_out
        )
        normed, first_pull = jax.vjp(layer_norm, start_rows + mixing, gain1, shift1)
        normed_all = lax.all_gather(normed.astype(bf16), "mp", axis=0, tiled=True)
        upward = jnp.einsum("lnd,df->lnf", normed_all, w_up, preferred_element_type=f32) + b_up
        active_full, gelu_pull = jax.vjp(exact_gelu, upward)
        active = active_full.astype(bf16)
        branch = (
            lax.psum_scatter(
                jnp.einsum("lnf,fd->lnd", active, w_down, preferred_element_type=f32).astype(
                    jnp.bfloat16
                ),
                "mp",
                scatter_dimension=0,
                tiled=True,
            ).astype(jnp.float32)
            + b_down
        )
        result, second_pull = jax.vjp(layer_norm, normed + branch, gain2, shift2)
        outputs.append(result.astype(bf16))
        grad_result = (
            cotangent[:, offset : offset + per_micro].astype(f32) * live_mask[None, :, None]
        )
        grad_second, grad_gain2, grad_shift2 = second_pull(grad_result)
        branch_grad = grad_second.astype(bf16)
        branch_all = lax.all_gather(branch_grad, "mp", axis=0, tiled=True)
        acc_w_down = acc_w_down + jnp.einsum(
            "lnf,lnd->fd", active, branch_all, preferred_element_type=f32
        )
        grad_active = jnp.einsum("lnd,fd->lnf", branch_all, w_down, preferred_element_type=f32)
        up_grad = gelu_pull(grad_active)[0].astype(bf16)
        acc_b_up = acc_b_up + jnp.sum(up_grad.astype(f32), axis=(0, 1))
        acc_w_up = acc_w_up + jnp.einsum(
            "lnd,lnf->df", normed_all, up_grad, preferred_element_type=f32
        )
        grad_normed = grad_second + lax.psum_scatter(
            jnp.einsum("lnf,df->lnd", up_grad, w_up, preferred_element_type=f32).astype(
                jnp.bfloat16
            ),
            "mp",
            scatter_dimension=0,
            tiled=True,
        ).astype(jnp.float32)
        grad_first, grad_gain1, grad_shift1 = first_pull(grad_normed)
        mixing_grad = grad_first.astype(bf16)
        mixing_all = lax.all_gather(mixing_grad, "mp", axis=0, tiled=True)
        acc_w_out = acc_w_out + jnp.einsum(
            "lnh,lnd->hd", context, mixing_all, preferred_element_type=f32
        )
        context_grad = jnp.einsum("lnd,hd->lnh", mixing_all, w_out, preferred_element_type=f32)
        context_grad = context_grad.astype(bf16).reshape(length, per_micro, heads_here, HD)
        again = jnp.einsum("qnhe,knhe->nhqk", queries, key_rows, preferred_element_type=f32) * 0.125
        attend_again = jnp.exp(again - log_total)
        grad_attend = jnp.einsum(
            "qnhe,knhe->nhqk", context_grad, values, preferred_element_type=f32
        )
        grad_values = jnp.einsum(
            "nhqk,qnhe->knhe", attend_again.astype(bf16), context_grad, preferred_element_type=f32
        )
        row_dot = jnp.sum(attend_again * grad_attend, axis=-1, keepdims=True)
        score_grad = (attend_again * (grad_attend - row_dot)).astype(bf16)
        grad_queries = (
            jnp.einsum("nhqk,knhe->qnhe", score_grad, key_rows, preferred_element_type=f32) * 0.125
        )
        grad_keys = (
            jnp.einsum("nhqk,qnhe->knhe", score_grad, queries, preferred_element_type=f32) * 0.125
        )
        proj_grad = jnp.stack([grad_queries, grad_keys, grad_values]).astype(bf16)
        proj_grad = proj_grad.reshape(3, length, per_micro, head_cols)
        bias_sums = jnp.sum(proj_grad.astype(f32), axis=(1, 2))
        acc_b_qv = acc_b_qv + jnp.stack([bias_sums[0], bias_sums[2]])
        acc_w_qkv = acc_w_qkv + jnp.einsum(
            "lnd,clne->cde", hidden, proj_grad, preferred_element_type=f32
        )
        grad_start = grad_first + lax.psum_scatter(
            jnp.einsum("clne,cde->lnd", proj_grad, w_qkv, preferred_element_type=f32).astype(
                jnp.bfloat16
            ),
            "mp",
            scatter_dimension=0,
            tiled=True,
        ).astype(jnp.float32)
        input_grads.append(grad_start)
        time_grad = jnp.sum(grad_start, axis=0)
        acc_w_time = acc_w_time + jnp.einsum(
            "nd,ne->de", sinus_part.astype(f32), time_grad, precision=high
        )
        acc_table = acc_table + jnp.einsum("nb,nd->bd", onehot_part, time_grad, precision=high)
        acc_vectors = acc_vectors + jnp.stack(
            [
                jnp.sum(mixing_grad.astype(f32), axis=(0, 1)),
                grad_gain1,
                grad_shift1,
                jnp.sum(branch_grad.astype(f32), axis=(0, 1)),
                grad_gain2,
                grad_shift2,
            ]
        )
    output = jnp.concatenate(outputs, axis=1)
    grad_tokens = jnp.concatenate(input_grads, axis=1)
    qkv_sum, out_sum, upper_sum, lower_sum = (
        lax.psum_scatter(acc_w_qkv * weighting, "dp", scatter_dimension=1, tiled=True),
        lax.psum_scatter(
            (acc_w_out * weighting)[:, :, None], "dp", scatter_dimension=1, tiled=True
        ),
        lax.psum_scatter((acc_w_up * weighting)[None], "dp", scatter_dimension=1, tiled=True),
        lax.psum_scatter(
            (acc_w_down * weighting)[:, :, None], "dp", scatter_dimension=1, tiled=True
        ),
    )
    full_qv = lax.dynamic_update_slice(
        jnp.zeros((2, model_width), f32), acc_b_qv, (jnp.int32(0), block_here * head_cols)
    )
    full_up = lax.dynamic_update_slice(
        jnp.zeros((unit_cols * split_count,), f32), acc_b_up, (block_here * unit_cols,)
    )
    time_sum, table_sum, qv_sum, vector_sum, up_sum = (
        lax.psum_scatter(acc_w_time * weighting, ("dp", "mp"), scatter_dimension=1, tiled=True),
        lax.psum_scatter(acc_table * weighting, ("dp", "mp"), scatter_dimension=1, tiled=True),
        lax.psum_scatter(full_qv * weighting, ("dp", "mp"), scatter_dimension=1, tiled=True),
        lax.psum_scatter(acc_vectors * weighting, ("dp", "mp"), scatter_dimension=1, tiled=True),
        lax.psum_scatter(
            (full_up * weighting)[None], ("dp", "mp"), scatter_dimension=1, tiled=True
        ),
    )
    return (
        output,
        grad_tokens,
        time_sum,
        table_sum,
        qkv_sum,
        qv_sum,
        out_sum[:, :, 0],
        vector_sum[0],
        vector_sum[1],
        vector_sum[2],
        upper_sum[0],
        up_sum[0],
        lower_sum[:, :, 0],
        vector_sum[3],
        vector_sum[4],
        vector_sum[5],
    )


def solution(mesh):
    return jax.shard_map(
        on_device,
        mesh=mesh,
        in_specs=(
            P("mp", "dp", None),
            P("dp"),
            P("dp"),
            P(),
            P(),
            P(),
            P(None, None, "mp"),
            P(None, "mp"),
            P("mp", None),
            P(),
            P(),
            P(),
            P(None, "mp"),
            P("mp"),
            P("mp", None),
            P(),
            P(),
            P(),
            P("mp", "dp", None),
        ),
        out_specs=(
            P("mp", "dp", None),
            P("mp", "dp", None),
            P(None, ("dp", "mp")),
            P(None, ("dp", "mp")),
            P(None, "dp", "mp"),
            P(None, ("dp", "mp")),
            P("mp", "dp"),
            P(("dp", "mp")),
            P(("dp", "mp")),
            P(("dp", "mp")),
            P("dp", "mp"),
            P(("dp", "mp")),
            P("mp", "dp"),
            P(("dp", "mp")),
            P(("dp", "mp")),
            P(("dp", "mp")),
        ),
        check_vma=False,
    )
```

profile of v0, /device:TPU:0, one launch (start us, length us, event | category | flops | bytes accessed | tf_op | source)
XLA Modules:
  0.0 1696.1 jit_solution(2392259200255360863)
XLA Ops:
  8.8 2.5 fusion.157
  17.9 45.4 %all-gather.9.cloned.1.call-done = bf16[512,2,1024]{2,0,1:T(8,128)(2,1)} async-done(((bf16[128,2,1024]{2,0,1:T(8,128)(2,1)}), bf16[512,2,1024]{2,0,1:T(8,128)(2,1)}) %all-gather.9.cloned.1.call-update) | async-done | bytes 2097168 | tf_op jit(solution)/shard_map/all_gather | solution.py:90
  63.3 3.9 fusion.68
  77.1 33.1 %all-gather.13.cloned.1.call-done = bf16[512,2,1024]{2,0,1:T(8,128)(2,1)} async-done(((bf16[128,2,1024]{2,0,1:T(8,128)(2,1)}), bf16[512,2,1024]{2,0,1:T(8,128)(2,1)}) %all-gather.13.cloned.1.call-update) | async-done | bytes 2097168 | tf_op jit(solution)/shard_map/all_gather | solution.py:90
  110.2 3.9 fusion.69
  123.7 32.0 %reduce-scatter.26.cloned.1.call-done = bf16[128,2,1024]{2,0,1:T(8,128)(2,1)} async-done(((bf16[512,2,1024]{2,0,1:T(8,128)(2,1)}), bf16[128,2,1024]{2,0,1:T(8,128)(2,1)}) %reduce-scatter.26.cloned.1.call-update) | async-done | bytes 524304 | tf_op jit(solution)/shard_map/reduce_scatter | solution.py:111
  157.0 44.1 %reduce-scatter.30.cloned.1.call-done = bf16[128,2,1024]{2,0,1:T(8,128)(2,1)} async-done(((bf16[512,2,1024]{2,0,1:T(8,128)(2,1)}), bf16[128,2,1024]{2,0,1:T(8,128)(2,1)}) %reduce-scatter.30.cloned.1.call-update) | async-done | bytes 524304 | tf_op jit(solution)/shard_map/reduce_scatter | solution.py:111
  204.3 2.8 fusion.110
  208.2 44.4 %all-gather.15.cloned.1.call-done = bf16[512,2,1024]{2,0,1:T(8,128)(2,1)} async-done(((bf16[128,2,1024]{2,0,1:T(8,128)(2,1)}), bf16[512,2,1024]{2,0,1:T(8,128)(2,1)}) %all-gather.15.cloned.1.call-update) | async-done | bytes 2097168 | tf_op jit(solution)/shard_map/all_gather | solution.py:122
  252.6 5.8 fusion.50
  258.4 40.8 %all-gather.11.cloned.1.call-done = bf16[512,2,1024]{2,0,1:T(8,128)(2,1)} async-done(((bf16[128,2,1024]{2,0,1:T(8,128)(2,1)}), bf16[512,2,1024]{2,0,1:T(8,128)(2,1)}) %all-gather.11.cloned.1.call-update) | async-done | bytes 2097168 | tf_op jit(solution)/shard_map/all_gather | solution.py:122
  299.2 8.9 fusion.106
  308.1 20.7 %multiply_convert_fusion.3 = (bf16[512,2,1024]{2,0,1:T(8,128)(2,1)S(1)}, f32[512,2,1024]{2,0,1:T(8,128)}, bf16[512,2,1024]{2,0,1:T(8,128)(2,1)}, f32[512,2,1024]{2,0,1:T(8,128)}) fusion(f32[512,2,1024]{2,0,1:T(8,128)S(1)} %get-tuple-element.145, f32[1024]{0:T(1024)S(1)} %copy-done.64, u8[512,1024]{1,0:T(8,128)(4,1)S(1)} %get-tuple-element.49, ...), kind=kLoop, calls=%fused_computation.59 | loop fusion | flops 147849216 | bytes 23072768 | tf_op jit(solution)/shard_map/convert_element_type | solution.py:125
  330.2 3.6 fusion.60
  333.9 5.9 fusion.63
  341.4 3.4 fusion.156
  344.8 31.7 %reduce-scatter.28.cloned.1.call-done = bf16[128,2,1024]{2,0,1:T(8,128)(2,1)} async-done(((bf16[512,2,1024]{2,0,1:T(8,128)(2,1)}), bf16[128,2,1024]{2,0,1:T(8,128)(2,1)}) %reduce-scatter.28.cloned.1.call-update) | async-done | bytes 524304 | tf_op jit(solution)/shard_map/reduce_scatter | solution.py:127
  376.5 45.7 %reduce-scatter.32.cloned.1.call-done = bf16[128,2,1024]{2,0,1:T(8,128)(2,1)} async-done(((bf16[512,2,1024]{2,0,1:T(8,128)(2,1)}), bf16[128,2,1024]{2,0,1:T(8,128)(2,1)}) %reduce-scatter.32.cloned.1.call-update) | async-done | bytes 524304 | tf_op jit(solution)/shard_map/reduce_scatter | solution.py:127
  422.2 2.6 fusion.150
  426.4 2.3 fusion.149
  433.0 43.1 %all-gather.17.cloned.1.call-done = bf16[512,2,1024]{2,0,1:T(8,128)(2,1)} async-done(((bf16[128,2,1024]{2,0,1:T(8,128)(2,1)}), bf16[512,2,1024]{2,0,1:T(8,128)(2,1)}) %all-gather.17.cloned.1.call-update) | async-done | bytes 2097168 | tf_op jit(solution)/shard_map/all_gather | solution.py:144
  476.1 8.3 convert_reduce_fusion.1
  485.8 3.7 fusion.54
  489.8 32.4 %all-gather.21.cloned.1.call-done = bf16[512,2,1024]{2,0,1:T(8,128)(2,1)} async-done(((bf16[128,2,1024]{2,0,1:T(8,128)(2,1)}), bf16[512,2,1024]{2,0,1:T(8,128)(2,1)}) %all-gather.21.cloned.1.call-update) | async-done | bytes 2097168 | tf_op jit(solution)/shard_map/all_gather | solution.py:144
  522.1 8.3 convert_reduce_fusion
  531.8 3.7 fusion.57
  535.6 31.5 %reduce-scatter.34.cloned.1.call-done = bf16[128,2,1024]{2,0,1:T(8,128)(2,1)} async-done(((bf16[512,2,1024]{2,0,1:T(8,128)(2,1)}), bf16[128,2,1024]{2,0,1:T(8,128)(2,1)}) %reduce-scatter.34.cloned.1.call-update) | async-done | bytes 524304 | tf_op jit(solution)/shard_map/reduce_scatter | solution.py:154
  567.1 45.5 %reduce-scatter.38.cloned.1.call-done = bf16[128,2,1024]{2,0,1:T(8,128)(2,1)} async-done(((bf16[512,2,1024]{2,0,1:T(8,128)(2,1)}), bf16[128,2,1024]{2,0,1:T(8,128)(2,1)}) %reduce-scatter.38.cloned.1.call-update) | async-done | bytes 524304 | tf_op jit(solution)/shard_map/reduce_scatter | solution.py:154
  612.6 3.5 multiply_reduce_fusion.7
  624.5 41.2 %all-gather.19.cloned.1.call-done = bf16[512,2,1024]{2,0,1:T(8,128)(2,1)} async-done(((bf16[128,2,1024]{2,0,1:T(8,128)(2,1)}), bf16[512,2,1024]{2,0,1:T(8,128)(2,1)}) %all-gather.19.cloned.1.call-update) | async-done | bytes 2097168 | tf_op jit(solution)/shard_map/all_gather | solution.py:164
  665.7 2.3 convolution_convert_fusion.3
  668.0 5.0 fusion.91
  673.2 5.0 multiply_reduce_fusion.1
  678.2 4.7 multiply_convert_fusion.1
  686.0 3.8 fusion.88
  690.0 4.7 bitcast_convert_fusion.1
  695.0 16.8 all-gather.23.cloned.1.call-done
  711.8 2.3 convolution_convert_fusion.2
  714.1 5.0 fusion.94
  719.4 4.8 multiply_reduce_fusion
  724.1 4.8 multiply_convert_fusion
  731.9 3.8 fusion.90
  735.9 4.8 bitcast_convert_fusion
  743.6 6.7 fusion.164
  751.7 7.2 fusion.11
  759.1 4.8 fusion.163
  763.9 4.3 fusion.13
  771.3 5.7 fusion.32
  778.6 23.4 %reduce-scatter.40.cloned.1.call-done = bf16[128,2,1024]{2,0,1:T(8,128)(2,1)} async-done(((bf16[512,2,1024]{2,0,1:T(8,128)(2,1)}), bf16[128,2,1024]{2,0,1:T(8,128)(2,1)}) %reduce-scatter.40.cloned.1.call-update) | async-done | bytes 524304 | tf_op jit(solution)/shard_map/reduce_scatter | solution.py:193
  802.0 2.2 fusion.144
  805.6 6.6 fusion.31
  812.6 2.3 convolution_bitcast_fusion
  814.9 3.3 fusion.84
  820.2 4.1 add_multiply_fusion
  827.3 114.4 %reduce-scatter.58.cloned.1.call-done = f32[128,1]{1,0:T(8,128)} async-done(((f32[4096,1]{1,0:T(8,128)}), f32[128,1]{1,0:T(8,128)}) %reduce-scatter.58.cloned.1.call-update) | async-done | bytes 528
  943.1 133.0 %reduce-scatter.56.cloned.1.call-done = f32[32,6]{1,0:T(8,128)} async-done(((f32[1024,6]{1,0:T(8,128)}), f32[32,6]{1,0:T(8,128)}) %reduce-scatter.56.cloned.1.call-update) | async-done | bytes 784
  1080.7 46.5 %reduce-scatter.50.cloned.1.call-done = f32[1024,128,1]{0,1,2:T(8,128)} async-done(((f32[1024,1024,1]{0,1,2:T(8,128)}), f32[1024,128,1]{0,1,2:T(8,128)}) %reduce-scatter.50.cloned.1.call-update) | async-done | bytes 524304 | tf_op jit(solution)/shard_map/reduce_scatter | solution.py:225
  1129.2 52.9 %reduce-scatter.48.cloned.1.call-done = f32[1,128,1024]{1,2,0:T(8,128)} async-done(((f32[1,1024,1024]{1,2,0:T(8,128)}), f32[1,128,1024]{1,2,0:T(8,128)}) %reduce-scatter.48.cloned.1.call-update) | async-done | bytes 524304 | tf_op jit(solution)/shard_map/reduce_scatter | solution.py:224
  1184.1 134.7 %reduce-scatter.54.cloned.1.call-done = f32[32,2]{1,0:T(8,128)} async-done(((f32[1024,2]{1,0:T(8,128)}), f32[32,2]{1,0:T(8,128)}) %reduce-scatter.54.cloned.1.call-update) | async-done | bytes 272
  1321.7 2.7 copy.105
  1324.4 127.6 %reduce-scatter.52.cloned.1.call-done = f32[32,32]{1,0:T(8,128)} async-done(((f32[1024,32]{1,0:T(8,128)}), f32[32,32]{1,0:T(8,128)}) %reduce-scatter.52.cloned.1.call-update) | async-done | bytes 4112
  1453.3 44.6 %reduce-scatter.44.cloned.1.call-done = f32[3,128,256]{1,2,0:T(8,128)} async-done(((f32[3,1024,256]{1,2,0:T(8,128)}), f32[3,128,256]{1,2,0:T(8,128)}) %reduce-scatter.44.cloned.1.call-update) | async-done | bytes 393232 | tf_op jit(solution)/shard_map/reduce_scatter | solution.py:220
  1499.8 38.1 %reduce-scatter.46.cloned.1.call-done = f32[256,128,1]{1,0,2:T(8,128)} async-done(((f32[256,1024,1]{1,0,2:T(8,128)}), f32[256,128,1]{1,0,2:T(8,128)}) %reduce-scatter.46.cloned.1.call-update) | async-done | bytes 131088 | tf_op jit(solution)/shard_map/reduce_scatter | solution.py:221
  1537.9 151.3 %reduce-scatter.42.cloned.1.call-done = f32[1024,32]{0,1:T(8,128)} async-done(((f32[1024,1024]{0,1:T(8,128)}), f32[1024,32]{0,1:T(8,128)}) %reduce-scatter.42.cloned.1.call-update) | async-done | bytes 131088 | tf_op jit(solution)/shard_map/reduce_scatter | solution.py:236
  (299 shorter events, 91.0 us)
Async XLA Ops:
  7.2 245.4 %copy-start = (bf16[1024,1024]{1,0:T(8,128)(2,1)S(1)}, bf16[1024,1024]{1,0:T(8,128)(2,1)}, u32[]{:S(2)}) copy-start(bf16[1024,1024]{1,0:T(8,128)(2,1)} %param.31) | copy-start | bytes 6291460
  7.2 6.2 copy-start.53
  7.2 56.1 %all-gather.9.cloned.1.call-start = ((), (), s32[]{:S(2)}) async-start(), calls=%async_computation.17 | async-start | bytes 2621440 | tf_op jit(solution)/shard_map/all_gather | solution.py:90
  8.1 9.5 copy-start.62
  11.3 6.5 copy-start.67
  14.5 95.6 %all-gather.13.cloned.1.call-start = ((), (), s32[]{:S(2)}) async-start(), calls=%async_computation.21 | async-start | bytes 2621440 | tf_op jit(solution)/shard_map/all_gather | solution.py:90
  17.7 138.0 %reduce-scatter.26.cloned.1.call-start = ((), (), s32[]{:S(2)}) async-start(), calls=%async_computation.18 | async-start | bytes 2621440 | tf_op jit(solution)/shard_map/reduce_scatter | solution.py:111
  76.8 124.3 %reduce-scatter.30.cloned.1.call-start = ((), (), s32[]{:S(2)}) async-start(), calls=%async_computation.22 | async-start | bytes 2621440 | tf_op jit(solution)/shard_map/reduce_scatter | solution.py:111
  120.7 34.9 %copy-start.54 = (f32[1024]{0:T(1024)S(1)}, f32[1024]{0:T(1024)}, u32[]{:S(2)}) copy-start(f32[1024]{0:T(1024)} %param.28) | copy-start | bytes 12292
  121.5 82.7 %copy-start.55 = (f32[1024]{0:T(1024)S(1)}, f32[1024]{0:T(1024)}, u32[]{:S(2)}) copy-start(f32[1024]{0:T(1024)} %param.29) | copy-start | bytes 12292
  121.5 82.7 %copy-start.60 = (f32[1024]{0:T(1024)S(1)}, f32[1024]{0:T(1024)}, u32[]{:S(2)}) copy-start(f32[1024]{0:T(1024)} %param.30) | copy-start | bytes 12292
  123.7 128.9 %all-gather.15.cloned.1.call-start = ((), (), s32[]{:S(2)}) async-start(), calls=%async_computation.23 | async-start | bytes 2621440 | tf_op jit(solution)/shard_map/all_gather | solution.py:122
  207.2 92.1 %all-gather.11.cloned.1.call-start = ((), (), s32[]{:S(2)}) async-start(), calls=%async_computation.19 | async-start | bytes 2621440 | tf_op jit(solution)/shard_map/all_gather | solution.py:122
  207.7 91.5 %copy-start.64 = (f32[1024]{0:T(1024)S(1)}, f32[1024]{0:T(1024)}, u32[]{:S(2)}) copy-start(f32[1024]{0:T(1024)} %param.32) | copy-start | bytes 12292
  207.7 168.7 %reduce-scatter.28.cloned.1.call-start = ((), (), s32[]{:S(2)}) async-start(), calls=%async_computation.20 | async-start | bytes 2621440 | tf_op jit(solution)/shard_map/reduce_scatter | solution.py:127
  299.2 8.9 copy-start.24
  308.1 20.7 %copy-start.25 = (f32[512,2,1024]{2,0,1:T(8,128)}, f32[512,2,1024]{2,0,1:T(8,128)S(1)}, u32[]{:S(2)}) copy-start(f32[512,2,1024]{2,0,1:T(8,128)S(1)} %get-tuple-element.145) | copy-start | bytes 12582916
  308.1 22.0 %copy-start.69 = (bf16[1024,1024]{1,0:T(8,128)(2,1)S(1)}, bf16[1024,1024]{1,0:T(8,128)(2,1)}, u32[]{:S(2)}) copy-start(bf16[1024,1024]{1,0:T(8,128)(2,1)} %param.33) | copy-start | bytes 6291460
  333.8 88.3 %reduce-scatter.32.cloned.1.call-start = ((), (), s32[]{:S(2)}) async-start(), calls=%async_computation.24 | async-start | bytes 2621440 | tf_op jit(solution)/shard_map/reduce_scatter | solution.py:127
  333.9 6.2 copy-start.68
  339.8 82.4 %copy-start.65 = (f32[1024]{0:T(1024)S(1)}, f32[1024]{0:T(1024)}, u32[]{:S(2)}) copy-start(f32[1024]{0:T(1024)} %param.34) | copy-start | bytes 12292
  339.8 136.3 %all-gather.17.cloned.1.call-start = ((), (), s32[]{:S(2)}) async-start(), calls=%async_computation.25 | async-start | bytes 2621440 | tf_op jit(solution)/shard_map/all_gather | solution.py:144
  344.8 80.5 %copy-start.61 = (f32[1024]{0:T(1024)S(1)}, f32[1024]{0:T(1024)}, u32[]{:S(2)}) copy-start(f32[1024]{0:T(1024)} %param.35) | copy-start | bytes 12292
  344.8 81.5 %copy-start.66 = (f32[1024]{0:T(1024)S(1)}, f32[1024]{0:T(1024)}, u32[]{:S(2)}) copy-start(f32[1024]{0:T(1024)} %param.36) | copy-start | bytes 12292
  430.6 91.5 %all-gather.21.cloned.1.call-start = ((), (), s32[]{:S(2)}) async-start(), calls=%async_computation.29 | async-start | bytes 2621440 | tf_op jit(solution)/shard_map/all_gather | solution.py:144
  432.9 134.2 %reduce-scatter.34.cloned.1.call-start = ((), (), s32[]{:S(2)}) async-start(), calls=%async_computation.26 | async-start | bytes 2621440 | tf_op jit(solution)/shard_map/reduce_scatter | solution.py:154
  489.5 123.1 %reduce-scatter.38.cloned.1.call-start = ((), (), s32[]{:S(2)}) async-start(), calls=%async_computation.30 | async-start | bytes 2621440 | tf_op jit(solution)/shard_map/reduce_scatter | solution.py:154
  535.5 80.6 %copy-start.7 = (bf16[128,2,1024]{2,0,1:T(8,128)(2,1)S(1)}, bf16[128,2,1024]{2,0,1:T(8,128)(2,1)}, u32[]{:S(2)}) copy-start(bf16[128,2,1024]{2,0,1:T(8,128)(2,1)} %reduce-scatter.26.cloned.1.call-done) | copy-start | bytes 1572868
  535.6 130.1 %all-gather.19.cloned.1.call-start = ((), (), s32[]{:S(2)}) async-start(), calls=%async_computation.27 | async-start | bytes 2621440 | tf_op jit(solution)/shard_map/all_gather | solution.py:164
  616.1 4.2 copy-start.6
  618.2 47.5 %copy-start.49 = (bf16[256,1024]{1,0:T(8,128)(2,1)S(1)}, bf16[256,1024]{1,0:T(8,128)(2,1)}, u32[]{:S(2)}) copy-start(bf16[256,1024]{1,0:T(8,128)(2,1)} %param.27) | copy-start | bytes 1572868
  620.2 91.6 %all-gather.23.cloned.1.call-start = ((), (), s32[]{:S(2)}) async-start(), calls=%async_computation.31 | async-start | bytes 2621440 | tf_op jit(solution)/shard_map/all_gather | solution.py:164
  624.0 153.0 %reduce-scatter.36.cloned.1.call-start = ((), (), s32[]{:S(2)}) async-start(), calls=%async_computation.28 | async-start | bytes 2621440 | tf_op jit(solution)/shard_map/reduce_scatter | solution.py:193
  668.0 5.2 copy-start.46
  673.2 96.6 %copy-start.29 = (bf16[1,512,2,256]{3,1,0,2:T(8,128)(2,1)}, bf16[1,512,2,256]{3,1,0,2:T(8,128)(2,1)S(1)}, u32[]{:S(2)}) copy-start(bf16[1,512,2,256]{3,1,0,2:T(8,128)(2,1)S(1)} %copy.86) | copy-start | bytes 1572868
  678.2 6.7 copy-start.21
  686.0 83.8 %copy-start.30 = (bf16[1,512,2,256]{3,1,0,2:T(8,128)(2,1)}, bf16[1,512,2,256]{3,1,0,2:T(8,128)(2,1)S(1)}, u32[]{:S(2)}) copy-start(bf16[1,512,2,256]{3,1,0,2:T(8,128)(2,1)S(1)} %copy.84) | copy-start | bytes 1572868
  690.0 4.8 copy-start.31
  690.0 21.8 %copy-start.50 = (bf16[256,1024]{1,0:T(8,128)(2,1)S(1)}, bf16[256,1024]{1,0:T(8,128)(2,1)}, u32[]{:S(2)}) copy-start(bf16[256,1024]{1,0:T(8,128)(2,1)} %param.27) | copy-start | bytes 1572868
  694.8 107.2 %reduce-scatter.40.cloned.1.call-start = ((), (), s32[]{:S(2)}) async-start(), calls=%async_computation.32 | async-start | bytes 2621440 | tf_op jit(solution)/shard_map/reduce_scatter | solution.py:193
  714.1 5.2 copy-start.44
  719.3 16.5 copy-start.33
  724.1 6.7 copy-start.17
  731.9 8.8 copy-start.35
  735.9 4.8 copy-start.37
  740.7 201.0 %reduce-scatter.58.cloned.1.call-start = ((), (), s32[]{:S(2)}) async-start(), calls=%async_computation.41 | async-start | bytes 2162688
  743.5 8.2 copy-start.26
  743.5 332.7 %reduce-scatter.56.cloned.1.call-start = ((), (), s32[]{:S(2)}) async-start(), calls=%async_computation.40 | async-start | bytes 540672
  751.5 375.7 %reduce-scatter.50.cloned.1.call-start = ((), (), s32[]{:S(2)}) async-start(), calls=%async_computation.37 | async-start | bytes 4718592 | tf_op jit(solution)/shard_map/reduce_scatter | solution.py:225
  759.0 4.8 copy-start.70
  759.0 423.1 %reduce-scatter.48.cloned.1.call-start = ((), (), s32[]{:S(2)}) async-start(), calls=%async_computation.36 | async-start | bytes 4718592 | tf_op jit(solution)/shard_map/reduce_scatter | solution.py:224
  759.1 4.8 copy-start.72
  768.2 550.6 %reduce-scatter.54.cloned.1.call-start = ((), (), s32[]{:S(2)}) async-start(), calls=%async_computation.39 | async-start | bytes 540672
  771.2 5.8 copy-start.11
  771.2 7.1 copy-start.63
  771.2 30.8 %copy-start.13 = (f32[128,2,1024]{2,0,1:T(8,128)S(1)}, f32[128,2,1024]{2,0,1:T(8,128)}, u32[]{:S(2)}) copy-start(f32[128,2,1024]{2,0,1:T(8,128)} %copy-done.12) | copy-start | bytes 3145732
  771.2 680.7 %reduce-scatter.52.cloned.1.call-start = ((), (), s32[]{:S(2)}) async-start(), calls=%async_computation.38 | async-start | bytes 540672
  805.5 7.0 copy-start.42
  805.6 692.3 %reduce-scatter.44.cloned.1.call-start = ((), (), s32[]{:S(2)}) async-start(), calls=%async_computation.34 | async-start | bytes 3538944 | tf_op jit(solution)/shard_map/reduce_scatter | solution.py:220
  812.2 6.0 copy-start.57
  812.2 6.0 copy-start.59
  812.2 725.6 %reduce-scatter.46.cloned.1.call-start = ((), (), s32[]{:S(2)}) async-start(), calls=%async_computation.35 | async-start | bytes 1179648 | tf_op jit(solution)/shard_map/reduce_scatter | solution.py:221
  818.2 871.0 %reduce-scatter.42.cloned.1.call-start = ((), (), s32[]{:S(2)}) async-start(), calls=%async_computation.33 | async-start | bytes 4325376 | tf_op jit(solution)/shard_map/reduce_scatter | solution.py:236
  1320.2 369.0 %copy-start.1 = (bf16[1024,1024]{1,0:T(8,128)(2,1)S(1)}, bf16[1024,1024]{1,0:T(8,128)(2,1)}, u32[]{:S(2)}) copy-start(bf16[1024,1024]{1,0:T(8,128)(2,1)} %param.31) | copy-start | bytes 6291460
  (35 other events, 68.3 us)
Sparse Core Ops, SparseCore 0:
  14.7 48.6 all-gather.8
  65.5 44.6 all-gather.12
  113.0 42.5 reduce-scatter.25
  157.9 43.1 reduce-scatter.29
  207.3 45.2 all-gather.14
  254.6 44.6 all-gather.10
  333.9 42.4 reduce-scatter.27
  378.9 43.2 reduce-scatter.31
  430.8 45.2 all-gather.16
  477.5 44.6 all-gather.20
  524.4 42.5 reduce-scatter.33
  569.3 43.1 reduce-scatter.37
  620.3 45.2 all-gather.18
  667.1 44.6 all-gather.22
  713.9 42.5 reduce-scatter.35
  758.8 43.1 reduce-scatter.39
  804.1 137.5 reduce-scatter.57
  943.9 132.2 reduce-scatter.55
  1079.5 47.5 reduce-scatter.49
  1130.8 51.3 reduce-scatter.47
  1184.4 134.4 reduce-scatter.53
  1321.1 130.7 reduce-scatter.51
  1455.3 42.5 reduce-scatter.43
  1501.8 36.0 reduce-scatter.45
  1540.8 148.2 reduce-scatter.41
where the time goes:
time: 1700 us
  waiting for transfers between devices  1390 us (82%)
  matrix products  162 us (10%)
  other arithmetic  69.6 us (4%)
  local copies, waits for them, and re-layouts  50.7 us (3%)
    unnamed x29, waiting for transfers between devices  511 us
    reduce_scatter x1, waiting for transfers between devices, on_device(): lax.psum_scatter(acc_w_time * weighting, ('dp', 'mp'), scatter_dimension=...  151 us
    all_gather x2, waiting for transfers between devices, on_device(): normed_all = lax.all_gather(normed.astype(bf16), 'mp', axis=0, tiled=True)  85.2 us
    all_gather x2, waiting for transfers between devices, on_device(): hidden = lax.all_gather(start_rows.astype(bf16), 'mp', axis=0, tiled=True)  78.5 us
    reduce_scatter x2, waiting for transfers between devices, on_device(): lax.psum_scatter(jnp.einsum('lnf,fd->lnd', active, w_down, preferred_elem...  77.3 us
    reduce_scatter x2, waiting for transfers between devices, on_device(): lax.psum_scatter(jnp.einsum('lnf,df->lnd', up_grad, w_up, preferred_eleme...  76.9 us
    reduce_scatter x2, waiting for transfers between devices, on_device(): lax.psum_scatter(jnp.einsum('lnh,hd->lnd', context, w_out, preferred_elem...  76.1 us
    all_gather x2, waiting for transfers between devices, on_device(): branch_all = lax.all_gather(branch_grad, 'mp', axis=0, tiled=True)  75.5 us
  transfers between devices with their start and end apart: 25, of which 24 were waited for; matrix products, arithmetic and copies ran while one was open for 12% of the time, Pallas kernels for 0%

commit v1 on v0

v1 whole, which is shorter than its diff:
```python
import functools
import math

import jax
import jax.numpy as jnp
from jax import lax
from jax.experimental import pallas as pl
from jax.experimental.pallas import tpu as pltpu
from jax.sharding import PartitionSpec as P

HD = 64
f32 = jnp.float32
bf16 = jnp.bfloat16
VMEM_LIMIT = 56 * 2**20
PATHS = ((2, 4), (4, 2))


def params(**more):
    return pltpu.CompilerParams(vmem_limit_bytes=VMEM_LIMIT, **more)


def dot(a, b, dims):
    return lax.dot_general(a, b, (dims, ((), ())), preferred_element_type=f32)


def sinusoid(steps, model_width):
    half_width = model_width // 2
    freqs = jnp.exp(-math.log(10000.0) * jnp.arange(half_width, dtype=f32) / half_width)
    angles = steps[:, None] * freqs[None, :]
    return jnp.concatenate([jnp.sin(angles), jnp.cos(angles)], axis=-1).astype(bf16)


def assemble_body(plan, n_out, place_ref, *refs):
    pieces = refs[: len(plan)]
    outs = refs[len(plan) : len(plan) + n_out]
    sems = refs[-1]
    here = place_ref[0]
    copies = []
    for piece, (path, masks, spans) in zip(pieces, plan):
        for i, mask in enumerate(masks):
            for out, (axes, start, size) in zip(outs, spans):
                lead = (slice(None),) * axes
                src = piece.at[i].at[lead + (pl.ds(start, size),)]
                dst = out.at[lead + (here ^ mask, path)]
                copies.append(pltpu.make_async_copy(src, dst, sems.at[len(copies)]))
    for copy in copies:
        copy.start()
    for copy in copies:
        copy.wait()


def assemble(place, pieces, plan, shapes):
    n_copies = sum(len(masks) * len(spans) for _, masks, spans in plan)
    hbm = pl.BlockSpec(memory_space=pl.ANY)
    return pl.pallas_call(
        functools.partial(assemble_body, plan, len(shapes)),
        out_shape=[jax.ShapeDtypeStruct(s, bf16) for s in shapes],
        in_specs=[pl.BlockSpec(memory_space=pltpu.SMEM)] + [hbm] * len(pieces),
        out_specs=[hbm] * len(shapes),
        scratch_shapes=[pltpu.SemaphoreType.DMA((n_copies,))],
        compiler_params=params(),
        name="assemble",
    )(place, *pieces)


def attend_body(q_ref, k_ref, v_ref, p_ref, c_ref):
    q, k, v = q_ref[...], k_ref[...], v_ref[...]
    lane = lax.broadcasted_iota(jnp.int32, q.shape, 1)
    joined = None
    for hh in range(2):
        mine = (lane // HD) == hh
        kh = jnp.where(mine, k, jnp.zeros_like(k))
        st = dot(kh, q, ((1,), (1,))) * 0.125
        top = jnp.max(st, axis=0, keepdims=True)
        e = jnp.exp(st - top)
        p = (e * (1.0 / jnp.sum(e, axis=0, keepdims=True))).astype(bf16)
        p_ref[hh] = p
        c = dot(p, v, ((0,), (0,)))
        joined = c if joined is None else jnp.where(mine, c, joined)
    c_ref[...] = joined.astype(bf16)


def attend(q, k, v):
    length, cols = q.shape
    pairs = cols // (2 * HD)
    block = pl.BlockSpec((length, 2 * HD), lambda i: (0, i))
    return pl.pallas_call(
        attend_body,
        grid=(pairs,),
        out_shape=[
            jax.ShapeDtypeStruct((2 * pairs, length, length), bf16),
            jax.ShapeDtypeStruct((length, cols), bf16),
        ],
        in_specs=[block] * 3,
        out_specs=[pl.BlockSpec((2, length, length), lambda i: (i, 0, 0)), block],
        compiler_params=params(),
        name="attend",
    )(q, k, v)


def attend_back_body(q_ref, k_ref, v_ref, p_ref, g_ref, dq_ref, dk_ref, dv_ref):
    q, k, v, g = q_ref[...], k_ref[...], v_ref[...], g_ref[...]
    lane = lax.broadcasted_iota(jnp.int32, q.shape, 1)
    dq = dk = dv = None
    for hh in range(2):
        mine = (lane // HD) == hh
        zero = jnp.zeros_like(q)
        gh = jnp.where(mine, g, zero)
        kh = jnp.where(mine, k, zero)
        qh = jnp.where(mine, q, zero)
        p = p_ref[hh]
        dpt = dot(v, gh, ((1,), (1,)))
        pf = p.astype(f32)
        row = jnp.sum(pf * dpt, axis=0, keepdims=True)
        ds = (pf * (dpt - row)).astype(bf16)
        a = dot(p, gh, ((1,), (0,)))
        b = dot(ds, qh, ((1,), (0,)))
        c = dot(ds, kh, ((0,), (0,)))
        dv = a if dv is None else dv + a
        dk = b if dk is None else dk + b
        dq = c if dq is None else dq + c
    dq_ref[...] = (dq * 0.125).astype(bf16)
    dk_ref[...] = (dk * 0.125).astype(bf16)
    dv_ref[...] = dv.astype(bf16)


def attend_back(q, k, v, p, g):
    length, cols = q.shape
    pairs = cols // (2 * HD)
    block = pl.BlockSpec((length, 2 * HD), lambda i: (0, i))
    return pl.pallas_call(
        attend_back_body,
        grid=(pairs,),
        out_shape=[jax.ShapeDtypeStruct((length, cols), bf16)] * 3,
        in_specs=[block] * 3 + [pl.BlockSpec((2, length, length), lambda i: (i, 0, 0)), block],
        out_specs=[block] * 3,
        compiler_params=params(),
        name="attend_back",
    )(q, k, v, p, g)


def weight_grad_body(on_rows, order, width, a_ref, a2_ref, b_ref, b2_ref, keep_ref, send_ref):
    g = dot(a_ref[...], b_ref[...], ((0,), (0,))) + dot(a2_ref[...], b2_ref[...], ((0,), (0,)))
    g = g.astype(bf16)
    for out, picks in ((keep_ref, order[:2]), (send_ref, order[2:])):
        for i, j in enumerate(picks):
            span = slice(j * width, (j + 1) * width)
            out[i] = g[span] if on_rows else g[:, span]


def weight_grad(on_rows, path, width, a, a2, b, b2):
    order = (0, 2, 1, 3) if path == 0 else (0, 1, 2, 3)
    rows, cols = a.shape[1], b.shape[1]
    tile = (width, cols) if on_rows else (rows, width)
    full = pl.BlockSpec(memory_space=pltpu.VMEM)
    out = jax.ShapeDtypeStruct((2,) + tile, bf16)
    return pl.pallas_call(
        functools.partial(weight_grad_body, on_rows, order, width),
        out_shape=[out, out],
        in_specs=[full] * 4,
        out_specs=[full] * 2,
        compiler_params=params(),
        name="weight_grad",
    )(a, a2, b, b2)


def norm_stats(values):
    center = values - jnp.mean(values, axis=-1, keepdims=True)
    inv = lax.rsqrt(jnp.mean(center * center, axis=-1, keepdims=True) + 1e-05)
    return center * inv, inv


def norm_back(grad, n, inv, gain):
    gn = grad * gain
    return (gn - jnp.mean(gn, -1, keepdims=True) - n * jnp.mean(gn * n, -1, keepdims=True)) * inv


def on_device(
    tokens,
    timesteps,
    buckets,
    counts,
    w_time,
    table,
    w_qkv,
    b_qv,
    w_out,
    b_out,
    gain1,
    shift1,
    w_up,
    b_up,
    w_down,
    b_down,
    gain2,
    shift2,
    cotangent,
):
    mpn = lax.axis_size("mp")
    dpn = lax.axis_size("dp")
    extra = dpn.bit_length() - 4
    me = lax.axis_index("dp")
    z = lax.axis_index("mp")
    q8 = me >> extra
    width = w_time.shape[0]
    positions, slots = tokens.shape[:2]
    length = positions * mpn
    head_cols = w_qkv.shape[2]
    units = w_up.shape[1]
    chunk = width // 8

    def flip(x, mask):
        step = mask << extra
        return lax.ppermute(x, "dp", [(i, i ^ step) for i in range(dpn)])

    def shift(x, s):
        return lax.ppermute(x, "mp", [(i, (i + s) % mpn) for i in range(mpn)])

    def to_items(x):
        x = lax.all_to_all(jnp.moveaxis(x, 1, 0), "mp", 0, 0, tiled=False)
        return x.reshape(length, width)

    def to_positions(x):
        x = lax.all_to_all(x.reshape(mpn, positions, width), "mp", 0, 0, tiled=False)
        return jnp.moveaxis(x, 0, 1)

    def spread(part):
        arrived = [shift(part, s) for s in range(1, mpn)]
        pieces, plan = [], []
        for path, (first, second) in enumerate(PATHS):
            mine = jnp.stack([a[path] for a in arrived])
            held = jnp.stack([mine, flip(mine, first)])
            far = flip(held, second)
            near = (0, first)
            beyond = (second, first | second)
            pieces += [held, far, flip(held, 1), flip(far, 1)]
            plan += [(path, m) for m in (near, beyond)]
            plan += [(path, tuple(v ^ 1 for v in m)) for m in (near, beyond)]
        return pieces, plan

    def eighth(shard, axis):
        dims = shard.shape
        rows = dims[axis] // 16
        shaped = shard.reshape(dims[:axis] + (8, 2, rows) + dims[axis + 1 :])
        return jnp.moveaxis(lax.dynamic_index_in_dim(shaped, q8, axis, False), axis, 0)

    place = q8.astype(jnp.int32)[None]
    n_far = mpn - 1

    pieces, plan = spread(eighth(w_qkv, 1))
    rows = chunk // 2
    (far_qkv,) = assemble(
        place,
        pieces,
        [(p, m, ((2, 0, rows),)) for p, m in plan],
        [(n_far, 3, 8, 2, rows, head_cols)],
    )
    far_qkv = far_qkv.reshape(n_far, 3, width, head_cols)
    wq = [w_qkv] + [far_qkv[s] for s in range(n_far)]

    out_rows, up_rows, down_rows = head_cols // 16, width // 16, units // 16
    pieces, plan = spread(jnp.concatenate([eighth(w_out, 0), eighth(w_up, 0)], axis=1))
    far_out, far_up = assemble(
        place,
        pieces,
        [(p, m, ((1, 0, out_rows), (1, out_rows, up_rows))) for p, m in plan],
        [(n_far, 8, 2, out_rows, width), (n_far, 8, 2, up_rows, units)],
    )
    far_out = far_out.reshape(n_far, head_cols, width)
    far_up = far_up.reshape(n_far, width, units)
    wo = [w_out] + [far_out[s] for s in range(n_far)]
    wu = [w_up] + [far_up[s] for s in range(n_far)]

    pieces, plan = spread(eighth(w_down, 0))
    (far_down,) = assemble(
        place,
        pieces,
        [(p, m, ((1, 0, down_rows),)) for p, m in plan],
        [(n_far, 8, 2, down_rows, width)],
    )
    far_down = far_down.reshape(n_far, units, width)
    wd = [w_down] + [far_down[s] for s in range(n_far)]

    biases = jnp.concatenate([b_up, b_qv[0], b_qv[1]])
    biases = [biases] + [shift(biases, s) for s in range(1, mpn)]

    total_live = jnp.sum(counts).astype(f32)
    weighting = 1.0 / total_live
    live = (z < lax.dynamic_index_in_dim(counts, me, 0, False)).astype(f32)
    my_step = lax.dynamic_index_in_dim(timesteps, z, 0, True)
    my_bucket = lax.dynamic_index_in_dim(buckets, z, 0, False)
    time_embed = jnp.dot(
        sinusoid(my_step.astype(f32), width), w_time, preferred_element_type=f32
    ) + lax.dynamic_index_in_dim(table, my_bucket, 0, True)

    start = to_items(tokens).astype(f32) + time_embed
    hidden = start.astype(bf16)

    qkv, probs, ctx = [], [], []
    for s in range(mpn):
        pq = dot(hidden, wq[s][0], ((1,), (0,))) + biases[s][units : units + head_cols]
        pk = dot(hidden, wq[s][1], ((1,), (0,)))
        pv = dot(hidden, wq[s][2], ((1,), (0,))) + biases[s][units + head_cols :]
        qkv.append((pq.astype(bf16), pk.astype(bf16), pv.astype(bf16)))
        p, c = attend(*qkv[s])
        probs.append(p)
        ctx.append(c)
    mixing = b_out + sum(dot(ctx[s], wo[s], ((1,), (0,))) for s in range(mpn))
    n1, inv1 = norm_stats(start + mixing)
    normed = n1 * gain1 + shift1
    normed_low = normed.astype(bf16)
    active, slope = [], []
    for s in range(mpn):
        u = dot(normed_low, wu[s], ((1,), (0,))) + biases[s][:units]
        phi = 0.5 + 0.5 * lax.erf(u * (2.0**-0.5))
        active.append((u * phi).astype(bf16))
        slope.append((phi + u * jnp.exp(-0.5 * u * u) * (2.0 * math.pi) ** -0.5).astype(bf16))
    branch = b_down + sum(dot(active[s], wd[s], ((1,), (0,))) for s in range(mpn))
    n2, inv2 = norm_stats(normed + branch)
    output = to_positions((n2 * gain2 + shift2).astype(bf16))

    grad_result = to_items(cotangent).astype(f32) * live
    grad_gain2 = jnp.sum(grad_result * n2, axis=0)
    grad_shift2 = jnp.sum(grad_result, axis=0)
    grad_second = norm_back(grad_result, n2, inv2, gain2)
    branch_grad = grad_second.astype(bf16)
    grad_b_down = jnp.sum(branch_grad.astype(f32), axis=0)

    def pick(x, flipped):
        spans = [
            lax.dynamic_slice_in_dim(x, (q8 ^ (j * 2) ^ flipped) * chunk, chunk, 1)
            for j in range(4)
        ]
        return jnp.concatenate(spans, axis=1)

    def pair_pick(x):
        return pick(x, 0), flip(pick(x, 1), 1)

    def reduced(on_rows, mine, theirs, picked, picked2):
        total = None
        for path, (first, second) in enumerate(PATHS):
            for s in range(path * mpn // 2, (path + 1) * mpn // 2):
                if on_rows:
                    pair = weight_grad(True, path, chunk, picked, picked2, mine[s], theirs[s])
                else:
                    pair = weight_grad(False, path, chunk, mine[s], theirs[s], picked, picked2)
                keep, sent = pair
                came = flip(sent, first)
                second_part = (keep[1].astype(f32) + came[1].astype(f32)).astype(bf16)
                part = keep[0].astype(f32) + came[0].astype(f32) + flip(second_part, second).astype(f32)
                if s:
                    part = shift(part.astype(bf16), -s).astype(f32)
                total = part if total is None else total + part
        axis = 0 if on_rows else 1
        for t in reversed(range(extra)):
            half = total.shape[axis] // 2
            bit = (me >> t) & 1
            keep = lax.dynamic_slice_in_dim(total, bit * half, half, axis)
            sent = lax.dynamic_slice_in_dim(total, (1 - bit) * half, half, axis)
            total = keep + lax.ppermute(sent, "dp", [(i, i ^ (1 << t)) for i in range(dpn)])
        return total * weighting

    active2 = [flip(a, 1) for a in active]
    grad_w_down = reduced(False, active, active2, *pair_pick(branch_grad))

    up_grad = [
        (dot(branch_grad, wd[s], ((1,), (1,))) * slope[s].astype(f32)).astype(bf16)
        for s in range(mpn)
    ]
    grad_b_up = [jnp.sum(g.astype(f32), axis=0) for g in up_grad]
    up_grad2 = [flip(g, 1) for g in up_grad]
    grad_w_up = reduced(True, up_grad, up_grad2, *pair_pick(normed_low))
    grad_normed = grad_second + sum(dot(up_grad[s], wu[s], ((1,), (1,))) for s in range(mpn))
    grad_gain1 = jnp.sum(grad_normed * n1, axis=0)
    grad_shift1 = jnp.sum(grad_normed, axis=0)
    grad_first = norm_back(grad_normed, n1, inv1, gain1)
    mixing_grad = grad_first.astype(bf16)
    grad_b_out = jnp.sum(mixing_grad.astype(f32), axis=0)
    ctx2 = [flip(c, 1) for c in ctx]
    grad_w_out = reduced(False, ctx, ctx2, *pair_pick(mixing_grad))
    proj_grad, grad_b_q, grad_b_v = [], [], []
    grad_tokens = grad_first
    for s in range(mpn):
        cg = dot(mixing_grad, wo[s], ((1,), (1,))).astype(bf16)
        dq, dk, dv = attend_back(*qkv[s], probs[s], cg)
        grad_b_q.append(jnp.sum(dq.astype(f32), axis=0))
        grad_b_v.append(jnp.sum(dv.astype(f32), axis=0))
        proj_grad.append(jnp.concatenate([dq, dk, dv], axis=1))
        for c, g in enumerate((dq, dk, dv)):
            grad_tokens = grad_tokens + dot(g, wq[s][c], ((1,), (1,)))
    proj_grad2 = [flip(g, 1) for g in proj_grad]
    grad_w_qkv = reduced(True, proj_grad, proj_grad2, *pair_pick(hidden))
    grad_w_qkv = jnp.moveaxis(grad_w_qkv.reshape(grad_w_qkv.shape[0], 3, head_cols), 1, 0)
    time_grad = jnp.sum(grad_tokens, axis=0)
    grad_tokens = to_positions(grad_tokens.astype(bf16)).astype(f32)

    devices = dpn * mpn

    def in_order(parts):
        turned = jnp.stack([parts[-i % mpn] for i in range(mpn)] * 2)
        return lax.dynamic_slice_in_dim(turned, (mpn - z) % mpn, mpn, 0).reshape(-1)

    vectors = [
        in_order(grad_b_q),
        in_order(grad_b_v),
        grad_b_out,
        grad_gain1,
        grad_shift1,
        grad_b_down,
        grad_gain2,
        grad_shift2,
        in_order(grad_b_up),
    ]
    spread_out = jnp.concatenate([v.reshape(devices, -1) for v in vectors], axis=1)
    facts = jnp.stack([my_step[0].astype(f32), my_bucket.astype(f32)])
    facts = jnp.broadcast_to(facts[None], (devices, 2))
    both = ("dp", "mp")
    gathered = lax.all_to_all(jnp.concatenate([spread_out, facts], axis=1), both, 0, 0, tiled=True)
    summed = jnp.sum(gathered[:, :-2], axis=0) * weighting
    steps, rows_of = gathered[:, -2], gathered[:, -1]
    per = width // devices
    small = [summed[i * per : (i + 1) * per] for i in range(8)]
    grad_b_up = summed[8 * per :]
    grads = lax.all_to_all(time_grad.reshape(devices, per), both, 0, 0, tiled=True)
    high = lax.Precision.HIGHEST
    grad_w_time = (
        jnp.einsum("nd,ne->de", sinusoid(steps, width).astype(f32), grads, precision=high)
        * weighting
    )
    onehot = (rows_of[:, None] == jnp.arange(table.shape[0], dtype=f32)[None, :]).astype(f32)
    grad_table = jnp.einsum("nb,nd->bd", onehot, grads, precision=high) * weighting
    return (
        output,
        grad_tokens,
        grad_w_time,
        grad_table,
        grad_w_qkv,
        jnp.stack(small[:2]),
        grad_w_out,
        small[2],
        small[3],
        small[4],
        grad_w_up,
        grad_b_up,
        grad_w_down,
        small[5],
        small[6],
        small[7],
    )


def solution(mesh):
    return jax.shard_map(
        on_device,
        mesh=mesh,
        in_specs=(
            P("mp", "dp", None),
            P("dp"),
            P("dp"),
            P(),
            P(),
            P(),
            P(None, None, "mp"),
            P(None, "mp"),
            P("mp", None),
            P(),
            P(),
            P(),
            P(None, "mp"),
            P("mp"),
            P("mp", None),
            P(),
            P(),
            P(),
            P("mp", "dp", None),
        ),
        out_specs=(
            P("mp", "dp", None),
            P("mp", "dp", None),
            P(None, ("dp", "mp")),
            P(None, ("dp", "mp")),
            P(None, "dp", "mp"),
            P(None, ("dp", "mp")),
            P("mp", "dp"),
            P(("dp", "mp")),
            P(("dp", "mp")),
            P(("dp", "mp")),
            P("dp", "mp"),
            P(("dp", "mp")),
            P("mp", "dp"),
            P(("dp", "mp")),
            P(("dp", "mp")),
            P(("dp", "mp")),
        ),
        check_vma=False,
    )
```

time: 1700 us -> 1200 us (0.71)
  waiting for transfers between devices: 1390 us -> 148 us
  Pallas kernels: 0 us -> 675 us
  starting transfers between devices: 3.08 us -> 124 us
  matrix products: 162 us -> 94.7 us
    pallas_call x0 -> x27, Pallas kernels: none -> 675 us  [the longest x3 576 us: assemble(): pl.pallas_call(functools.partial(assemble_body, plan, len(shapes)), out_s...]
    reduce_scatter x13 -> x0, waiting for transfers between devices: 587 us -> none  [the longest x1 151 us: on_device(): lax.psum_scatter(acc_w_time * weighting, ('dp', 'mp'), scatter_dimension=...]
    unnamed x29 -> x0, waiting for transfers between devices: 511 us -> none
    all_gather x8 -> x0, waiting for transfers between devices: 297 us -> none  [the longest x2 85.2 us: on_device(): normed_all = lax.all_gather(normed.astype(bf16), 'mp', axis=0, tiled=True)]
    ppermute x0 -> x100, waiting for transfers between devices: none -> 138 us  [the longest x24 74.2 us: shift(): return lax.ppermute(x, 'mp', [(i, (i + s) % mpn) for i in range(mpn)])]
    ppermute x0 -> x100, starting transfers between devices: none -> 100 us  [the longest x76 53.3 us: flip(): return lax.ppermute(x, 'dp', [(i, i ^ step) for i in range(dpn)])]
    dot_general x44 -> x51, matrix products: 162 us -> 94.7 us  [the longest x48 90.9 us: dot(): return lax.dot_general(a, b, (dims, ((), ())), preferred_element_type=f32)]
    all_to_all x0 -> x6, starting transfers between devices: none -> 23.6 us  [the longest x2 9.06 us: to_items(): x = lax.all_to_all(jnp.moveaxis(x, 1, 0), 'mp', 0, 0, tiled=False)]
  transfers between devices with their start and end apart: 25 -> 106, of which waited for: 24 -> 26; matrix products, arithmetic and copies ran while one was open for 12% -> 19% of each run, Pallas kernels for 0% -> 57%
where the time goes in v1:
time: 1200 us; the launch traced here: 1190 us
  Pallas kernels  675 us (56%)
  waiting for transfers between devices  148 us (12%)
  starting transfers between devices  124 us (10%)
  matrix products  94.7 us (8%)
  other arithmetic  78.1 us (7%)
  local copies, waits for them, and re-layouts  61.5 us (5%)
    pallas_call x3, Pallas kernels, assemble(): pl.pallas_call(functools.partial(assemble_body, plan, len(shapes)), out_s...  576 us
    dot_general x48, matrix products, dot(): return lax.dot_general(a, b, (dims, ((), ())), preferred_element_type=f32)  90.9 us
    ppermute x24, waiting for transfers between devices, shift(): return lax.ppermute(x, 'mp', [(i, (i + s) % mpn) for i in range(mpn)])  74.2 us
    ppermute x76, waiting for transfers between devices, flip(): return lax.ppermute(x, 'dp', [(i, i ^ step) for i in range(dpn)])  63.4 us
    pallas_call x16, Pallas kernels, weight_grad(): pl.pallas_call(functools.partial(weight_grad_body, on_rows, order, width)...  57.4 us
    ppermute x76, starting transfers between devices, flip(): return lax.ppermute(x, 'dp', [(i, i ^ step) for i in range(dpn)])  53.3 us
    ppermute x24, starting transfers between devices, shift(): return lax.ppermute(x, 'mp', [(i, (i + s) % mpn) for i in range(mpn)])  47.1 us
    unnamed x350, local copies, waits for them, and re-layouts  27.1 us
  transfers between devices with their start and end apart: 106, of which 26 were waited for; matrix products, arithmetic and copies ran while one was open for 19% of the time, Pallas kernels for 57%

profile of v1, /device:TPU:0, one launch (start us, length us, event | category | flops | bytes accessed | tf_op | source)
XLA Modules:
  0.0 1189.0 jit_solution(14179771169800047536)
XLA Ops:
  2.4 3.0 collective-permute-start
  14.4 4.6 all-to-all-start
  46.9 20.9 %collective-permute-done.25 = bf16[2,64,1024]{2,1,0:T(8,128)(2,1)S(1)} collective-permute-done((bf16[2,64,1024]{2,1,0:T(8,128)(2,1)S(1)}, bf16[2,64,1024]{2,1,0:T(8,128)(2,1)S(1)}, u32[]{:S(2)}, u32[]{:S(2)}) %collective-permute-start.25) | collective-permute-done | bytes 262176 | tf_op jit(solution)/shard_map/ppermute | solution.py:217
  67.8 25.5 %collective-permute-done.26 = bf16[2,64,1024]{2,1,0:T(8,128)(2,1)S(1)} collective-permute-done((bf16[2,64,1024]{2,1,0:T(8,128)(2,1)S(1)}, bf16[2,64,1024]{2,1,0:T(8,128)(2,1)S(1)}, u32[]{:S(2)}, u32[]{:S(2)}) %collective-permute-start.26) | collective-permute-done | bytes 262176 | tf_op jit(solution)/shard_map/ppermute | solution.py:217
  93.3 7.2 collective-permute-start.24
  116.6 5.5 collective-permute-done.28
  124.4 4.4 all-to-all-start.2
  139.2 3.6 collective-permute-done.8.refs_5_
  147.0 2.7 all-to-all-done.2
  149.8 2.9 fusion.31
  153.3 4.5 attend.4
  165.4 144.2 %assemble.3 = bf16[3,3,8,2,64,256]{5,4,3,2,1,0:T(8,128)(2,1)} custom-call(s32[1]{0:T(128)} %bitcast.12.place_ref, bf16[2,3,3,64,256]{4,3,2,1,0:T(8,128)(2,1)} %pad_maximum_fusion.4.refs_0_, bf16[2,3,3,64,256]{4,3,2,1,0:T(8,128)(2,1)} %collective-permute-done.4.refs_1_, bf16[2,3,3,64,256]{4,3,2,1,0:T(8,128)(2,1)} %collective-permute-done.5.refs_2_, ...), custom_call_target="tpu_custom_call" | custom-call | tf_op jit(solution)/shard_map/assemble/pallas_call | solution.py:55
  309.6 3.8 fusion.108
  324.6 4.6 attend.5
  329.1 4.5 attend.6
  338.6 4.7 attend.7
  343.4 191.8 %assemble.5 = bf16[3,8,2,64,1024]{4,3,2,1,0:T(8,128)(2,1)} custom-call(s32[1]{0:T(128)} %bitcast.12.place_ref, bf16[2,3,64,1024]{3,2,1,0:T(8,128)(2,1)} %pad_maximum_fusion.2.refs_0_, bf16[2,3,64,1024]{3,2,1,0:T(8,128)(2,1)} %collective-permute-done.29.refs_1_, bf16[2,3,64,1024]{3,2,1,0:T(8,128)(2,1)} %collective-permute-done.30.refs_2_, ...), custom_call_target="tpu_custom_call" | custom-call | tf_op jit(solution)/shard_map/assemble/pallas_call | solution.py:55
  535.3 5.8 fusion.106
  542.0 239.6 %assemble.4 = (bf16[3,8,2,16,1024]{4,3,2,1,0:T(8,128)(2,1)}, bf16[3,8,2,64,1024]{4,3,2,1,0:T(8,128)(2,1)}) custom-call(s32[1]{0:T(128)} %bitcast.12.place_ref, bf16[2,3,80,1024]{3,2,1,0:T(8,128)(2,1)} %pad_maximum_fusion.refs_0_, bf16[2,3,80,1024]{3,2,1,0:T(8,128)(2,1)} %collective-permute-done.16.refs_1_, ...), custom_call_target="tpu_custom_call" | custom-call | tf_op jit(solution)/shard_map/assemble/pallas_call | solution.py:55
  790.9 2.7 multiply_convert_fusion.7
  796.4 2.7 multiply_convert_fusion.6
  812.3 2.7 convert_reduce_fusion.3
  815.0 2.7 convert_reduce_fusion
  817.7 2.7 convert_reduce_fusion.1
  820.4 2.8 convert_reduce_fusion.2
  827.1 2.8 multiply_reduce_fusion
  837.7 5.7 attend_back.4
  846.6 5.7 attend_back.5
  855.7 6.2 attend_back.6
  865.2 5.8 attend_back.7
  891.2 3.3 all-to-all-start.4
  894.5 2.8 fusion.49
  898.8 2.9 fusion.135
  925.3 5.5 collective-permute-done.57
  932.2 3.9 collective-permute-done.61
  938.4 2.8 collective-permute-done.65
  946.0 3.8 collective-permute-done.62
  951.1 3.0 collective-permute-done.66
  957.1 3.5 collective-permute-start.59
  962.5 3.3 collective-permute-done.63
  967.3 9.3 fusion.104
  985.0 5.8 all-to-all-done.5
  990.8 3.7 all-to-all-start.3
  997.7 3.6 weight_grad.16
  1003.6 3.6 weight_grad.17
  1007.2 3.6 weight_grad.18
  1010.8 3.5 weight_grad.19
  1016.5 4.1 weight_grad.28
  1020.6 4.1 weight_grad.29
  1024.7 4.1 weight_grad.30
  1028.8 4.1 weight_grad.31
  1032.9 4.1 weight_grad.24
  1038.0 4.1 weight_grad.25
  1043.2 4.0 weight_grad.26
  1048.3 4.1 weight_grad.27
  1058.7 24.8 %collective-permute-done.42 = bf16[128,768]{1,0:T(8,128)(2,1)S(1)} collective-permute-done((bf16[128,768]{1,0:T(8,128)(2,1)S(1)}, bf16[128,768]{1,0:T(8,128)(2,1)S(1)}, u32[]{:S(2)}, u32[]{:S(2)}) %collective-permute-start.42) | collective-permute-done | bytes 196640 | tf_op jit(solution)/shard_map/ppermute | solution.py:214
  1085.4 4.2 collective-permute-done.46
  1091.3 5.1 all-to-all-start.1
  1111.5 3.8 collective-permute-start.43
  1124.3 7.5 collective-permute-start.51
  1148.0 3.6 collective-permute-start.91
  1158.1 2.9 collective-permute-start.75
  1162.2 15.7 %collective-permute-done.95 = bf16[1024,128]{1,0:T(8,128)(2,1)S(1)} collective-permute-done((bf16[1024,128]{1,0:T(8,128)(2,1)S(1)}, bf16[1024,128]{1,0:T(8,128)(2,1)S(1)}, u32[]{:S(2)}, u32[]{:S(2)}) %collective-permute-start.95) | collective-permute-done | bytes 262176 | tf_op jit(solution)/shard_map/ppermute | solution.py:217
  1179.9 7.8 collective-permute-done.79
  (725 shorter events, 279.3 us)
Async XLA Ops:
  2.4 38.5 %collective-permute-start = (bf16[2,3,64,256]{3,2,1,0:T(8,128)(2,1)}, bf16[2,3,64,256]{3,2,1,0:T(8,128)(2,1)}, u32[]{:S(2)}, u32[]{:S(2)}) collective-permute-start(bf16[2,3,64,256]{3,2,1,0:T(8,128)(2,1)} %copy_bitcast_fusion.2), channel_id=1, source_target_pairs={{0,1},{1,2},{2,3},{3,0},{4,5},{5,6},{6,7},{7,4},{8,9},{9,10},{10,1... | collective-permute-start | bytes 589832 | tf_op jit(solution)/shard_map/ppermute | solution.py:217
  5.5 37.9 %collective-permute-start.1 = (bf16[2,3,64,256]{3,2,1,0:T(8,128)(2,1)}, bf16[2,3,64,256]{3,2,1,0:T(8,128)(2,1)}, u32[]{:S(2)}, u32[]{:S(2)}) collective-permute-start(bf16[2,3,64,256]{3,2,1,0:T(8,128)(2,1)} %copy_bitcast_fusion.2), channel_id=1, source_target_pairs={{0,2},{1,3},{2,0},{3,1},{4,6},{5,7},{6,4},{7,5},{8,10},{9,11},{10,... | collective-permute-start | bytes 589832 | tf_op jit(solution)/shard_map/ppermute | solution.py:217
  8.1 36.9 %collective-permute-start.2 = (bf16[2,3,64,256]{3,2,1,0:T(8,128)(2,1)}, bf16[2,3,64,256]{3,2,1,0:T(8,128)(2,1)}, u32[]{:S(2)}, u32[]{:S(2)}) collective-permute-start(bf16[2,3,64,256]{3,2,1,0:T(8,128)(2,1)} %copy_bitcast_fusion.2), channel_id=1, source_target_pairs={{0,3},{1,0},{2,1},{3,2},{4,7},{5,4},{6,5},{7,6},{8,11},{9,8},{10,9... | collective-permute-start | bytes 589832 | tf_op jit(solution)/shard_map/ppermute | solution.py:217
  10.9 24.4 %collective-permute-start.11 = (f32[1536]{0:T(1024)S(1)}, f32[1536]{0:T(1024)S(1)}, u32[]{:S(2)}, u32[]{:S(2)}) collective-permute-start(f32[1536]{0:T(1024)S(1)} %pad_maximum_fusion.21), channel_id=1, source_target_pairs={{0,1},{1,2},{2,3},{3,0},{4,5},{5,6},{6,7},{7,4},{8,9},{9,10},{10,1... | collective-permute-start | bytes 18440 | tf_op jit(solution)/shard_map/ppermute | solution.py:217
  11.6 26.6 %collective-permute-start.23 = (f32[1536]{0:T(1024)S(1)}, f32[1536]{0:T(1024)S(1)}, u32[]{:S(2)}, u32[]{:S(2)}) collective-permute-start(f32[1536]{0:T(1024)S(1)} %pad_maximum_fusion.21), channel_id=1, source_target_pairs={{0,2},{1,3},{2,0},{3,1},{4,6},{5,7},{6,4},{7,5},{8,10},{9,11},{10,... | collective-permute-start | bytes 18440 | tf_op jit(solution)/shard_map/ppermute | solution.py:217
  14.4 110.0 %all-to-all-start = ((bf16[4,128,1024]{2,1,0:T(8,128)(2,1)}), bf16[4,128,1024]{2,1,0:T(8,128)(2,1)S(1)}, u32[]{:S(2)}, u32[]{:S(2)}) async-start(bf16[4,128,1024]{2,1,0:T(8,128)(2,1)} %bitcast.347), calls=%async_computation | async-start | bytes 2097152 | tf_op jit(solution)/shard_map/all_to_all | solution.py:220
  35.3 68.5 %collective-permute-start.12 = (bf16[2,80,1024]{2,1,0:T(8,128)(2,1)}, bf16[2,80,1024]{2,1,0:T(8,128)(2,1)S(1)}, u32[]{:S(2)}, u32[]{:S(2)}) collective-permute-start(bf16[2,80,1024]{2,1,0:T(8,128)(2,1)} %pad_maximum_fusion.18), channel_id=1, source_target_pairs={{0,1},{1,2},{2,3},{3,0},{4,5},{5,6},{6,7},{7,4},{8,9},{9,10},{10,1... | collective-permute-start | bytes 983048 | tf_op jit(solution)/shard_map/ppermute | solution.py:217
  38.2 67.1 %collective-permute-start.13 = (bf16[2,80,1024]{2,1,0:T(8,128)(2,1)}, bf16[2,80,1024]{2,1,0:T(8,128)(2,1)S(1)}, u32[]{:S(2)}, u32[]{:S(2)}) collective-permute-start(bf16[2,80,1024]{2,1,0:T(8,128)(2,1)} %pad_maximum_fusion.18), channel_id=1, source_target_pairs={{0,2},{1,3},{2,0},{3,1},{4,6},{5,7},{6,4},{7,5},{8,10},{9,11},{10,... | collective-permute-start | bytes 983048 | tf_op jit(solution)/shard_map/ppermute | solution.py:217
  40.9 65.0 %collective-permute-start.14 = (bf16[2,80,1024]{2,1,0:T(8,128)(2,1)}, bf16[2,80,1024]{2,1,0:T(8,128)(2,1)S(1)}, u32[]{:S(2)}, u32[]{:S(2)}) collective-permute-start(bf16[2,80,1024]{2,1,0:T(8,128)(2,1)} %pad_maximum_fusion.18), channel_id=1, source_target_pairs={{0,3},{1,0},{2,1},{3,2},{4,7},{5,4},{6,5},{7,6},{8,11},{9,8},{10,9... | collective-permute-start | bytes 983048 | tf_op jit(solution)/shard_map/ppermute | solution.py:217
  43.4 24.4 %collective-permute-start.25 = (bf16[2,64,1024]{2,1,0:T(8,128)(2,1)S(1)}, bf16[2,64,1024]{2,1,0:T(8,128)(2,1)S(1)}, u32[]{:S(2)}, u32[]{:S(2)}) collective-permute-start(bf16[2,64,1024]{2,1,0:T(8,128)(2,1)S(1)} %copy-done.107), channel_id=1, source_target_pairs={{0,1},{1,2},{2,3},{3,0},{4,5},{5,6},{6,7},{7,4},{8,9},{9,10},{10,1... | collective-permute-start | bytes 786440 | tf_op jit(solution)/shard_map/ppermute | solution.py:217
  44.9 48.4 %collective-permute-start.26 = (bf16[2,64,1024]{2,1,0:T(8,128)(2,1)S(1)}, bf16[2,64,1024]{2,1,0:T(8,128)(2,1)S(1)}, u32[]{:S(2)}, u32[]{:S(2)}) collective-permute-start(bf16[2,64,1024]{2,1,0:T(8,128)(2,1)S(1)} %copy-done.107), channel_id=1, source_target_pairs={{0,2},{1,3},{2,0},{3,1},{4,6},{5,7},{6,4},{7,5},{8,10},{9,11},{10,... | collective-permute-start | bytes 786440 | tf_op jit(solution)/shard_map/ppermute | solution.py:217
  67.8 32.7 %collective-permute-start.27 = (bf16[2,64,1024]{2,1,0:T(8,128)(2,1)S(1)}, bf16[2,64,1024]{2,1,0:T(8,128)(2,1)S(1)}, u32[]{:S(2)}, u32[]{:S(2)}) collective-permute-start(bf16[2,64,1024]{2,1,0:T(8,128)(2,1)S(1)} %copy-done.107), channel_id=1, source_target_pairs={{0,3},{1,0},{2,1},{3,2},{4,7},{5,4},{6,5},{7,6},{8,11},{9,8},{10,9... | collective-permute-start | bytes 786440 | tf_op jit(solution)/shard_map/ppermute | solution.py:217
  93.3 22.0 %collective-permute-start.24 = (f32[1536]{0:T(1024)S(1)}, f32[1536]{0:T(1024)S(1)}, u32[]{:S(2)}, u32[]{:S(2)}) collective-permute-start(f32[1536]{0:T(1024)S(1)} %pad_maximum_fusion.21), channel_id=1, source_target_pairs={{0,3},{1,0},{2,1},{3,2},{4,7},{5,4},{6,5},{7,6},{8,11},{9,8},{10,9... | collective-permute-start | bytes 18440 | tf_op jit(solution)/shard_map/ppermute | solution.py:217
  105.9 25.1 %collective-permute-start.32 = (bf16[3,64,1024]{2,1,0:T(8,128)(2,1)}, bf16[3,64,1024]{2,1,0:T(8,128)(2,1)}, u32[]{:S(2)}, u32[]{:S(2)}) collective-permute-start(bf16[3,64,1024]{2,1,0:T(8,128)(2,1)} %get-tuple-element.281), channel_id=1, source_target_pairs={{0,16},{4,20},{8,24},{12,28},{16,0},{20,4},{24,8},{28,12},{1,17},{... | collective-permute-start | bytes 1179656 | tf_op jit(solution)/shard_map/ppermute | solution.py:214
  109.6 23.4 %collective-permute-start.15 = (bf16[3,80,1024]{2,1,0:T(8,128)(2,1)}, bf16[3,80,1024]{2,1,0:T(8,128)(2,1)}, u32[]{:S(2)}, u32[]{:S(2)}) collective-permute-start(bf16[3,80,1024]{2,1,0:T(8,128)(2,1)} %get-tuple-element.279), channel_id=1, source_target_pairs={{0,8},{4,12},{8,0},{12,4},{16,24},{20,28},{24,16},{28,20},{1,9},{5... | collective-permute-start | bytes 1474568 | tf_op jit(solution)/shard_map/ppermute | solution.py:214
  113.7 21.9 %collective-permute-start.19 = (bf16[3,80,1024]{2,1,0:T(8,128)(2,1)}, bf16[3,80,1024]{2,1,0:T(8,128)(2,1)}, u32[]{:S(2)}, u32[]{:S(2)}) collective-permute-start(bf16[3,80,1024]{2,1,0:T(8,128)(2,1)} %get-tuple-element.277), channel_id=1, source_target_pairs={{0,16},{4,20},{8,24},{12,28},{16,0},{20,4},{24,8},{28,12},{1,17},{... | collective-permute-start | bytes 1474568 | tf_op jit(solution)/shard_map/ppermute | solution.py:214
  115.3 27.5 %collective-permute-start.8 = (bf16[2,3,3,64,256]{4,3,2,1,0:T(8,128)(2,1)}, bf16[2,3,3,64,256]{4,3,2,1,0:T(8,128)(2,1)}, u32[]{:S(2)}, u32[]{:S(2)}) collective-permute-start(bf16[2,3,3,64,256]{4,3,2,1,0:T(8,128)(2,1)} %pad_maximum_fusion.5.refs_4_), channel_id=1, source_target_pairs={{0,8},{4,12},{8,0},{12,4},{16,24},{20,28},{24,16},{28,20},{1,9},{5... | collective-permute-start | bytes 1769480 | tf_op jit(solution)/shard_map/ppermute | solution.py:214
  124.4 25.3 %all-to-all-start.2 = ((bf16[4,128,1024]{2,1,0:T(8,128)(2,1)}), bf16[4,128,1024]{2,1,0:T(8,128)(2,1)}, u32[]{:S(2)}, u32[]{:S(2)}) async-start(bf16[4,128,1024]{2,1,0:T(8,128)(2,1)} %bitcast.348), calls=%async_computation.2 | async-start | bytes 2097152 | tf_op jit(solution)/shard_map/all_to_all | solution.py:220
  131.0 30.6 %collective-permute-start.5 = (bf16[2,3,3,64,256]{4,3,2,1,0:T(8,128)(2,1)}, bf16[2,3,3,64,256]{4,3,2,1,0:T(8,128)(2,1)}, u32[]{:S(2)}, u32[]{:S(2)}) collective-permute-start(bf16[2,3,3,64,256]{4,3,2,1,0:T(8,128)(2,1)} %pad_maximum_fusion.4.refs_0_), channel_id=1, source_target_pairs={{0,4},{4,0},{8,12},{12,8},{16,20},{20,16},{24,28},{28,24},{1,5},{5... | collective-permute-start | bytes 1769480 | tf_op jit(solution)/shard_map/ppermute | solution.py:214
  133.0 28.7 %collective-permute-start.9 = (bf16[2,3,3,64,256]{4,3,2,1,0:T(8,128)(2,1)}, bf16[2,3,3,64,256]{4,3,2,1,0:T(8,128)(2,1)}, u32[]{:S(2)}, u32[]{:S(2)}) collective-permute-start(bf16[2,3,3,64,256]{4,3,2,1,0:T(8,128)(2,1)} %pad_maximum_fusion.5.refs_4_), channel_id=1, source_target_pairs={{0,4},{4,0},{8,12},{12,8},{16,20},{20,16},{24,28},{28,24},{1,5},{5... | collective-permute-start | bytes 1769480 | tf_op jit(solution)/shard_map/ppermute | solution.py:214
  135.6 181.9 %collective-permute-start.29 = (bf16[2,3,64,1024]{3,2,1,0:T(8,128)(2,1)}, bf16[2,3,64,1024]{3,2,1,0:T(8,128)(2,1)}, u32[]{:S(2)}, u32[]{:S(2)}) collective-permute-start(bf16[2,3,64,1024]{3,2,1,0:T(8,128)(2,1)} %pad_maximum_fusion.2.refs_0_), channel_id=1, source_target_pairs={{0,16},{4,20},{8,24},{12,28},{16,0},{20,4},{24,8},{28,12},{1,17},{... | collective-permute-start | bytes 2359304 | tf_op jit(solution)/shard_map/ppermute | solution.py:214
  142.8 22.1 %collective-permute-start.6 = (bf16[2,3,3,64,256]{4,3,2,1,0:T(8,128)(2,1)}, bf16[2,3,3,64,256]{4,3,2,1,0:T(8,128)(2,1)}, u32[]{:S(2)}, u32[]{:S(2)}) collective-permute-start(bf16[2,3,3,64,256]{4,3,2,1,0:T(8,128)(2,1)} %collective-permute-done.4.refs_1_), channel_id=1, source_target_pairs={{0,4},{4,0},{8,12},{12,8},{16,20},{20,16},{24,28},{28,24},{1,5},{5... | collective-permute-start | bytes 1769480 | tf_op jit(solution)/shard_map/ppermute | solution.py:214
  161.7 159.8 %collective-permute-start.30 = (bf16[2,3,64,1024]{3,2,1,0:T(8,128)(2,1)}, bf16[2,3,64,1024]{3,2,1,0:T(8,128)(2,1)}, u32[]{:S(2)}, u32[]{:S(2)}) collective-permute-start(bf16[2,3,64,1024]{3,2,1,0:T(8,128)(2,1)} %pad_maximum_fusion.2.refs_0_), channel_id=1, source_target_pairs={{0,4},{4,0},{8,12},{12,8},{16,20},{20,16},{24,28},{28,24},{1,5},{5... | collective-permute-start | bytes 2359304 | tf_op jit(solution)/shard_map/ppermute | solution.py:214
  161.8 155.8 %collective-permute-start.33 = (bf16[2,3,64,1024]{3,2,1,0:T(8,128)(2,1)S(1)}, bf16[2,3,64,1024]{3,2,1,0:T(8,128)(2,1)}, u32[]{:S(2)}, u32[]{:S(2)}) collective-permute-start(bf16[2,3,64,1024]{3,2,1,0:T(8,128)(2,1)S(1)} %copy-done.15), channel_id=1, source_target_pairs={{0,8},{4,12},{8,0},{12,4},{16,24},{20,28},{24,16},{28,20},{1,9},{5... | collective-permute-start | bytes 2359304 | tf_op jit(solution)/shard_map/ppermute | solution.py:214
  163.3 158.7 %collective-permute-start.16 = (bf16[2,3,80,1024]{3,2,1,0:T(8,128)(2,1)S(1)}, bf16[2,3,80,1024]{3,2,1,0:T(8,128)(2,1)}, u32[]{:S(2)}, u32[]{:S(2)}) collective-permute-start(bf16[2,3,80,1024]{3,2,1,0:T(8,128)(2,1)S(1)} %copy-done.13), channel_id=1, source_target_pairs={{0,16},{4,20},{8,24},{12,28},{16,0},{20,4},{24,8},{28,12},{1,17},{... | collective-permute-start | bytes 2949128 | tf_op jit(solution)/shard_map/ppermute | solution.py:214
  164.9 157.2 %collective-permute-start.20 = (bf16[2,3,80,1024]{3,2,1,0:T(8,128)(2,1)S(1)}, bf16[2,3,80,1024]{3,2,1,0:T(8,128)(2,1)}, u32[]{:S(2)}, u32[]{:S(2)}) collective-permute-start(bf16[2,3,80,1024]{3,2,1,0:T(8,128)(2,1)S(1)} %copy-done.14), channel_id=1, source_target_pairs={{0,8},{4,12},{8,0},{12,4},{16,24},{20,28},{24,16},{28,20},{1,9},{5... | collective-permute-start | bytes 2949128 | tf_op jit(solution)/shard_map/ppermute | solution.py:214
  321.5 219.5 %collective-permute-start.17 = (bf16[2,3,80,1024]{3,2,1,0:T(8,128)(2,1)S(1)}, bf16[2,3,80,1024]{3,2,1,0:T(8,128)(2,1)}, u32[]{:S(2)}, u32[]{:S(2)}) collective-permute-start(bf16[2,3,80,1024]{3,2,1,0:T(8,128)(2,1)S(1)} %copy-done.13), channel_id=1, source_target_pairs={{0,4},{4,0},{8,12},{12,8},{16,20},{20,16},{24,28},{28,24},{1,5},{5... | collective-permute-start | bytes 2949128 | tf_op jit(solution)/shard_map/ppermute | solution.py:214
  321.6 219.9 %collective-permute-start.21 = (bf16[2,3,80,1024]{3,2,1,0:T(8,128)(2,1)S(1)}, bf16[2,3,80,1024]{3,2,1,0:T(8,128)(2,1)}, u32[]{:S(2)}, u32[]{:S(2)}) collective-permute-start(bf16[2,3,80,1024]{3,2,1,0:T(8,128)(2,1)S(1)} %copy-done.14), channel_id=1, source_target_pairs={{0,4},{4,0},{8,12},{12,8},{16,20},{20,16},{24,28},{28,24},{1,5},{5... | collective-permute-start | bytes 2949128 | tf_op jit(solution)/shard_map/ppermute | solution.py:214
  322.1 219.4 %collective-permute-start.18 = (bf16[2,3,80,1024]{3,2,1,0:T(8,128)(2,1)}, bf16[2,3,80,1024]{3,2,1,0:T(8,128)(2,1)}, u32[]{:S(2)}, u32[]{:S(2)}) collective-permute-start(bf16[2,3,80,1024]{3,2,1,0:T(8,128)(2,1)} %collective-permute-done.16.refs_1_), channel_id=1, source_target_pairs={{0,4},{4,0},{8,12},{12,8},{16,20},{20,16},{24,28},{28,24},{1,5},{5... | collective-permute-start | bytes 2949128 | tf_op jit(solution)/shard_map/ppermute | solution.py:214
  322.5 219.4 %collective-permute-start.22 = (bf16[2,3,80,1024]{3,2,1,0:T(8,128)(2,1)}, bf16[2,3,80,1024]{3,2,1,0:T(8,128)(2,1)}, u32[]{:S(2)}, u32[]{:S(2)}) collective-permute-start(bf16[2,3,80,1024]{3,2,1,0:T(8,128)(2,1)} %collective-permute-done.20.refs_5_), channel_id=1, source_target_pairs={{0,4},{4,0},{8,12},{12,8},{16,20},{20,16},{24,28},{28,24},{1,5},{5... | collective-permute-start | bytes 2949128 | tf_op jit(solution)/shard_map/ppermute | solution.py:214
  343.3 565.3 %collective-permute-start.52 = (bf16[512,256]{1,0:T(8,128)(2,1)}, bf16[512,256]{1,0:T(8,128)(2,1)}, u32[]{:S(2)}, u32[]{:S(2)}) collective-permute-start(bf16[512,256]{1,0:T(8,128)(2,1)} %get-tuple-element.70.a_ref), channel_id=1, source_target_pairs={{0,4},{4,0},{8,12},{12,8},{16,20},{20,16},{24,28},{28,24},{1,5},{5... | collective-permute-start | bytes 786440 | tf_op jit(solution)/shard_map/ppermute | solution.py:214
  541.0 375.1 %collective-permute-start.56 = (bf16[512,256]{1,0:T(8,128)(2,1)}, bf16[512,256]{1,0:T(8,128)(2,1)}, u32[]{:S(2)}, u32[]{:S(2)}) collective-permute-start(bf16[512,256]{1,0:T(8,128)(2,1)} %get-tuple-element.71.a_ref), channel_id=1, source_target_pairs={{0,4},{4,0},{8,12},{12,8},{16,20},{20,16},{24,28},{28,24},{1,5},{5... | collective-permute-start | bytes 786440 | tf_op jit(solution)/shard_map/ppermute | solution.py:214
  541.5 377.2 %collective-permute-start.60 = (bf16[512,256]{1,0:T(8,128)(2,1)}, bf16[512,256]{1,0:T(8,128)(2,1)}, u32[]{:S(2)}, u32[]{:S(2)}) collective-permute-start(bf16[512,256]{1,0:T(8,128)(2,1)} %get-tuple-element.73.a_ref), channel_id=1, source_target_pairs={{0,4},{4,0},{8,12},{12,8},{16,20},{20,16},{24,28},{28,24},{1,5},{5... | collective-permute-start | bytes 786440 | tf_op jit(solution)/shard_map/ppermute | solution.py:214
  541.6 380.3 %collective-permute-start.64 = (bf16[512,256]{1,0:T(8,128)(2,1)}, bf16[512,256]{1,0:T(8,128)(2,1)}, u32[]{:S(2)}, u32[]{:S(2)}) collective-permute-start(bf16[512,256]{1,0:T(8,128)(2,1)} %get-tuple-element.74.a_ref), channel_id=1, source_target_pairs={{0,4},{4,0},{8,12},{12,8},{16,20},{20,16},{24,28},{28,24},{1,5},{5... | collective-permute-start | bytes 786440 | tf_op jit(solution)/shard_map/ppermute | solution.py:214
  891.2 89.9 %all-to-all-start.4 = ((f32[32,1,386]{2,1,0:T(1,128)}), f32[32,1,386]{2,1,0:T(1,128)}, u32[]{:S(2)}, u32[]{:S(2)}) async-start(f32[32,1,386]{2,1,0:T(1,128)} %copy.79), calls=%async_computation.4 | async-start | bytes 131072 | tf_op jit(solution)/shard_map/all_to_all | solution.py:418
  909.5 34.2 %collective-permute-start.36 = (bf16[512,512]{1,0:T(8,128)(2,1)}, bf16[512,512]{1,0:T(8,128)(2,1)S(1)}, u32[]{:S(2)}, u32[]{:S(2)}) collective-permute-start(bf16[512,512]{1,0:T(8,128)(2,1)} %pad_maximum_fusion.7), channel_id=1, source_target_pairs={{0,4},{4,0},{8,12},{12,8},{16,20},{20,16},{24,28},{28,24},{1,5},{5... | collective-permute-start | bytes 1572872 | tf_op jit(solution)/shard_map/ppermute | solution.py:214
  916.1 40.9 %collective-permute-start.85 = (bf16[512,512]{1,0:T(8,128)(2,1)}, bf16[512,512]{1,0:T(8,128)(2,1)S(1)}, u32[]{:S(2)}, u32[]{:S(2)}) collective-permute-start(bf16[512,512]{1,0:T(8,128)(2,1)} %pad_maximum_fusion.13), channel_id=1, source_target_pairs={{0,4},{4,0},{8,12},{12,8},{16,20},{20,16},{24,28},{28,24},{1,5},{5... | collective-permute-start | bytes 1572872 | tf_op jit(solution)/shard_map/ppermute | solution.py:214
  918.7 41.8 %collective-permute-start.68 = (bf16[512,512]{1,0:T(8,128)(2,1)}, bf16[512,512]{1,0:T(8,128)(2,1)S(1)}, u32[]{:S(2)}, u32[]{:S(2)}) collective-permute-start(bf16[512,512]{1,0:T(8,128)(2,1)} %pad_maximum_fusion.11), channel_id=1, source_target_pairs={{0,4},{4,0},{8,12},{12,8},{16,20},{20,16},{24,28},{28,24},{1,5},{5... | collective-permute-start | bytes 1572872 | tf_op jit(solution)/shard_map/ppermute | solution.py:214
  921.9 44.8 %collective-permute-start.37 = (bf16[512,768]{1,0:T(8,128)(2,1)}, bf16[512,768]{1,0:T(8,128)(2,1)}, u32[]{:S(2)}, u32[]{:S(2)}) collective-permute-start(bf16[512,768]{1,0:T(8,128)(2,1)} %constant_dynamic-update-slice_fusion.b_ref), channel_id=1, source_target_pairs={{0,4},{4,0},{8,12},{12,8},{16,20},{20,16},{24,28},{28,24},{1,5},{5... | collective-permute-start | bytes 2359304 | tf_op jit(solution)/shard_map/ppermute | solution.py:214
  943.7 23.6 %collective-permute-start.40 = (bf16[512,768]{1,0:T(8,128)(2,1)}, bf16[512,768]{1,0:T(8,128)(2,1)}, u32[]{:S(2)}, u32[]{:S(2)}) collective-permute-start(bf16[512,768]{1,0:T(8,128)(2,1)} %copy-done.49), channel_id=1, source_target_pairs={{0,4},{4,0},{8,12},{12,8},{16,20},{20,16},{24,28},{28,24},{1,5},{5... | collective-permute-start | bytes 2359304 | tf_op jit(solution)/shard_map/ppermute | solution.py:214
  962.5 32.9 %collective-permute-start.84 = (bf16[512,1024]{1,0:T(8,128)(2,1)}, bf16[512,1024]{1,0:T(8,128)(2,1)}, u32[]{:S(2)}, u32[]{:S(2)}) collective-permute-start(bf16[512,1024]{1,0:T(8,128)(2,1)} %copy-done.52), channel_id=1, source_target_pairs={{0,4},{4,0},{8,12},{12,8},{16,20},{20,16},{24,28},{28,24},{1,5},{5... | collective-permute-start | bytes 3145736 | tf_op jit(solution)/shard_map/ppermute | solution.py:214
  965.7 30.3 %collective-permute-start.88 = (bf16[512,1024]{1,0:T(8,128)(2,1)}, bf16[512,1024]{1,0:T(8,128)(2,1)}, u32[]{:S(2)}, u32[]{:S(2)}) collective-permute-start(bf16[512,1024]{1,0:T(8,128)(2,1)} %copy-done.53), channel_id=1, source_target_pairs={{0,4},{4,0},{8,12},{12,8},{16,20},{20,16},{24,28},{28,24},{1,5},{5... | collective-permute-start | bytes 3145736 | tf_op jit(solution)/shard_map/ppermute | solution.py:214
  966.7 29.4 %collective-permute-start.92 = (bf16[512,1024]{1,0:T(8,128)(2,1)}, bf16[512,1024]{1,0:T(8,128)(2,1)}, u32[]{:S(2)}, u32[]{:S(2)}) collective-permute-start(bf16[512,1024]{1,0:T(8,128)(2,1)} %copy-done.54), channel_id=1, source_target_pairs={{0,4},{4,0},{8,12},{12,8},{16,20},{20,16},{24,28},{28,24},{1,5},{5... | collective-permute-start | bytes 3145736 | tf_op jit(solution)/shard_map/ppermute | solution.py:214
  967.2 28.2 %collective-permute-start.48 = (bf16[512,768]{1,0:T(8,128)(2,1)}, bf16[512,768]{1,0:T(8,128)(2,1)}, u32[]{:S(2)}, u32[]{:S(2)}) collective-permute-start(bf16[512,768]{1,0:T(8,128)(2,1)} %constant_dynamic-update-slice_fusion.9.b_ref), channel_id=1, source_target_pairs={{0,4},{4,0},{8,12},{12,8},{16,20},{20,16},{24,28},{28,24},{1,5},{5... | collective-permute-start | bytes 2359304 | tf_op jit(solution)/shard_map/ppermute | solution.py:214
  990.8 100.5 %all-to-all-start.3 = ((bf16[4,128,1024]{2,1,0:T(8,128)(2,1)}), bf16[4,128,1024]{2,1,0:T(8,128)(2,1)S(1)}, u32[]{:S(2)}, u32[]{:S(2)}) async-start(bf16[4,128,1024]{2,1,0:T(8,128)(2,1)} %bitcast.59), calls=%async_computation.3 | async-start | bytes 2097152 | tf_op jit(solution)/shard_map/all_to_all | solution.py:224
  995.4 41.6 %collective-permute-start.72 = (bf16[512,1024]{1,0:T(8,128)(2,1)}, bf16[512,1024]{1,0:T(8,128)(2,1)S(1)}, u32[]{:S(2)}, u32[]{:S(2)}) collective-permute-start(bf16[512,1024]{1,0:T(8,128)(2,1)} %copy-done.56), channel_id=1, source_target_pairs={{0,4},{4,0},{8,12},{12,8},{16,20},{20,16},{24,28},{28,24},{1,5},{5... | collective-permute-start | bytes 3145736 | tf_op jit(solution)/shard_map/ppermute | solution.py:214
  996.0 46.2 %collective-permute-start.76 = (bf16[512,1024]{1,0:T(8,128)(2,1)}, bf16[512,1024]{1,0:T(8,128)(2,1)S(1)}, u32[]{:S(2)}, u32[]{:S(2)}) collective-permute-start(bf16[512,1024]{1,0:T(8,128)(2,1)} %copy-done.55), channel_id=1, source_target_pairs={{0,4},{4,0},{8,12},{12,8},{16,20},{20,16},{24,28},{28,24},{1,5},{5... | collective-permute-start | bytes 3145736 | tf_op jit(solution)/shard_map/ppermute | solution.py:214
  996.1 51.2 %collective-permute-start.80 = (bf16[512,1024]{1,0:T(8,128)(2,1)S(1)}, bf16[512,1024]{1,0:T(8,128)(2,1)S(1)}, u32[]{:S(2)}, u32[]{:S(2)}) collective-permute-start(bf16[512,1024]{1,0:T(8,128)(2,1)S(1)} %get-tuple-element.338.b_ref), channel_id=1, source_target_pairs={{0,4},{4,0},{8,12},{12,8},{16,20},{20,16},{24,28},{28,24},{1,5},{5... | collective-permute-start | bytes 3145736 | tf_op jit(solution)/shard_map/ppermute | solution.py:214
  1001.3 51.0 %collective-permute-start.38 = (bf16[2,128,768]{2,1,0:T(8,128)(2,1)}, bf16[2,128,768]{2,1,0:T(8,128)(2,1)}, u32[]{:S(2)}, u32[]{:S(2)}) collective-permute-start(bf16[2,128,768]{2,1,0:T(8,128)(2,1)} %get-tuple-element.93), channel_id=1, source_target_pairs={{0,8},{4,12},{8,0},{12,4},{16,24},{20,28},{24,16},{28,20},{1,9},{5... | collective-permute-start | bytes 1179656 | tf_op jit(solution)/shard_map/ppermute | solution.py:214
  1014.3 40.8 %collective-permute-start.41 = (bf16[2,128,768]{2,1,0:T(8,128)(2,1)}, bf16[2,128,768]{2,1,0:T(8,128)(2,1)S(1)}, u32[]{:S(2)}, u32[]{:S(2)}) collective-permute-start(bf16[2,128,768]{2,1,0:T(8,128)(2,1)} %get-tuple-element.95), channel_id=1, source_target_pairs={{0,8},{4,12},{8,0},{12,4},{16,24},{20,28},{24,16},{28,20},{1,9},{5... | collective-permute-start | bytes 1179656 | tf_op jit(solution)/shard_map/ppermute | solution.py:214
  1047.3 53.5 %collective-permute-start.86 = (bf16[2,1024,128]{2,1,0:T(8,128)(2,1)}, bf16[2,1024,128]{2,1,0:T(8,128)(2,1)}, u32[]{:S(2)}, u32[]{:S(2)}) collective-permute-start(bf16[2,1024,128]{2,1,0:T(8,128)(2,1)} %get-tuple-element.117), channel_id=1, source_target_pairs={{0,8},{4,12},{8,0},{12,4},{16,24},{20,28},{24,16},{28,20},{1,9},{5... | collective-permute-start | bytes 1572872 | tf_op jit(solution)/shard_map/ppermute | solution.py:214
  1052.3 50.5 %collective-permute-start.89 = (bf16[2,1024,128]{2,1,0:T(8,128)(2,1)}, bf16[2,1024,128]{2,1,0:T(8,128)(2,1)}, u32[]{:S(2)}, u32[]{:S(2)}) collective-permute-start(bf16[2,1024,128]{2,1,0:T(8,128)(2,1)} %get-tuple-element.119), channel_id=1, source_target_pairs={{0,8},{4,12},{8,0},{12,4},{16,24},{20,28},{24,16},{28,20},{1,9},{5... | collective-permute-start | bytes 1572872 | tf_op jit(solution)/shard_map/ppermute | solution.py:214
  1055.1 50.5 %collective-permute-start.93 = (bf16[2,1024,128]{2,1,0:T(8,128)(2,1)}, bf16[2,1024,128]{2,1,0:T(8,128)(2,1)}, u32[]{:S(2)}, u32[]{:S(2)}) collective-permute-start(bf16[2,1024,128]{2,1,0:T(8,128)(2,1)} %get-tuple-element.121), channel_id=1, source_target_pairs={{0,16},{4,20},{8,24},{12,28},{16,0},{20,4},{24,8},{28,12},{1,17},{... | collective-permute-start | bytes 1572872 | tf_op jit(solution)/shard_map/ppermute | solution.py:214
  1056.2 52.3 %collective-permute-start.97 = (bf16[2,1024,128]{2,1,0:T(8,128)(2,1)}, bf16[2,1024,128]{2,1,0:T(8,128)(2,1)}, u32[]{:S(2)}, u32[]{:S(2)}) collective-permute-start(bf16[2,1024,128]{2,1,0:T(8,128)(2,1)} %get-tuple-element.123), channel_id=1, source_target_pairs={{0,16},{4,20},{8,24},{12,28},{16,0},{20,4},{24,8},{28,12},{1,17},{... | collective-permute-start | bytes 1572872 | tf_op jit(solution)/shard_map/ppermute | solution.py:214
  1057.4 26.1 %collective-permute-start.42 = (bf16[128,768]{1,0:T(8,128)(2,1)S(1)}, bf16[128,768]{1,0:T(8,128)(2,1)S(1)}, u32[]{:S(2)}, u32[]{:S(2)}) collective-permute-start(bf16[128,768]{1,0:T(8,128)(2,1)S(1)} %fusion.77), channel_id=1, source_target_pairs={{0,16},{4,20},{8,24},{12,28},{16,0},{20,4},{24,8},{28,12},{1,17},{... | collective-permute-start | bytes 589832 | tf_op jit(solution)/shard_map/ppermute | solution.py:214
  1091.3 29.5 %all-to-all-start.1 = ((bf16[4,128,1024]{2,1,0:T(8,128)(2,1)}), bf16[4,128,1024]{2,1,0:T(8,128)(2,1)S(1)}, u32[]{:S(2)}, u32[]{:S(2)}) async-start(bf16[4,128,1024]{2,1,0:T(8,128)(2,1)} %bitcast.53), calls=%async_computation.1 | async-start | bytes 2097152 | tf_op jit(solution)/shard_map/all_to_all | solution.py:224
  1105.6 27.9 %collective-permute-start.81 = (bf16[2,128,1024]{2,1,0:T(8,128)(2,1)}, bf16[2,128,1024]{2,1,0:T(8,128)(2,1)}, u32[]{:S(2)}, u32[]{:S(2)}) collective-permute-start(bf16[2,128,1024]{2,1,0:T(8,128)(2,1)} %get-tuple-element.115), channel_id=1, source_target_pairs={{0,16},{4,20},{8,24},{12,28},{16,0},{20,4},{24,8},{28,12},{1,17},{... | collective-permute-start | bytes 1572872 | tf_op jit(solution)/shard_map/ppermute | solution.py:214
  1108.4 27.5 %collective-permute-start.39 = (bf16[128,768]{1,0:T(8,128)(2,1)}, bf16[128,768]{1,0:T(8,128)(2,1)}, u32[]{:S(2)}, u32[]{:S(2)}) collective-permute-start(bf16[128,768]{1,0:T(8,128)(2,1)} %fusion.76), channel_id=1, source_target_pairs={{0,16},{4,20},{8,24},{12,28},{16,0},{20,4},{24,8},{28,12},{1,17},{... | collective-permute-start | bytes 589832 | tf_op jit(solution)/shard_map/ppermute | solution.py:214
  1111.5 25.7 %collective-permute-start.43 = (bf16[128,768]{1,0:T(8,128)(2,1)}, bf16[128,768]{1,0:T(8,128)(2,1)}, u32[]{:S(2)}, u32[]{:S(2)}) collective-permute-start(bf16[128,768]{1,0:T(8,128)(2,1)} %fusion.63), channel_id=1, source_target_pairs={{0,3},{1,0},{2,1},{3,2},{4,7},{5,4},{6,5},{7,6},{8,11},{9,8},{10,9... | collective-permute-start | bytes 589832 | tf_op jit(solution)/shard_map/ppermute | solution.py:217
  1133.5 24.6 %collective-permute-start.87 = (bf16[1024,128]{1,0:T(8,128)(2,1)S(1)}, bf16[1024,128]{1,0:T(8,128)(2,1)}, u32[]{:S(2)}, u32[]{:S(2)}) collective-permute-start(bf16[1024,128]{1,0:T(8,128)(2,1)S(1)} %fusion.72), channel_id=1, source_target_pairs={{0,16},{4,20},{8,24},{12,28},{16,0},{20,4},{24,8},{28,12},{1,17},{... | collective-permute-start | bytes 786440 | tf_op jit(solution)/shard_map/ppermute | solution.py:214
  1152.7 25.1 %collective-permute-start.95 = (bf16[1024,128]{1,0:T(8,128)(2,1)S(1)}, bf16[1024,128]{1,0:T(8,128)(2,1)S(1)}, u32[]{:S(2)}, u32[]{:S(2)}) collective-permute-start(bf16[1024,128]{1,0:T(8,128)(2,1)S(1)} %fusion.33), channel_id=1, source_target_pairs={{0,2},{1,3},{2,0},{3,1},{4,6},{5,7},{6,4},{7,5},{8,10},{9,11},{10,... | collective-permute-start | bytes 786440 | tf_op jit(solution)/shard_map/ppermute | solution.py:217
  1154.0 23.8 %collective-permute-start.99 = (bf16[1024,128]{1,0:T(8,128)(2,1)S(1)}, bf16[1024,128]{1,0:T(8,128)(2,1)S(1)}, u32[]{:S(2)}, u32[]{:S(2)}) collective-permute-start(bf16[1024,128]{1,0:T(8,128)(2,1)S(1)} %fusion.32), channel_id=1, source_target_pairs={{0,1},{1,2},{2,3},{3,0},{4,5},{5,6},{6,7},{7,4},{8,9},{9,10},{10,1... | collective-permute-start | bytes 786440 | tf_op jit(solution)/shard_map/ppermute | solution.py:217
  1156.1 23.8 %collective-permute-start.71 = (bf16[128,1024]{1,0:T(8,128)(2,1)S(1)}, bf16[128,1024]{1,0:T(8,128)(2,1)S(1)}, u32[]{:S(2)}, u32[]{:S(2)}) collective-permute-start(bf16[128,1024]{1,0:T(8,128)(2,1)S(1)} %copy-done.106), channel_id=1, source_target_pairs={{0,16},{4,20},{8,24},{12,28},{16,0},{20,4},{24,8},{28,12},{1,17},{... | collective-permute-start | bytes 786440 | tf_op jit(solution)/shard_map/ppermute | solution.py:214
  1161.1 26.6 %collective-permute-start.79 = (bf16[128,1024]{1,0:T(8,128)(2,1)S(1)}, bf16[128,1024]{1,0:T(8,128)(2,1)S(1)}, u32[]{:S(2)}, u32[]{:S(2)}) collective-permute-start(bf16[128,1024]{1,0:T(8,128)(2,1)S(1)} %fusion.40), channel_id=1, source_target_pairs={{0,2},{1,3},{2,0},{3,1},{4,6},{5,7},{6,4},{7,5},{8,10},{9,11},{10,... | collective-permute-start | bytes 786440 | tf_op jit(solution)/shard_map/ppermute | solution.py:217
  (210 other events, 2719.2 us)

commit v2 on v1

v2 whole, which is shorter than its diff:
```python
import functools
import math

import jax
import jax.numpy as jnp
from jax import lax
from jax.experimental import pallas as pl
from jax.experimental.pallas import tpu as pltpu
from jax.sharding import PartitionSpec as P

HD = 64
f32 = jnp.float32
bf16 = jnp.bfloat16
VMEM_LIMIT = 56 * 2**20
PATHS = ((2, 4), (4, 2))


def params(**more):
    return pltpu.CompilerParams(vmem_limit_bytes=VMEM_LIMIT, **more)


def dot(a, b, dims):
    return lax.dot_general(a, b, (dims, ((), ())), preferred_element_type=f32)


def sinusoid(steps, model_width):
    half_width = model_width // 2
    freqs = jnp.exp(-math.log(10000.0) * jnp.arange(half_width, dtype=f32) / half_width)
    angles = steps[:, None] * freqs[None, :]
    return jnp.concatenate([jnp.sin(angles), jnp.cos(angles)], axis=-1).astype(bf16)


class Gathered:
    def __init__(self, own, pieces, plan, lead, start):
        self.arrays = [own] + pieces
        self.plan = plan
        self.lead = len(lead)
        self.start = start
        self.dims = own.shape
        self.copies = 1 + sum(len(masks) for _, masks in plan)

    def scratch(self, shards):
        return [
            pltpu.VMEM((shards,) + self.dims, bf16),
            pltpu.SemaphoreType.DMA((shards, self.copies)),
        ]

    def _copies(self, refs, place, into, sems, shard):
        lead = (slice(None),) * self.lead
        made = []
        for ref, (path, masks) in zip(refs[1:], self.plan):
            for i, mask in enumerate(masks):
                at = lead + (pl.ds(self.start, self.dims[-2]),)
                made.append(
                    pltpu.make_async_copy(
                        ref.at[i, shard - 1].at[at],
                        into.at[(shard,) + lead + (place ^ mask, path)],
                        sems.at[shard, len(made)],
                    )
                )
        return made

    def start_all(self, refs, place, into, sems, shards):
        pltpu.make_async_copy(refs[0], into.at[0], sems.at[0, 0]).start()
        for shard in range(1, shards):
            for copy in self._copies(refs, place, into, sems, shard):
                copy.start()

    def wait(self, refs, place, into, sems, shard):
        @pl.when(shard == 0)
        def _():
            pltpu.make_async_copy(refs[0], into.at[0], sems.at[0, 0]).wait()

        @pl.when(shard > 0)
        def _():
            for copy in self._copies(refs, place, into, sems, shard):
                copy.wait()


HBM = pl.BlockSpec(memory_space=pl.ANY)
SMEM = pl.BlockSpec(memory_space=pltpu.SMEM)


def whole(shape):
    return pl.BlockSpec(shape, lambda *_: (0,) * len(shape))


def cost(flops, transcendentals, moved):
    return pl.CostEstimate(flops=flops, transcendentals=transcendentals, bytes_accessed=moved)


def attend_body(
    first, shards, gathered, place_ref, x_ref, bias_ref, *refs
):
    n = len(gathered.arrays)
    w_refs, (qkv_ref, p_ref, c_ref, w, sems) = refs[:n], refs[n:]
    s, pair = pl.program_id(0), pl.program_id(1)
    place = place_ref[0]
    cols = w.shape[-1]

    @pl.when((s == 0) & (pair == 0))
    def _():
        if first == 0:
            gathered.start_all(w_refs, place, w, sems, shards)
        else:
            for shard in range(1, shards + 1):
                for copy in gathered._copies(w_refs, place, w, sems, shard):
                    copy.start()

    @pl.when(pair == 0)
    def _():
        shard = s + first
        gathered.wait(w_refs, place, w, sems, shard)
        for c in range(3):
            wide = w[shard, c].reshape(x_ref.shape[1], cols)
            out = dot(x_ref[...], wide, ((1,), (0,))) + bias_ref[0, c]
            qkv_ref[0, :, c * cols : (c + 1) * cols] = out.astype(bf16)

    at = pl.multiple_of(pair * 2 * HD, 2 * HD)
    q = qkv_ref[0, :, pl.ds(at, 2 * HD)]
    k = qkv_ref[0, :, pl.ds(cols + at, 2 * HD)]
    v = qkv_ref[0, :, pl.ds(2 * cols + at, 2 * HD)]
    lane = lax.broadcasted_iota(jnp.int32, q.shape, 1)
    joined = None
    for hh in range(2):
        mine = (lane // HD) == hh
        kh = jnp.where(mine, k, jnp.zeros_like(k))
        st = dot(kh, q, ((1,), (1,))) * 0.125
        top = jnp.max(st, axis=0, keepdims=True)
        e = jnp.exp(st - top)
        p = (e * (1.0 / jnp.sum(e, axis=0, keepdims=True))).astype(bf16)
        p_ref[0, hh] = p
        c = dot(p, v, ((0,), (0,)))
        joined = c if joined is None else jnp.where(mine, c, joined)
    c_ref[0] = joined.astype(bf16)


def attend(first, shards, gathered, place, x, bias):
    length, width = x.shape
    cols = gathered.dims[-1]
    pairs = cols // (2 * HD)
    n_w = len(gathered.arrays)
    return pl.pallas_call(
        functools.partial(attend_body, first, shards, gathered),
        grid=(shards, pairs),
        out_shape=[
            jax.ShapeDtypeStruct((shards, length, 3 * cols), bf16),
            jax.ShapeDtypeStruct((shards, 2 * pairs, length, length), bf16),
            jax.ShapeDtypeStruct((shards, length, cols), bf16),
        ],
        in_specs=[SMEM, whole(x.shape), pl.BlockSpec((1, 3, 1, cols), lambda s, i: (s, 0, 0, 0))]
        + [HBM] * n_w,
        out_specs=[
            pl.BlockSpec((1, length, 3 * cols), lambda s, i: (s, 0, 0)),
            pl.BlockSpec((1, 2, length, length), lambda s, i: (s, i, 0, 0)),
            pl.BlockSpec((1, length, 2 * HD), lambda s, i: (s, 0, i)),
        ],
        scratch_shapes=gathered.scratch(shards + (1 if first else 0)),
        compiler_params=params(),
        cost_estimate=cost(
            shards * (6 * length * width * cols + 8 * pairs * length * length * HD),
            shards * 2 * pairs * length * length,
            shards * (6 * width * cols + 4 * pairs * length * length),
        ),
        name="attend",
    )(place, x, bias, *gathered.arrays)


def norm_stats(values):
    center = values - jnp.mean(values, axis=-1, keepdims=True)
    inv = lax.rsqrt(jnp.mean(center * center, axis=-1, keepdims=True) + 1e-05)
    return center * inv, inv


def norm_back(grad, n, inv, gain):
    gn = grad * gain
    return (gn - jnp.mean(gn, -1, keepdims=True) - n * jnp.mean(gn * n, -1, keepdims=True)) * inv


def up_body(shards, g_out, g_up, place_ref, near_ref, far_ref, x_ref, te_ref, vec_ref, bias_ref, *refs):
    n_out, n_up = len(g_out.arrays), len(g_up.arrays)
    shared = [refs[0]] + list(refs[1:n_out])
    up_refs = [refs[n_out]] + list(refs[1:n_out])
    n1_ref, inv_ref, low_ref, act_ref, slope_ref, wo, o_sems, wu, u_sems, acc = refs[n_out + 1 :]
    s = pl.program_id(0)
    place = place_ref[0]
    length, width = acc.shape

    @pl.when(s == 0)
    def _():
        g_out.start_all(shared, place, wo, o_sems, shards)
        g_up.start_all(up_refs, place, wu, u_sems, shards)
        g_out.wait(shared, place, wo, o_sems, 0)
        acc[...] = dot(near_ref[0], wo[0].reshape(-1, width), ((1,), (0,)))
        for shard in range(1, shards):
            for copy in g_out._copies(shared, place, wo, o_sems, shard):
                copy.wait()
            acc[...] += dot(far_ref[shard - 1], wo[shard].reshape(-1, width), ((1,), (0,)))

        def rows(i, _):
            at = pl.ds(pl.multiple_of(i * 64, 64), 64)
            start = x_ref[at, :].astype(f32) + te_ref[...]
            n1, inv = norm_stats(start + (acc[at, :] + vec_ref[0:1, :]))
            n1_ref[at, :] = n1
            inv_ref[at, :] = jnp.broadcast_to(inv, (64, inv_ref.shape[1]))
            low_ref[at, :] = (n1 * vec_ref[1:2, :] + vec_ref[2:3, :]).astype(bf16)
            return 0

        lax.fori_loop(0, length // 64, rows, 0)

    g_up.wait(up_refs, place, wu, u_sems, s)
    units = wu.shape[-1]
    for n in range(units // 256):
        span = slice(n * 256, (n + 1) * 256)
        u = dot(low_ref[...], wu[s, :, :, :, span].reshape(width, 256), ((1,), (0,)))
        u = u + bias_ref[0, :, span]
        phi = 0.5 + 0.5 * lax.erf(u * (2.0**-0.5))
        act_ref[0, :, span] = (u * phi).astype(bf16)
        slope_ref[0, :, span] = (
            phi + u * jnp.exp(-0.5 * u * u) * (2.0 * math.pi) ** -0.5
        ).astype(bf16)


def up_project(g_out, g_up, place, near, far, x, time_embed, vec, bias):
    length, width = x.shape
    shards = far.shape[0] + 1
    units = g_up.dims[-1]
    block = pl.BlockSpec((1, length, units), lambda s: (s, 0, 0))
    return pl.pallas_call(
        functools.partial(up_body, shards, g_out, g_up),
        grid=(shards,),
        out_shape=[
            jax.ShapeDtypeStruct((length, width), f32),
            jax.ShapeDtypeStruct((length, 128), f32),
            jax.ShapeDtypeStruct((length, width), bf16),
            jax.ShapeDtypeStruct((shards, length, units), bf16),
            jax.ShapeDtypeStruct((shards, length, units), bf16),
        ],
        in_specs=[
            SMEM,
            whole(near.shape),
            whole(far.shape),
            whole(x.shape),
            whole(time_embed.shape),
            whole(vec.shape),
            pl.BlockSpec((1, 1, units), lambda s: (s, 0, 0)),
        ]
        + [HBM] * (len(g_out.arrays) + 1),
        out_specs=[
            whole((length, width)),
            whole((length, 128)),
            whole((length, width)),
            block,
            block,
        ],
        scratch_shapes=g_out.scratch(shards) + g_up.scratch(shards) + [pltpu.VMEM((length, width), f32)],
        compiler_params=params(),
        cost_estimate=cost(
            2 * length * width * (width + shards * units),
            2 * shards * length * units,
            2 * width * (width + shards * units) + 4 * shards * length * units,
        ),
        name="up_project",
    )(place, near, far, x, time_embed, vec, bias, *g_out.arrays, g_up.arrays[0])


def down_body(shards, gathered, place_ref, live_ref, act_ref, n1_ref, cot_ref, vec_ref, *refs):
    n = len(gathered.arrays)
    w_refs, (out_ref, gs_ref, bg_ref, sums_ref, w, sems, acc) = refs[:n], refs[n:]
    s = pl.program_id(0)
    place = place_ref[0]
    length, width = acc.shape

    @pl.when(s == 0)
    def _():
        gathered.start_all(w_refs, place, w, sems, shards)

    gathered.wait(w_refs, place, w, sems, s)
    part = dot(act_ref[0], w[s].reshape(-1, width), ((1,), (0,)))

    @pl.when(s == 0)
    def _():
        acc[...] = part

    @pl.when(s > 0)
    def _():
        acc[...] += part

    @pl.when(s == shards - 1)
    def _():
        live = live_ref[0]

        def rows(i, sums):
            at = pl.ds(pl.multiple_of(i * 64, 64), 64)
            normed = n1_ref[at, :] * vec_ref[1:2, :] + vec_ref[2:3, :]
            n2, inv = norm_stats(normed + (acc[at, :] + vec_ref[0:1, :]))
            out_ref[at, :] = (n2 * vec_ref[3:4, :] + vec_ref[4:5, :]).astype(bf16)
            grad = cot_ref[at, :].astype(f32) * live
            second = norm_back(grad, n2, inv, vec_ref[3:4, :])
            gs_ref[at, :] = second
            low = second.astype(bf16)
            bg_ref[at, :] = low
            add = (low.astype(f32), grad * n2, grad)
            return tuple(a + jnp.sum(b, axis=0, keepdims=True) for a, b in zip(sums, add))

        zero = jnp.zeros((1, width), f32)
        sums = lax.fori_loop(0, length // 64, rows, (zero, zero, zero))
        for i, v in enumerate(sums):
            sums_ref[i : i + 1, :] = v


def down_project(gathered, place, live, act, n1, cot, vec):
    shards, length, units = act.shape
    width = n1.shape[1]
    return pl.pallas_call(
        functools.partial(down_body, shards, gathered),
        grid=(shards,),
        out_shape=[
            jax.ShapeDtypeStruct((length, width), bf16),
            jax.ShapeDtypeStruct((length, width), f32),
            jax.ShapeDtypeStruct((length, width), bf16),
            jax.ShapeDtypeStruct((3, width), f32),
        ],
        in_specs=[
            SMEM,
            SMEM,
            pl.BlockSpec((1, length, units), lambda s: (s, 0, 0)),
            whole(n1.shape),
            whole(cot.shape),
            whole(vec.shape),
        ]
        + [HBM] * len(gathered.arrays),
        out_specs=[whole((length, width))] * 3 + [whole((3, width))],
        scratch_shapes=gathered.scratch(shards) + [pltpu.VMEM((length, width), f32)],
        compiler_params=params(),
        cost_estimate=cost(
            2 * length * width * shards * units,
            0,
            2 * shards * units * (width + length) + 12 * length * width,
        ),
        name="down_project",
    )(place, live, act, n1, cot, vec, *gathered.arrays)


def up_back_body(shards, g_down, g_up, place_ref, bg_ref, slope_ref, gs_ref, n1_ref, inv_ref, vec_ref, *refs):
    n_d, n_u = len(g_down.arrays), len(g_up.arrays)
    d_refs, u_refs = refs[:n_d], refs[n_d : n_d + n_u]
    ug_ref, bias_ref, gf_ref, mg_ref, sums_ref, wd, d_sems, wu, u_sems, acc = refs[n_d + n_u :]
    s = pl.program_id(0)
    place = place_ref[0]
    length, width = acc.shape

    @pl.when(s == 0)
    def _():
        g_down.start_all(d_refs, place, wd, d_sems, shards)
        g_up.start_all(u_refs, place, wu, u_sems, shards)
        acc[...] = gs_ref[...]

    g_down.wait(d_refs, place, wd, d_sems, s)
    units = ug_ref.shape[2]
    for n in range(units // 256):
        span = slice(n * 256, (n + 1) * 256)
        rows = wd[s, 2 * n : 2 * n + 2].reshape(256, width)
        grad = dot(bg_ref[...], rows, ((1,), (1,)))
        low = (grad * slope_ref[0, :, span].astype(f32)).astype(bf16)
        ug_ref[0, :, span] = low
        bias_ref[0, :, span] = jnp.sum(low.astype(f32), axis=0, keepdims=True)
    g_up.wait(u_refs, place, wu, u_sems, s)
    acc[...] += dot(ug_ref[0], wu[s].reshape(width, units), ((1,), (1,)))

    @pl.when(s == shards - 1)
    def _():
        def rows(i, sums):
            at = pl.ds(pl.multiple_of(i * 64, 64), 64)
            n1, grad = n1_ref[at, :], acc[at, :]
            first = norm_back(grad, n1, inv_ref[at, 0:1], vec_ref[1:2, :])
            gf_ref[at, :] = first
            low = first.astype(bf16)
            mg_ref[at, :] = low
            add = (low.astype(f32), grad * n1, grad)
            return tuple(a + jnp.sum(b, axis=0, keepdims=True) for a, b in zip(sums, add))

        zero = jnp.zeros((1, width), f32)
        sums = lax.fori_loop(0, length // 64, rows, (zero, zero, zero))
        for i, v in enumerate(sums):
            sums_ref[i : i + 1, :] = v


def up_back(g_down, g_up, place, bg, slope, gs, n1, inv, vec):
    shards, length, units = slope.shape
    width = n1.shape[1]
    block = pl.BlockSpec((1, length, units), lambda s: (s, 0, 0))
    return pl.pallas_call(
        functools.partial(up_back_body, shards, g_down, g_up),
        grid=(shards,),
        out_shape=[
            jax.ShapeDtypeStruct((shards, length, units), bf16),
            jax.ShapeDtypeStruct((shards, 1, units), f32),
            jax.ShapeDtypeStruct((length, width), f32),
            jax.ShapeDtypeStruct((length, width), bf16),
            jax.ShapeDtypeStruct((3, width), f32),
        ],
        in_specs=[
            SMEM,
            whole(bg.shape),
            block,
            whole(gs.shape),
            whole(n1.shape),
            whole(inv.shape),
            whole(vec.shape),
        ]
        + [HBM] * (len(g_down.arrays) + len(g_up.arrays)),
        out_specs=[
            block,
            pl.BlockSpec((1, 1, units), lambda s: (s, 0, 0)),
            whole((length, width)),
            whole((length, width)),
            whole((3, width)),
        ],
        scratch_shapes=g_down.scratch(shards)
        + g_up.scratch(shards)
        + [pltpu.VMEM((length, width), f32)],
        compiler_params=params(),
        cost_estimate=cost(
            4 * length * width * shards * units,
            0,
            4 * shards * units * (width + length) + 16 * length * width,
        ),
        name="up_back",
    )(place, bg, slope, gs, n1, inv, vec, *g_down.arrays, *g_up.arrays)


def attend_back_body(shards, g_out, g_qkv, place_ref, mg_ref, near_ref, far_ref, pn_ref, pf_ref, gf_ref, *refs):
    n_o, n_q = len(g_out.arrays), len(g_qkv.arrays)
    o_refs, q_refs = refs[:n_o], refs[n_o : n_o + n_q]
    pg_ref, gt_ref, bias_ref, tg_ref, wo, o_sems, wq, q_sems, acc, cg = refs[n_o + n_q :]
    s, pair = pl.program_id(0), pl.program_id(1)
    place = place_ref[0]
    length, width = acc.shape
    cols = wq.shape[-1]

    @pl.when((s == 0) & (pair == 0))
    def _():
        g_out.start_all(o_refs, place, wo, o_sems, shards)
        g_qkv.start_all(q_refs, place, wq, q_sems, shards)
        acc[...] = gf_ref[...]

    @pl.when(pair == 0)
    def _():
        g_out.wait(o_refs, place, wo, o_sems, s)
        cg[...] = dot(mg_ref[...], wo[s].reshape(cols, width), ((1,), (1,))).astype(bf16)

    at = pl.multiple_of(pair * 2 * HD, 2 * HD)

    def one(qkv, p_of):
        q = qkv[0, :, pl.ds(at, 2 * HD)]
        k = qkv[0, :, pl.ds(cols + at, 2 * HD)]
        v = qkv[0, :, pl.ds(2 * cols + at, 2 * HD)]
        g = cg[:, pl.ds(at, 2 * HD)]
        lane = lax.broadcasted_iota(jnp.int32, q.shape, 1)
        dq = dk = dv = None
        for hh in range(2):
            mine = (lane // HD) == hh
            zero = jnp.zeros_like(q)
            gh = jnp.where(mine, g, zero)
            kh = jnp.where(mine, k, zero)
            qh = jnp.where(mine, q, zero)
            p = p_of[0, hh]
            dpt = dot(v, gh, ((1,), (1,)))
            pf = p.astype(f32)
            row = jnp.sum(pf * dpt, axis=0, keepdims=True)
            ds = (pf * (dpt - row)).astype(bf16)
            a = dot(p, gh, ((1,), (0,)))
            b = dot(ds, qh, ((1,), (0,)))
            c = dot(ds, kh, ((0,), (0,)))
            dv = a if dv is None else dv + a
            dk = b if dk is None else dk + b
            dq = c if dq is None else dq + c
        for c, g in enumerate((dq * 0.125, dk * 0.125, dv)):
            low = g.astype(bf16)
            pg_ref[0, :, pl.ds(c * cols + at, 2 * HD)] = low
            bias_ref[0, :, pl.ds(c * cols + at, 2 * HD)] = jnp.sum(
                low.astype(f32), axis=0, keepdims=True
            )

    @pl.when(s == 0)
    def _():
        one(near_ref, pn_ref)

    @pl.when(s > 0)
    def _():
        one(far_ref, pf_ref)

    @pl.when(pair == pl.num_programs(1) - 1)
    def _():
        g_qkv.wait(q_refs, place, wq, q_sems, s)
        for c in range(3):
            acc[...] += dot(
                pg_ref[0, :, c * cols : (c + 1) * cols],
                wq[s, c].reshape(width, cols),
                ((1,), (1,)),
            )

    @pl.when((pair == pl.num_programs(1) - 1) & (s == shards - 1))
    def _():
        def rows(i, total):
            rows_at = pl.ds(pl.multiple_of(i * 64, 64), 64)
            grad = acc[rows_at, :]
            gt_ref[rows_at, :] = grad.astype(bf16)
            return total + jnp.sum(grad, axis=0, keepdims=True)

        tg_ref[...] = lax.fori_loop(0, length // 64, rows, jnp.zeros((1, width), f32))


def attend_back(g_out, g_qkv, place, mg, near, far, p_near, p_far, gf):
    length, width = mg.shape
    shards = far.shape[0] + 1
    cols = g_qkv.dims[-1]
    pairs = cols // (2 * HD)
    last = pairs - 1

    def before(s, i):
        return (0, jnp.where(s == 0, i, last), 0, 0)

    def after(s, i):
        return (jnp.maximum(s - 1, 0), jnp.where(s == 0, 0, i), 0, 0)

    return pl.pallas_call(
        functools.partial(attend_back_body, shards, g_out, g_qkv),
        grid=(shards, pairs),
        out_shape=[
            jax.ShapeDtypeStruct((shards, length, 3 * cols), bf16),
            jax.ShapeDtypeStruct((length, width), bf16),
            jax.ShapeDtypeStruct((shards, 1, 3 * cols), f32),
            jax.ShapeDtypeStruct((1, width), f32),
        ],
        in_specs=[
            SMEM,
            whole(mg.shape),
            whole(near.shape),
            pl.BlockSpec((1, length, 3 * cols), lambda s, i: (jnp.maximum(s - 1, 0), 0, 0)),
            pl.BlockSpec((1, 2, length, length), before),
            pl.BlockSpec((1, 2, length, length), after),
            whole(gf.shape),
        ]
        + [HBM] * (len(g_out.arrays) + len(g_qkv.arrays)),
        out_specs=[
            pl.BlockSpec((1, length, 3 * cols), lambda s, i: (s, 0, 0)),
            whole((length, width)),
            pl.BlockSpec((1, 1, 3 * cols), lambda s, i: (s, 0, 0)),
            whole((1, width)),
        ],
        scratch_shapes=g_out.scratch(shards)
        + g_qkv.scratch(shards)
        + [pltpu.VMEM((length, width), f32), pltpu.VMEM((length, cols), bf16)],
        compiler_params=params(),
        cost_estimate=cost(
            shards * (8 * length * width * cols + 20 * pairs * length * length * HD),
            0,
            shards * (8 * width * cols + 4 * pairs * length * length) + 8 * length * width,
        ),
        name="attend_back",
    )(place, mg, near, far, p_near, p_far, gf, *g_out.arrays, *g_qkv.arrays)


def weight_grad_body(order, n_pairs, place_ref, *refs):
    ins = refs[: 4 * n_pairs]
    keep_ref, send_ref = refs[4 * n_pairs : 4 * n_pairs + 2]
    turned = refs[4 * n_pairs + 2 :]
    place = place_ref[0]
    rows = keep_ref.shape[2]

    @pl.when(pl.program_id(0) == 0)
    def _():
        for p in range(n_pairs):
            for half in range(2):
                feature_ref = ins[4 * p + half]
                length = feature_ref.shape[0]
                for j in range(4):
                    at = pl.multiple_of((place ^ (2 * j)) * rows, rows)
                    block = feature_ref[:, pl.ds(at, rows)]
                    turned[p][j * rows : (j + 1) * rows, half * length : (half + 1) * length] = block.T

    at = 0
    for p in range(n_pairs):
        b_ref, b2_ref = ins[4 * p + 2 : 4 * p + 4]
        length, cols = b_ref.shape[1:]
        for n in range(cols // 256):
            span = slice(n * 256, (n + 1) * 256)
            g = dot(turned[p][:, :length], b_ref[0, :, span], ((1,), (0,)))
            g += dot(turned[p][:, length:], b2_ref[0, :, span], ((1,), (0,)))
            g = g.astype(bf16)
            for out, picks in ((keep_ref, order[:2]), (send_ref, order[2:])):
                for i, j in enumerate(picks):
                    out[0, i, :, at : at + 256] = g[j * rows : (j + 1) * rows]
            at += 256


def weight_grad(path, place, groups):
    order = (0, 2, 1, 3) if path == 0 else (0, 1, 2, 3)
    shards, length, _ = groups[0][2].shape
    half = shards // 2
    rows = groups[0][0].shape[1] // 8
    cols = sum(g[2].shape[2] for g in groups)
    base = path * half
    specs, args, scratch = [], [], []
    for feature, feature2, b, b2 in groups:
        block = pl.BlockSpec((1,) + b.shape[1:], lambda s: (s + base, 0, 0))
        specs += [whole(feature.shape)] * 2 + [block] * 2
        args += [feature, feature2, b, b2]
        scratch.append(pltpu.VMEM((4 * rows, 2 * length), bf16))
    out = jax.ShapeDtypeStruct((half, 2, rows, cols), bf16)
    return pl.pallas_call(
        functools.partial(weight_grad_body, order, len(groups)),
        grid=(half,),
        out_shape=[out, out],
        in_specs=[SMEM] + specs,
        out_specs=[pl.BlockSpec((1, 2, rows, cols), lambda s: (s, 0, 0, 0))] * 2,
        scratch_shapes=scratch,
        compiler_params=params(),
        cost_estimate=cost(
            half * 16 * rows * length * cols,
            0,
            half * (4 * length * cols + 8 * rows * cols) + 4 * length * 8 * rows,
        ),
        name="weight_grad",
    )(place, *args)


def on_device(
    tokens,
    timesteps,
    buckets,
    counts,
    w_time,
    table,
    w_qkv,
    b_qv,
    w_out,
    b_out,
    gain1,
    shift1,
    w_up,
    b_up,
    w_down,
    b_down,
    gain2,
    shift2,
    cotangent,
):
    mpn = lax.axis_size("mp")
    dpn = lax.axis_size("dp")
    extra = dpn.bit_length() - 4
    me = lax.axis_index("dp")
    z = lax.axis_index("mp")
    q8 = me >> extra
    width = w_time.shape[0]
    positions, slots = tokens.shape[:2]
    length = positions * mpn
    head_cols = w_qkv.shape[2]
    units = w_up.shape[1]

    def flip(x, mask):
        step = mask << extra
        return lax.ppermute(x, "dp", [(i, i ^ step) for i in range(dpn)])

    def shift(x, s):
        return lax.ppermute(x, "mp", [(i, (i + s) % mpn) for i in range(mpn)])

    def to_items(x):
        x = lax.all_to_all(jnp.moveaxis(x, 1, 0), "mp", 0, 0, tiled=False)
        return x.reshape(length, width)

    def to_positions(x):
        x = lax.all_to_all(x.reshape(mpn, positions, width), "mp", 0, 0, tiled=False)
        return jnp.moveaxis(x, 0, 1)

    def spread(arrived):
        pieces, plan = [], []
        for path, (first, second) in enumerate(PATHS):
            mine = jnp.stack([a[path] for a in arrived])
            held = jnp.stack([mine, flip(mine, first)])
            far = flip(held, second)
            near = (0, first)
            beyond = (second, first | second)
            pieces += [held, far, flip(held, 1), flip(far, 1)]
            plan += [(path, m) for m in (near, beyond)]
            plan += [(path, tuple(v ^ 1 for v in m)) for m in (near, beyond)]
        return pieces, plan

    def split(shard, axis):
        dims = shard.shape
        return shard.reshape(dims[:axis] + (8, 2, dims[axis] // 16) + dims[axis + 1 :])

    def eighth(shaped, axis):
        return jnp.moveaxis(lax.dynamic_index_in_dim(shaped, q8, axis, False), axis, 0)

    def along_z(part):
        return [shift(part, s) for s in range(1, mpn)]

    place = q8.astype(jnp.int32)[None]
    own_qkv, own_out, own_up, own_down = split(w_qkv, 1), split(w_out, 0), split(w_up, 0), split(w_down, 0)

    z_qkv = along_z(eighth(own_qkv, 1))
    pieces, plan = spread(z_qkv)
    g_qkv = Gathered(own_qkv, pieces, plan, (3,), 0)

    part = jnp.concatenate([eighth(own_out, 0), eighth(own_up, 0)], axis=1)
    part, _ = lax.optimization_barrier((part, z_qkv))
    z_up = along_z(part)
    pieces, plan = spread(z_up)
    g_out = Gathered(own_out, pieces, plan, (), 0)
    g_up = Gathered(own_up, pieces, plan, (), own_out.shape[2])

    part, _ = lax.optimization_barrier((eighth(own_down, 0), z_up))
    z_down = along_z(part)
    pieces, plan = spread(z_down)
    g_down = Gathered(own_down, pieces, plan, (), 0)

    biases = jnp.concatenate([b_up, b_qv[0], b_qv[1]])
    biases = jnp.stack([biases] + [shift(biases, s) for s in range(1, mpn)])
    up_bias = biases[:, None, :units]
    qkv_bias = biases[:, units:].reshape(mpn, 2, 1, head_cols)
    qkv_bias = jnp.stack([qkv_bias[:, 0], jnp.zeros_like(qkv_bias[:, 0]), qkv_bias[:, 1]], axis=1)

    total_live = jnp.sum(counts).astype(f32)
    weighting = 1.0 / total_live
    live = (z < lax.dynamic_index_in_dim(counts, me, 0, True)).astype(f32)
    my_step = lax.dynamic_index_in_dim(timesteps, z, 0, True)
    my_bucket = lax.dynamic_index_in_dim(buckets, z, 0, False)
    time_embed = jnp.dot(
        sinusoid(my_step.astype(f32), width), w_time, preferred_element_type=f32
    ) + lax.dynamic_index_in_dim(table, my_bucket, 0, True)

    x = to_items(tokens)
    hidden = (x.astype(f32) + time_embed).astype(bf16)

    g_near = Gathered(own_qkv, [], [], (3,), 0)
    qkv_near, p_near, ctx_near = attend(0, 1, g_near, place, hidden, qkv_bias[:1])
    qkv_far, p_far, ctx_far = attend(1, mpn - 1, g_qkv, place, hidden, qkv_bias[1:])
    n1, inv1, normed_low, active, slope = up_project(
        g_out, g_up, place, ctx_near, ctx_far, x, time_embed, jnp.stack([b_out, gain1, shift1]), up_bias
    )
    late_cot, _ = lax.optimization_barrier((cotangent, z_down))
    cot = to_items(late_cot)
    output, grad_second, branch_grad, sums2 = down_project(
        g_down, place, live, active, n1, cot, jnp.stack([b_down, gain1, shift1, gain2, shift2])
    )
    output = to_positions(output)

    def reduced(groups):
        total = None
        for path, (first, second) in enumerate(PATHS):
            keep, sent = weight_grad(path, place, groups)
            came = flip(sent, first)
            passed = (keep[:, 1].astype(f32) + came[:, 1].astype(f32)).astype(bf16)
            part = keep[:, 0].astype(f32) + came[:, 0].astype(f32) + flip(passed, second).astype(f32)
            for i in range(mpn // 2):
                s = path * mpn // 2 + i
                piece = part[i] if s == 0 else shift(part[i].astype(bf16), -s).astype(f32)
                total = piece if total is None else total + piece
        for t in reversed(range(extra)):
            half = total.shape[0] // 2
            bit = (me >> t) & 1
            keep = lax.dynamic_slice_in_dim(total, bit * half, half, 0)
            sent = lax.dynamic_slice_in_dim(total, (1 - bit) * half, half, 0)
            total = keep + lax.ppermute(sent, "dp", [(i, i ^ (1 << t)) for i in range(dpn)])
        return total * weighting

    active2 = flip(active, 1)
    low2 = flip(normed_low, 1)
    ctx = jnp.concatenate([ctx_near, ctx_far])
    ctx2 = flip(ctx, 1)
    hidden2 = flip(hidden, 1)
    branch_grad2 = flip(branch_grad, 1)
    grad_w_down = reduced([(branch_grad, branch_grad2, active, active2)]).T
    up_grad, bias_up, grad_first, mixing_grad, sums1 = up_back(
        g_down, g_up, place, branch_grad, slope, grad_second, n1, inv1, jnp.stack([b_out, gain1, shift1])
    )
    grad_w_up = reduced([(normed_low, low2, up_grad, flip(up_grad, 1))])
    proj_grad, grad_tokens, bias_proj, time_grad = attend_back(
        g_out, g_qkv, place, mixing_grad, qkv_near, qkv_far, p_near, p_far, grad_first
    )
    both_grads = reduced(
        [
            (hidden, hidden2, proj_grad, flip(proj_grad, 1)),
            (mixing_grad, flip(mixing_grad, 1), ctx, ctx2),
        ]
    )
    grad_w_qkv = both_grads[:, : 3 * head_cols].reshape(-1, 3, head_cols)
    grad_w_qkv = jnp.moveaxis(grad_w_qkv, 1, 0)
    grad_w_out = both_grads[:, 3 * head_cols :].T
    grad_tokens = to_positions(grad_tokens).astype(f32)

    devices = dpn * mpn

    def in_order(parts):
        turned = jnp.stack([parts[-i % mpn] for i in range(mpn)] * 2)
        return lax.dynamic_slice_in_dim(turned, (mpn - z) % mpn, mpn, 0).reshape(-1)

    vectors = [
        in_order(bias_proj[:, 0, :head_cols]),
        in_order(bias_proj[:, 0, 2 * head_cols :]),
        sums1[0],
        sums1[1],
        sums1[2],
        sums2[0],
        sums2[1],
        sums2[2],
        in_order(bias_up[:, 0]),
    ]
    spread_out = jnp.concatenate([v.reshape(devices, -1) for v in vectors], axis=1)
    facts = jnp.stack([my_step[0].astype(f32), my_bucket.astype(f32)])
    facts = jnp.broadcast_to(facts[None], (devices, 2))
    both = ("dp", "mp")
    gathered = lax.all_to_all(jnp.concatenate([spread_out, facts], axis=1), both, 0, 0, tiled=True)
    summed = jnp.sum(gathered[:, :-2], axis=0) * weighting
    steps, rows_of = gathered[:, -2], gathered[:, -1]
    per = width // devices
    small = [summed[i * per : (i + 1) * per] for i in range(8)]
    grad_b_up = summed[8 * per :]
    grads = lax.all_to_all(time_grad.reshape(devices, per), both, 0, 0, tiled=True)
    high = lax.Precision.HIGHEST
    grad_w_time = (
        jnp.einsum("nd,ne->de", sinusoid(steps, width).astype(f32), grads, precision=high)
        * weighting
    )
    onehot = (rows_of[:, None] == jnp.arange(table.shape[0], dtype=f32)[None, :]).astype(f32)
    grad_table = jnp.einsum("nb,nd->bd", onehot, grads, precision=high) * weighting
    return (
        output,
        grad_tokens,
        grad_w_time,
        grad_table,
        grad_w_qkv,
        jnp.stack(small[:2]),
        grad_w_out,
        small[2],
        small[3],
        small[4],
        grad_w_up,
        grad_b_up,
        grad_w_down,
        small[5],
        small[6],
        small[7],
    )


def solution(mesh):
    return jax.shard_map(
        on_device,
        mesh=mesh,
        in_specs=(
            P("mp", "dp", None),
            P("dp"),
            P("dp"),
            P(),
            P(),
            P(),
            P(None, None, "mp"),
            P(None, "mp"),
            P("mp", None),
            P(),
            P(),
            P(),
            P(None, "mp"),
            P("mp"),
            P("mp", None),
            P(),
            P(),
            P(),
            P("mp", "dp", None),
        ),
        out_specs=(
            P("mp", "dp", None),
            P("mp", "dp", None),
            P(None, ("dp", "mp")),
            P(None, ("dp", "mp")),
            P(None, "dp", "mp"),
            P(None, ("dp", "mp")),
            P("mp", "dp"),
            P(("dp", "mp")),
            P(("dp", "mp")),
            P(("dp", "mp")),
            P("dp", "mp"),
            P(("dp", "mp")),
            P("mp", "dp"),
            P(("dp", "mp")),
            P(("dp", "mp")),
            P(("dp", "mp")),
        ),
        check_vma=False,
    )
```

time: 1200 us -> 532 us (0.44)
  Pallas kernels: 675 us -> 145 us
  matrix products: 94.7 us -> 2.92 us
  other arithmetic: 78.1 us -> 35.3 us
  waiting for transfers between devices: 148 us -> 181 us
  starting transfers between devices: 124 us -> 101 us
    pallas_call x27 -> x12, Pallas kernels: 675 us -> 145 us  [the longest x6 38.6 us: weight_grad(): pl.pallas_call(functools.partial(weight_grad_body, order, len(groups)), g...]
    dot_general x48 -> x0, matrix products: 90.9 us -> none  [dot(): return lax.dot_general(a, b, (dims, ((), ())), preferred_element_type=f32)]
    ppermute x76 -> x44, starting transfers between devices: 53.3 us -> 29.5 us  [flip(): return lax.ppermute(x, 'dp', [(i, i ^ step) for i in range(dpn)])]
    convert_element_type x32 -> x8, other arithmetic: 29.9 us -> 9.44 us  [the longest x6 6.69 us: reduced(): passed = (keep[:, 1].astype(f32) + came[:, 1].astype(f32)).astype(bf16)]
    all_to_all x2, waiting for transfers between devices: 2.03 us -> 20.6 us  [to_positions(): lax.all_to_all(x.reshape(mpn, positions, width), 'mp', 0, 0, tiled=False)]
    reduce_sum x14 -> x0, other arithmetic: 16.1 us -> none  [the longest x4 6.46 us: on_device(): grad_b_q.append(jnp.sum(dq.astype(f32), axis=0))]
    slice x10 -> x9, local copies, waits for them, and re-layouts: 15.4 us -> 2.24 us  [the longest x2 0.81 us: in_order(): turned = jnp.stack([parts[-i % mpn] for i in range(mpn)] * 2)]
    unnamed x350 -> x88, local copies, waits for them, and re-layouts: 27.1 us -> 16.8 us
  transfers between devices with their start and end apart: 106 -> 71, of which waited for: 26 -> 24; matrix products, arithmetic and copies ran while one was open for 19% -> 15% of each run, Pallas kernels for 57% -> 15%
where the time goes in v2:
time: 532 us; the launch traced here: 525 us
  waiting for transfers between devices  181 us (34%)
  Pallas kernels  145 us (27%)
  starting transfers between devices  101 us (19%)
  local copies, waits for them, and re-layouts  53.4 us (10%)
  other arithmetic  35.3 us (7%)
  between operations  6.6 us (1%)
    ppermute x21, waiting for transfers between devices, shift(): return lax.ppermute(x, 'mp', [(i, (i + s) % mpn) for i in range(mpn)])  79.3 us
    ppermute x44, waiting for transfers between devices, flip(): return lax.ppermute(x, 'dp', [(i, i ^ step) for i in range(dpn)])  69.3 us
    ppermute x21, starting transfers between devices, shift(): return lax.ppermute(x, 'mp', [(i, (i + s) % mpn) for i in range(mpn)])  48.1 us
    pallas_call x6, Pallas kernels, weight_grad(): pl.pallas_call(functools.partial(weight_grad_body, order, len(groups)), g...  38.6 us
    ppermute x44, starting transfers between devices, flip(): return lax.ppermute(x, 'dp', [(i, i ^ step) for i in range(dpn)])  29.5 us
    pallas_call x1, Pallas kernels, attend_back(): pl.pallas_call(functools.partial(attend_back_body, shards, g_out, g_qkv),...  29.3 us
    pallas_call x2, Pallas kernels, attend(): pl.pallas_call(functools.partial(attend_body, first, shards, gathered), g...  22.9 us
    pallas_call x1, Pallas kernels, up_back(): pl.pallas_call(functools.partial(up_back_body, shards, g_down, g_up), gri...  20.9 us
  transfers between devices with their start and end apart: 71, of which 24 were waited for; matrix products, arithmetic and copies ran while one was open for 15% of the time, Pallas kernels for 15%

profile of v2, /device:TPU:0, one launch (start us, length us, event | category | flops | bytes accessed | tf_op | source)
XLA Modules:
  0.0 525.1 jit_solution(11813430536054751170)
XLA Ops:
  1.8 5.1 collective-permute-start.5
  7.9 2.5 copy.183
  10.4 4.1 all-to-all-start
  14.5 3.9 collective-permute-start.2
  21.2 9.1 %collective-permute-done.4 = bf16[2,3,64,256]{3,2,1,0:T(8,128)(2,1)} collective-permute-done((bf16[2,3,64,256]{3,2,1,0:T(8,128)(2,1)S(1)}, bf16[2,3,64,256]{3,2,1,0:T(8,128)(2,1)}, u32[]{:S(2)}, u32[]{:S(2)}) %collective-permute-start.4) | collective-permute-done | bytes 196640 | tf_op jit(solution)/shard_map/ppermute | solution.py:668
  30.3 1.6 fusion.45
  31.9 1.6 fusion.44
  38.5 1.9 collective-permute-start.14
  45.0 7.6 %collective-permute-done.16 = bf16[2,80,1024]{2,1,0:T(8,128)(2,1)S(1)} collective-permute-done((bf16[2,80,1024]{2,1,0:T(8,128)(2,1)}, bf16[2,80,1024]{2,1,0:T(8,128)(2,1)S(1)}, u32[]{:S(2)}, u32[]{:S(2)}) %collective-permute-start.16) | collective-permute-done | bytes 327712 | tf_op jit(solution)/shard_map/ppermute | solution.py:668
  54.2 20.2 %collective-permute-done.15 = bf16[2,80,1024]{2,1,0:T(8,128)(2,1)S(1)} collective-permute-done((bf16[2,80,1024]{2,1,0:T(8,128)(2,1)}, bf16[2,80,1024]{2,1,0:T(8,128)(2,1)S(1)}, u32[]{:S(2)}, u32[]{:S(2)}) %collective-permute-start.15) | collective-permute-done | bytes 327712 | tf_op jit(solution)/shard_map/ppermute | solution.py:668
  74.4 3.0 collective-permute-start.26
  78.2 11.4 %collective-permute-done.27 = bf16[2,64,1024]{2,1,0:T(8,128)(2,1)S(1)} collective-permute-done((bf16[2,64,1024]{2,1,0:T(8,128)(2,1)S(1)}, bf16[2,64,1024]{2,1,0:T(8,128)(2,1)S(1)}, u32[]{:S(2)}, u32[]{:S(2)}) %collective-permute-start.27) | collective-permute-done | bytes 262176 | tf_op jit(solution)/shard_map/ppermute | solution.py:668
  89.6 10.8 %collective-permute-start.25 = (bf16[2,64,1024]{2,1,0:T(8,128)(2,1)S(1)}, bf16[2,64,1024]{2,1,0:T(8,128)(2,1)S(1)}, u32[]{:S(2)}, u32[]{:S(2)}) collective-permute-start(bf16[2,64,1024]{2,1,0:T(8,128)(2,1)S(1)} %dynamic-slice_bitcast_fusion), channel_id=1, source_target_pairs={{0,1},{1,2},{2,3},{3,0},{4,5},{5,6},{6,7},{7,4},{8,9},{9,10},{10,1... | collective-permute-start | bytes 786440 | tf_op jit(solution)/shard_map/ppermute | solution.py:668
  101.9 3.8 collective-permute-done.25
  107.3 2.3 collective-permute-start.1
  109.6 2.3 collective-permute-done.1
  111.9 2.5 collective-permute-start
  122.5 1.7 collective-permute-done.28
  129.1 7.9 %collective-permute-done.11.refs_6_.refs_15_ = bf16[2,3,3,64,256]{4,3,2,1,0:T(8,128)(2,1)} collective-permute-done((bf16[2,3,3,64,256]{4,3,2,1,0:T(8,128)(2,1)}, bf16[2,3,3,64,256]{4,3,2,1,0:T(8,128)(2,1)}, u32[]{:S(2)}, u32[]{:S(2)}) %collective-permute-start.11) | collective-permute-done | bytes 589856 | tf_op jit(solution)/shard_map/ppermute | solution.py:665
  150.3 2.5 copy.182
  154.2 1.9 pad_maximum_fusion.3.refs_5_
  156.2 4.0 all-to-all-start.1
  160.2 10.3 %collective-permute-done.29.refs_2_ = bf16[2,3,64,1024]{3,2,1,0:T(8,128)(2,1)} collective-permute-done((bf16[2,3,64,1024]{3,2,1,0:T(8,128)(2,1)}, bf16[2,3,64,1024]{3,2,1,0:T(8,128)(2,1)}, u32[]{:S(2)}, u32[]{:S(2)}) %collective-permute-start.29) | collective-permute-done | bytes 786464 | tf_op jit(solution)/shard_map/ppermute | solution.py:665
  174.3 7.2 %attend.2 = (bf16[1,512,768]{2,1,0:T(8,128)(2,1)}, bf16[1,4,512,512]{3,2,1,0:T(8,128)(2,1)}, bf16[1,512,256]{2,1,0:T(8,128)(2,1)}) custom-call(s32[1]{0:T(128)} %bitcast.place_ref, bf16[512,1024]{1,0:T(8,128)(2,1)} %add_convert_fusion.x_ref.refs_0_, f32[1,3,1,256]{3,2,1,0:T(1,128)} %slice.445.bias_ref, bf16[3,8,2,64,256]{4,3,2,1,0:T(8,128)(2,1)} %bitcast.194), custom_call_target="tpu_custom_call" | custom-call | flops 1073741824 | bytes 3670016 | tf_op jit(solution)/shard_map/attend/pallas_call | solution.py:143
  181.5 8.3 %collective-permute-done.33.refs_6_ = bf16[2,3,64,1024]{3,2,1,0:T(8,128)(2,1)} collective-permute-done((bf16[2,3,64,1024]{3,2,1,0:T(8,128)(2,1)}, bf16[2,3,64,1024]{3,2,1,0:T(8,128)(2,1)}, u32[]{:S(2)}, u32[]{:S(2)}) %collective-permute-start.33) | collective-permute-done | bytes 786464 | tf_op jit(solution)/shard_map/ppermute | solution.py:665
  190.9 15.6 %attend.3 = (bf16[3,512,768]{2,1,0:T(8,128)(2,1)}, bf16[3,4,512,512]{3,2,1,0:T(8,128)(2,1)}, bf16[3,512,256]{2,1,0:T(8,128)(2,1)}) custom-call(s32[1]{0:T(128)} %bitcast.place_ref, bf16[512,1024]{1,0:T(8,128)(2,1)} %add_convert_fusion.x_ref.refs_0_, f32[3,3,1,256]{3,2,1,0:T(1,128)} %slice.446.bias_ref, bf16[3,8,2,64,256]{4,3,2,1,0:T(8,128)(2,1)} %bitcast.195, ...), custom_call_target="tpu_custom_call" | custom-call | flops 3221225472 | bytes 11010048 | tf_op jit(solution)/shard_map/attend/pallas_call | solution.py:143
  207.5 18.3 %up_project.1 = (f32[512,1024]{1,0:T(8,128)}, f32[512,128]{1,0:T(8,128)}, bf16[512,1024]{1,0:T(8,128)(2,1)}, bf16[4,512,1024]{2,1,0:T(8,128)(2,1)}, bf16[4,512,1024]{2,1,0:T(8,128)(2,1)}) custom-call(s32[1]{0:T(128)} %bitcast.place_ref, bf16[1,512,256]{2,1,0:T(8,128)(2,1)} %get-tuple-element.55.near_ref, bf16[3,512,256]{2,1,0:T(8,128)(2,1)} %get-tuple-element.56.far_ref, ...), custom_call_target="tpu_custom_call" | custom-call | flops 5368709120 | bytes 18874368 | tf_op jit(solution)/shard_map/up_project/pallas_call | solution.py:229
  227.1 15.4 %down_project.1 = (bf16[512,1024]{1,0:T(8,128)(2,1)}, f32[512,1024]{1,0:T(8,128)}, bf16[512,1024]{1,0:T(8,128)(2,1)}, f32[3,1024]{1,0:T(4,128)}) custom-call(s32[1]{0:T(128)} %bitcast.place_ref, f32[1]{0:T(128)S(6)} %convert_element_type.246.live_ref, bf16[4,512,1024]{2,1,0:T(8,128)(2,1)} %get-tuple-element.58.act_ref.refs_2_, ...), custom_call_target="tpu_custom_call" | custom-call | flops 4294967296 | bytes 18874368 | tf_op jit(solution)/shard_map/down_project/pallas_call | solution.py:315
  242.5 20.9 %up_back.1 = (bf16[4,512,1024]{2,1,0:T(8,128)(2,1)}, f32[4,1,1024]{2,1,0:T(1,128)}, f32[512,1024]{1,0:T(8,128)}, bf16[512,1024]{1,0:T(8,128)(2,1)}, f32[3,1024]{1,0:T(4,128)}) custom-call(s32[1]{0:T(128)} %bitcast.place_ref, bf16[512,1024]{1,0:T(8,128)(2,1)} %get-tuple-element.63.bg_ref.refs_0_, bf16[4,512,1024]{2,1,0:T(8,128)(2,1)} %get-tuple-element.64.slope_ref, ...), custom_call_target="tpu_custom_call" | custom-call | flops 8589934592 | bytes 33554432 | tf_op jit(solution)/shard_map/up_back/pallas_call | solution.py:393
  263.4 29.3 %attend_back.1 = (bf16[4,512,768]{2,1,0:T(8,128)(2,1)}, bf16[512,1024]{1,0:T(8,128)(2,1)}, f32[4,1,768]{2,1,0:T(1,128)}, f32[1,1024]{1,0:T(1,128)}) custom-call(s32[1]{0:T(128)} %bitcast.place_ref, bf16[512,1024]{1,0:T(8,128)(2,1)} %get-tuple-element.67.mg_ref.refs_4_, bf16[1,512,768]{2,1,0:T(8,128)(2,1)} %get-tuple-element.68.near_ref, ...), custom_call_target="tpu_custom_call" | custom-call | flops 6979321856 | bytes 20971520 | tf_op jit(solution)/shard_map/attend_back/pallas_call | solution.py:528
  295.4 3.5 all-to-all-start.5
  301.7 4.3 all-to-all-done.5
  306.0 2.6 all-to-all-start.4
  308.7 7.3 %all-to-all-done.4 = f32[32,1,386]{2,1,0:T(1,128)S(1)} async-done(((f32[32,1,386]{2,1,0:T(1,128)}), f32[32,1,386]{2,1,0:T(1,128)S(1)}, u32[]{:S(2)}, u32[]{:S(2)}) %all-to-all-start.4) | async-done | bytes 49440 | tf_op jit(solution)/shard_map/all_to_all | solution.py:816
  316.0 4.4 all-to-all-start.2
  325.6 20.6 %all-to-all-done.2 = bf16[4,128,1024]{2,1,0:T(8,128)(2,1)} async-done(((bf16[4,128,1024]{2,1,0:T(8,128)(2,1)}), bf16[4,128,1024]{2,1,0:T(8,128)(2,1)}, u32[]{:S(2)}, u32[]{:S(2)}) %all-to-all-start.2) | async-done | bytes 1048608 | tf_op jit(solution)/shard_map/all_to_all | solution.py:675
  346.3 4.5 all-to-all-start.3
  352.0 7.2 %weight_grad.7 = (bf16[2,2,128,1024]{3,2,1,0:T(8,128)(2,1)}, bf16[2,2,128,1024]{3,2,1,0:T(8,128)(2,1)}) custom-call(s32[1]{0:T(128)} %bitcast.place_ref, bf16[512,1024]{1,0:T(8,128)(2,1)} %add_convert_fusion.x_ref.refs_0_, bf16[512,1024]{1,0:T(8,128)(2,1)} %copy-done.5, bf16[4,512,768]{2,1,0:T(8,128)(2,1)} %get-tuple-element.79.refs_2_, ...), custom_call_target="tpu_custom_call" | custom-call | flops 2147483648 | bytes 8388608 | tf_op jit(solution)/shard_map/weight_grad/pallas_call | solution.py:613
  361.4 7.2 %weight_grad.6 = (bf16[2,2,128,1024]{3,2,1,0:T(8,128)(2,1)}, bf16[2,2,128,1024]{3,2,1,0:T(8,128)(2,1)}) custom-call(s32[1]{0:T(128)} %bitcast.place_ref, bf16[512,1024]{1,0:T(8,128)(2,1)} %add_convert_fusion.x_ref.refs_0_, bf16[512,1024]{1,0:T(8,128)(2,1)} %copy-done.5, bf16[4,512,768]{2,1,0:T(8,128)(2,1)} %get-tuple-element.79.refs_2_, ...), custom_call_target="tpu_custom_call" | custom-call | flops 2147483648 | bytes 8388608 | tf_op jit(solution)/shard_map/weight_grad/pallas_call | solution.py:613
  368.6 2.3 copy.132
  374.2 3.0 copy.149
  378.8 2.7 copy.150
  381.4 4.7 collective-permute-done.43
  387.4 9.0 %collective-permute-done.40 = bf16[2,2,128,1024]{3,2,0,1:T(8,128)(2,1)S(1)} collective-permute-done((bf16[2,2,128,1024]{3,2,0,1:T(8,128)(2,1)}, bf16[2,2,128,1024]{3,2,0,1:T(8,128)(2,1)S(1)}, u32[]{:S(2)}, u32[]{:S(2)}) %collective-permute-start.40) | collective-permute-done | bytes 1048608 | tf_op jit(solution)/shard_map/ppermute | solution.py:665
  398.6 6.0 %weight_grad.8 = (bf16[2,2,128,1024]{3,2,1,0:T(8,128)(2,1)}, bf16[2,2,128,1024]{3,2,1,0:T(8,128)(2,1)}) custom-call(s32[1]{0:T(128)} %bitcast.place_ref, bf16[512,1024]{1,0:T(8,128)(2,1)} %get-tuple-element.84.refs_0_, bf16[512,1024]{1,0:T(8,128)(2,1)} %collective-permute-done.47.refs_1_, bf16[4,512,1024]{2,1,0:T(8,128)(2,1)} %get-tuple-element.85.refs_2_, ...), custom_call_target="tpu_custom_call" | custom-call | flops 2147483648 | bytes 8388608 | tf_op jit(solution)/shard_map/weight_grad/pallas_call | solution.py:613
  404.6 2.3 copy.139
  408.0 6.0 %weight_grad.9 = (bf16[2,2,128,1024]{3,2,1,0:T(8,128)(2,1)}, bf16[2,2,128,1024]{3,2,1,0:T(8,128)(2,1)}) custom-call(s32[1]{0:T(128)} %bitcast.place_ref, bf16[512,1024]{1,0:T(8,128)(2,1)} %get-tuple-element.84.refs_0_, bf16[512,1024]{1,0:T(8,128)(2,1)} %collective-permute-done.47.refs_1_, bf16[4,512,1024]{2,1,0:T(8,128)(2,1)} %get-tuple-element.85.refs_2_, ...), custom_call_target="tpu_custom_call" | custom-call | flops 2147483648 | bytes 8388608 | tf_op jit(solution)/shard_map/weight_grad/pallas_call | solution.py:613
  414.0 2.3 copy.142
  418.6 2.0 collective-permute-start.46
  420.9 2.4 collective-permute-start.45
  424.8 6.3 %weight_grad.11 = (bf16[2,2,128,1024]{3,2,1,0:T(8,128)(2,1)}, bf16[2,2,128,1024]{3,2,1,0:T(8,128)(2,1)}) custom-call(s32[1]{0:T(128)} %bitcast.place_ref, bf16[512,1024]{1,0:T(8,128)(2,1)} %get-tuple-element.63.bg_ref.refs_0_, bf16[512,1024]{1,0:T(8,128)(2,1)} %copy-done.8, bf16[4,512,1024]{2,1,0:T(8,128)(2,1)} %get-tuple-element.58.act_ref.refs_2_, ...), custom_call_target="tpu_custom_call" | custom-call | flops 2147483648 | bytes 8388608 | tf_op jit(solution)/shard_map/weight_grad/pallas_call | solution.py:613
  432.2 6.0 %weight_grad.10 = (bf16[2,2,128,1024]{3,2,1,0:T(8,128)(2,1)}, bf16[2,2,128,1024]{3,2,1,0:T(8,128)(2,1)}) custom-call(s32[1]{0:T(128)} %bitcast.place_ref, bf16[512,1024]{1,0:T(8,128)(2,1)} %get-tuple-element.63.bg_ref.refs_0_, bf16[512,1024]{1,0:T(8,128)(2,1)} %copy-done.8, bf16[4,512,1024]{2,1,0:T(8,128)(2,1)} %get-tuple-element.58.act_ref.refs_2_, ...), custom_call_target="tpu_custom_call" | custom-call | flops 2147483648 | bytes 8388608 | tf_op jit(solution)/shard_map/weight_grad/pallas_call | solution.py:613
  438.3 2.3 copy.145
  446.9 1.6 collective-permute-start.53
  448.5 16.6 %collective-permute-done.61 = bf16[2,2,128,1024]{3,2,1,0:T(8,128)(2,1)} collective-permute-done((bf16[2,2,128,1024]{3,2,1,0:T(8,128)(2,1)}, bf16[2,2,128,1024]{3,2,1,0:T(8,128)(2,1)}, u32[]{:S(2)}, u32[]{:S(2)}) %collective-permute-start.61) | collective-permute-done | bytes 1048608 | tf_op jit(solution)/shard_map/ppermute | solution.py:665
  469.2 8.9 %collective-permute-done.53 = bf16[2,128,1024]{2,1,0:T(8,128)(2,1)S(1)} collective-permute-done((bf16[2,128,1024]{2,1,0:T(8,128)(2,1)S(1)}, bf16[2,128,1024]{2,1,0:T(8,128)(2,1)S(1)}, u32[]{:S(2)}, u32[]{:S(2)}) %collective-permute-start.53) | collective-permute-done | bytes 524320 | tf_op jit(solution)/shard_map/ppermute | solution.py:665
  480.2 4.3 collective-permute-start.55
  487.5 1.9 collective-permute-start.64
  489.4 3.4 collective-permute-start.63
  495.6 7.1 %collective-permute-done.64 = bf16[128,1024]{1,0:T(8,128)(2,1)S(1)} collective-permute-done((bf16[128,1024]{1,0:T(8,128)(2,1)S(1)}, bf16[128,1024]{1,0:T(8,128)(2,1)S(1)}, u32[]{:S(2)}, u32[]{:S(2)}) %collective-permute-start.64) | collective-permute-done | bytes 262176 | tf_op jit(solution)/shard_map/ppermute | solution.py:668
  502.7 12.7 %collective-permute-done.63 = bf16[128,1024]{1,0:T(8,128)(2,1)S(1)} collective-permute-done((bf16[128,1024]{1,0:T(8,128)(2,1)S(1)}, bf16[128,1024]{1,0:T(8,128)(2,1)S(1)}, u32[]{:S(2)}, u32[]{:S(2)}) %collective-permute-start.63) | collective-permute-done | bytes 262176 | tf_op jit(solution)/shard_map/ppermute | solution.py:668
  516.3 2.0 copy.153
  518.4 4.4 collective-permute-done.51
  522.8 2.0 fusion.17
  (298 shorter events, 97.7 us)
Async XLA Ops:
  1.8 18.4 %collective-permute-start.5 = (bf16[2,3,64,256]{3,2,1,0:T(8,128)(2,1)S(1)}, bf16[2,3,64,256]{3,2,1,0:T(8,128)(2,1)}, u32[]{:S(2)}, u32[]{:S(2)}) collective-permute-start(bf16[2,3,64,256]{3,2,1,0:T(8,128)(2,1)S(1)} %copy_bitcast_fusion.2), channel_id=1, source_target_pairs={{0,3},{1,0},{2,1},{3,2},{4,7},{5,4},{6,5},{7,6},{8,11},{9,8},{10,9... | collective-permute-start | bytes 589832 | tf_op jit(solution)/shard_map/ppermute | solution.py:668
  6.9 23.4 %collective-permute-start.4 = (bf16[2,3,64,256]{3,2,1,0:T(8,128)(2,1)S(1)}, bf16[2,3,64,256]{3,2,1,0:T(8,128)(2,1)}, u32[]{:S(2)}, u32[]{:S(2)}) collective-permute-start(bf16[2,3,64,256]{3,2,1,0:T(8,128)(2,1)S(1)} %copy_bitcast_fusion.2), channel_id=1, source_target_pairs={{0,2},{1,3},{2,0},{3,1},{4,6},{5,7},{6,4},{7,5},{8,10},{9,11},{10,... | collective-permute-start | bytes 589832 | tf_op jit(solution)/shard_map/ppermute | solution.py:668
  6.9 25.0 %collective-permute-start.3 = (bf16[2,3,64,256]{3,2,1,0:T(8,128)(2,1)S(1)}, bf16[2,3,64,256]{3,2,1,0:T(8,128)(2,1)}, u32[]{:S(2)}, u32[]{:S(2)}) collective-permute-start(bf16[2,3,64,256]{3,2,1,0:T(8,128)(2,1)S(1)} %copy_bitcast_fusion.2), channel_id=1, source_target_pairs={{0,1},{1,2},{2,3},{3,0},{4,5},{5,6},{6,7},{7,4},{8,9},{9,10},{10,1... | collective-permute-start | bytes 589832 | tf_op jit(solution)/shard_map/ppermute | solution.py:668
  10.4 145.7 %all-to-all-start = ((bf16[4,128,1024]{2,1,0:T(8,128)(2,1)}), bf16[4,128,1024]{2,1,0:T(8,128)(2,1)S(1)}, u32[]{:S(2)}, u32[]{:S(2)}) async-start(bf16[4,128,1024]{2,1,0:T(8,128)(2,1)} %bitcast.192), calls=%async_computation | async-start | bytes 2097152 | tf_op jit(solution)/shard_map/all_to_all | solution.py:671
  14.5 92.8 %collective-permute-start.2 = (f32[1536]{0:T(1024)S(1)}, f32[1536]{0:T(1024)S(1)}, u32[]{:S(2)}, u32[]{:S(2)}) collective-permute-start(f32[1536]{0:T(1024)S(1)} %pad_maximum_fusion.19), channel_id=1, source_target_pairs={{0,3},{1,0},{2,1},{3,2},{4,7},{5,4},{6,5},{7,6},{8,11},{9,8},{10,9... | collective-permute-start | bytes 18440 | tf_op jit(solution)/shard_map/ppermute | solution.py:668
  38.4 14.3 %collective-permute-start.16 = (bf16[2,80,1024]{2,1,0:T(8,128)(2,1)}, bf16[2,80,1024]{2,1,0:T(8,128)(2,1)S(1)}, u32[]{:S(2)}, u32[]{:S(2)}) collective-permute-start(bf16[2,80,1024]{2,1,0:T(8,128)(2,1)} %pad_maximum_fusion.10), channel_id=1, source_target_pairs={{0,3},{1,0},{2,1},{3,2},{4,7},{5,4},{6,5},{7,6},{8,11},{9,8},{10,9... | collective-permute-start | bytes 983048 | tf_op jit(solution)/shard_map/ppermute | solution.py:668
  38.4 35.9 %collective-permute-start.15 = (bf16[2,80,1024]{2,1,0:T(8,128)(2,1)}, bf16[2,80,1024]{2,1,0:T(8,128)(2,1)S(1)}, u32[]{:S(2)}, u32[]{:S(2)}) collective-permute-start(bf16[2,80,1024]{2,1,0:T(8,128)(2,1)} %pad_maximum_fusion.10), channel_id=1, source_target_pairs={{0,2},{1,3},{2,0},{3,1},{4,6},{5,7},{6,4},{7,5},{8,10},{9,11},{10,... | collective-permute-start | bytes 983048 | tf_op jit(solution)/shard_map/ppermute | solution.py:668
  38.5 35.9 %collective-permute-start.14 = (bf16[2,80,1024]{2,1,0:T(8,128)(2,1)}, bf16[2,80,1024]{2,1,0:T(8,128)(2,1)S(1)}, u32[]{:S(2)}, u32[]{:S(2)}) collective-permute-start(bf16[2,80,1024]{2,1,0:T(8,128)(2,1)} %pad_maximum_fusion.10), channel_id=1, source_target_pairs={{0,1},{1,2},{2,3},{3,0},{4,5},{5,6},{6,7},{7,4},{8,9},{9,10},{10,1... | collective-permute-start | bytes 983048 | tf_op jit(solution)/shard_map/ppermute | solution.py:668
  42.4 72.0 %collective-permute-start.10 = (bf16[3,3,64,256]{3,2,1,0:T(8,128)(2,1)S(1)}, bf16[3,3,64,256]{3,2,1,0:T(8,128)(2,1)S(1)}, u32[]{:S(2)}, u32[]{:S(2)}) collective-permute-start(bf16[3,3,64,256]{3,2,1,0:T(8,128)(2,1)S(1)} %get-tuple-element.187), channel_id=1, source_target_pairs={{0,16},{4,20},{8,24},{12,28},{16,0},{20,4},{24,8},{28,12},{1,17},{... | collective-permute-start | bytes 884744 | tf_op jit(solution)/shard_map/ppermute | solution.py:665
  52.6 67.4 %collective-permute-start.7 = (bf16[2,3,3,64,256]{4,3,2,1,0:T(8,128)(2,1)S(1)}, bf16[2,3,3,64,256]{4,3,2,1,0:T(8,128)(2,1)S(1)}, u32[]{:S(2)}, u32[]{:S(2)}) collective-permute-start(bf16[2,3,3,64,256]{4,3,2,1,0:T(8,128)(2,1)S(1)} %pad_maximum_fusion.4.refs_1_.refs_10_), channel_id=1, source_target_pairs={{0,16},{4,20},{8,24},{12,28},{16,0},{20,4},{24,8},{28,12},{1,17},{... | collective-permute-start | bytes 1769480 | tf_op jit(solution)/shard_map/ppermute | solution.py:665
  74.4 26.0 %collective-permute-start.26 = (bf16[2,64,1024]{2,1,0:T(8,128)(2,1)S(1)}, bf16[2,64,1024]{2,1,0:T(8,128)(2,1)S(1)}, u32[]{:S(2)}, u32[]{:S(2)}) collective-permute-start(bf16[2,64,1024]{2,1,0:T(8,128)(2,1)S(1)} %dynamic-slice_bitcast_fusion), channel_id=1, source_target_pairs={{0,2},{1,3},{2,0},{3,1},{4,6},{5,7},{6,4},{7,5},{8,10},{9,11},{10,... | collective-permute-start | bytes 786440 | tf_op jit(solution)/shard_map/ppermute | solution.py:668
  77.4 12.2 %collective-permute-start.27 = (bf16[2,64,1024]{2,1,0:T(8,128)(2,1)S(1)}, bf16[2,64,1024]{2,1,0:T(8,128)(2,1)S(1)}, u32[]{:S(2)}, u32[]{:S(2)}) collective-permute-start(bf16[2,64,1024]{2,1,0:T(8,128)(2,1)S(1)} %dynamic-slice_bitcast_fusion), channel_id=1, source_target_pairs={{0,3},{1,0},{2,1},{3,2},{4,7},{5,4},{6,5},{7,6},{8,11},{9,8},{10,9... | collective-permute-start | bytes 786440 | tf_op jit(solution)/shard_map/ppermute | solution.py:668
  89.6 16.2 %collective-permute-start.25 = (bf16[2,64,1024]{2,1,0:T(8,128)(2,1)S(1)}, bf16[2,64,1024]{2,1,0:T(8,128)(2,1)S(1)}, u32[]{:S(2)}, u32[]{:S(2)}) collective-permute-start(bf16[2,64,1024]{2,1,0:T(8,128)(2,1)S(1)} %dynamic-slice_bitcast_fusion), channel_id=1, source_target_pairs={{0,1},{1,2},{2,3},{3,0},{4,5},{5,6},{6,7},{7,4},{8,9},{9,10},{10,1... | collective-permute-start | bytes 786440 | tf_op jit(solution)/shard_map/ppermute | solution.py:668
  100.4 17.0 %collective-permute-start.17 = (bf16[3,80,1024]{2,1,0:T(8,128)(2,1)S(1)}, bf16[3,80,1024]{2,1,0:T(8,128)(2,1)S(1)}, u32[]{:S(2)}, u32[]{:S(2)}) collective-permute-start(bf16[3,80,1024]{2,1,0:T(8,128)(2,1)S(1)} %get-tuple-element.175), channel_id=1, source_target_pairs={{0,8},{4,12},{8,0},{12,4},{16,24},{20,28},{24,16},{28,20},{1,9},{5... | collective-permute-start | bytes 1474568 | tf_op jit(solution)/shard_map/ppermute | solution.py:665
  105.7 13.3 %collective-permute-start.21 = (bf16[3,80,1024]{2,1,0:T(8,128)(2,1)S(1)}, bf16[3,80,1024]{2,1,0:T(8,128)(2,1)S(1)}, u32[]{:S(2)}, u32[]{:S(2)}) collective-permute-start(bf16[3,80,1024]{2,1,0:T(8,128)(2,1)S(1)} %get-tuple-element.173), channel_id=1, source_target_pairs={{0,16},{4,20},{8,24},{12,28},{16,0},{20,4},{24,8},{28,12},{1,17},{... | collective-permute-start | bytes 1474568 | tf_op jit(solution)/shard_map/ppermute | solution.py:665
  114.4 9.8 %collective-permute-start.28 = (bf16[3,64,1024]{2,1,0:T(8,128)(2,1)S(1)}, bf16[3,64,1024]{2,1,0:T(8,128)(2,1)S(1)}, u32[]{:S(2)}, u32[]{:S(2)}) collective-permute-start(bf16[3,64,1024]{2,1,0:T(8,128)(2,1)S(1)} %get-tuple-element.179), channel_id=1, source_target_pairs={{0,8},{4,12},{8,0},{12,4},{16,24},{20,28},{24,16},{28,20},{1,9},{5... | collective-permute-start | bytes 1179656 | tf_op jit(solution)/shard_map/ppermute | solution.py:665
  117.4 19.6 %collective-permute-start.11 = (bf16[2,3,3,64,256]{4,3,2,1,0:T(8,128)(2,1)}, bf16[2,3,3,64,256]{4,3,2,1,0:T(8,128)(2,1)}, u32[]{:S(2)}, u32[]{:S(2)}) collective-permute-start(bf16[2,3,3,64,256]{4,3,2,1,0:T(8,128)(2,1)} %pad_maximum_fusion.5.refs_5_.refs_14_), channel_id=1, source_target_pairs={{0,8},{4,12},{8,0},{12,4},{16,24},{20,28},{24,16},{28,20},{1,9},{5... | collective-permute-start | bytes 1769480 | tf_op jit(solution)/shard_map/ppermute | solution.py:665
  119.0 27.5 %collective-permute-start.12 = (bf16[2,3,3,64,256]{4,3,2,1,0:T(8,128)(2,1)}, bf16[2,3,3,64,256]{4,3,2,1,0:T(8,128)(2,1)}, u32[]{:S(2)}, u32[]{:S(2)}) collective-permute-start(bf16[2,3,3,64,256]{4,3,2,1,0:T(8,128)(2,1)} %pad_maximum_fusion.5.refs_5_.refs_14_), channel_id=1, source_target_pairs={{0,4},{4,0},{8,12},{12,8},{16,20},{20,16},{24,28},{28,24},{1,5},{5... | collective-permute-start | bytes 1769480 | tf_op jit(solution)/shard_map/ppermute | solution.py:665
  120.9 25.7 %collective-permute-start.32 = (bf16[3,64,1024]{2,1,0:T(8,128)(2,1)}, bf16[3,64,1024]{2,1,0:T(8,128)(2,1)}, u32[]{:S(2)}, u32[]{:S(2)}) collective-permute-start(bf16[3,64,1024]{2,1,0:T(8,128)(2,1)} %get-tuple-element.177), channel_id=1, source_target_pairs={{0,16},{4,20},{8,24},{12,28},{16,0},{20,4},{24,8},{28,12},{1,17},{... | collective-permute-start | bytes 1179656 | tf_op jit(solution)/shard_map/ppermute | solution.py:665
  124.2 30.0 %collective-permute-start.18 = (bf16[2,3,80,1024]{3,2,1,0:T(8,128)(2,1)}, bf16[2,3,80,1024]{3,2,1,0:T(8,128)(2,1)}, u32[]{:S(2)}, u32[]{:S(2)}) collective-permute-start(bf16[2,3,80,1024]{3,2,1,0:T(8,128)(2,1)} %pad_maximum_fusion.refs_1_.refs_10_), channel_id=1, source_target_pairs={{0,16},{4,20},{8,24},{12,28},{16,0},{20,4},{24,8},{28,12},{1,17},{... | collective-permute-start | bytes 2949128 | tf_op jit(solution)/shard_map/ppermute | solution.py:665
  127.6 43.5 %collective-permute-start.22 = (bf16[2,3,80,1024]{3,2,1,0:T(8,128)(2,1)}, bf16[2,3,80,1024]{3,2,1,0:T(8,128)(2,1)}, u32[]{:S(2)}, u32[]{:S(2)}) collective-permute-start(bf16[2,3,80,1024]{3,2,1,0:T(8,128)(2,1)} %pad_maximum_fusion.1.refs_5_.refs_14_), channel_id=1, source_target_pairs={{0,8},{4,12},{8,0},{12,4},{16,24},{20,28},{24,16},{28,20},{1,9},{5... | collective-permute-start | bytes 2949128 | tf_op jit(solution)/shard_map/ppermute | solution.py:665
  137.0 33.5 %collective-permute-start.29 = (bf16[2,3,64,1024]{3,2,1,0:T(8,128)(2,1)}, bf16[2,3,64,1024]{3,2,1,0:T(8,128)(2,1)}, u32[]{:S(2)}, u32[]{:S(2)}) collective-permute-start(bf16[2,3,64,1024]{3,2,1,0:T(8,128)(2,1)} %pad_maximum_fusion.2.refs_1_), channel_id=1, source_target_pairs={{0,16},{4,20},{8,24},{12,28},{16,0},{20,4},{24,8},{28,12},{1,17},{... | collective-permute-start | bytes 2359304 | tf_op jit(solution)/shard_map/ppermute | solution.py:665
  152.8 37.0 %collective-permute-start.19 = (bf16[2,3,80,1024]{3,2,1,0:T(8,128)(2,1)}, bf16[2,3,80,1024]{3,2,1,0:T(8,128)(2,1)S(1)}, u32[]{:S(2)}, u32[]{:S(2)}) collective-permute-start(bf16[2,3,80,1024]{3,2,1,0:T(8,128)(2,1)} %pad_maximum_fusion.refs_1_.refs_10_), channel_id=1, source_target_pairs={{0,4},{4,0},{8,12},{12,8},{16,20},{20,16},{24,28},{28,24},{1,5},{5... | collective-permute-start | bytes 2949128 | tf_op jit(solution)/shard_map/ppermute | solution.py:665
  152.9 37.5 %collective-permute-start.23 = (bf16[2,3,80,1024]{3,2,1,0:T(8,128)(2,1)}, bf16[2,3,80,1024]{3,2,1,0:T(8,128)(2,1)}, u32[]{:S(2)}, u32[]{:S(2)}) collective-permute-start(bf16[2,3,80,1024]{3,2,1,0:T(8,128)(2,1)} %pad_maximum_fusion.1.refs_5_.refs_14_), channel_id=1, source_target_pairs={{0,4},{4,0},{8,12},{12,8},{16,20},{20,16},{24,28},{28,24},{1,5},{5... | collective-permute-start | bytes 2949128 | tf_op jit(solution)/shard_map/ppermute | solution.py:665
  154.2 36.3 %collective-permute-start.20 = (bf16[2,3,80,1024]{3,2,1,0:T(8,128)(2,1)}, bf16[2,3,80,1024]{3,2,1,0:T(8,128)(2,1)}, u32[]{:S(2)}, u32[]{:S(2)}) collective-permute-start(bf16[2,3,80,1024]{3,2,1,0:T(8,128)(2,1)} %collective-permute-done.18.refs_2_.refs_11_), channel_id=1, source_target_pairs={{0,4},{4,0},{8,12},{12,8},{16,20},{20,16},{24,28},{28,24},{1,5},{5... | collective-permute-start | bytes 2949128 | tf_op jit(solution)/shard_map/ppermute | solution.py:665
  156.2 69.7 %all-to-all-start.1 = ((bf16[4,128,1024]{2,1,0:T(8,128)(2,1)}), bf16[4,128,1024]{2,1,0:T(8,128)(2,1)S(1)}, u32[]{:S(2)}, u32[]{:S(2)}) async-start(bf16[4,128,1024]{2,1,0:T(8,128)(2,1)} %bitcast.188), calls=%async_computation.1 | async-start | bytes 2097152 | tf_op jit(solution)/shard_map/all_to_all | solution.py:671
  170.5 19.3 %collective-permute-start.33 = (bf16[2,3,64,1024]{3,2,1,0:T(8,128)(2,1)}, bf16[2,3,64,1024]{3,2,1,0:T(8,128)(2,1)}, u32[]{:S(2)}, u32[]{:S(2)}) collective-permute-start(bf16[2,3,64,1024]{3,2,1,0:T(8,128)(2,1)} %pad_maximum_fusion.3.refs_5_), channel_id=1, source_target_pairs={{0,8},{4,12},{8,0},{12,4},{16,24},{20,28},{24,16},{28,20},{1,9},{5... | collective-permute-start | bytes 2359304 | tf_op jit(solution)/shard_map/ppermute | solution.py:665
  171.0 35.5 %collective-permute-start.24 = (bf16[2,3,80,1024]{3,2,1,0:T(8,128)(2,1)}, bf16[2,3,80,1024]{3,2,1,0:T(8,128)(2,1)S(1)}, u32[]{:S(2)}, u32[]{:S(2)}) collective-permute-start(bf16[2,3,80,1024]{3,2,1,0:T(8,128)(2,1)} %collective-permute-done.22.refs_6_.refs_15_), channel_id=1, source_target_pairs={{0,4},{4,0},{8,12},{12,8},{16,20},{20,16},{24,28},{28,24},{1,5},{5... | collective-permute-start | bytes 2949128 | tf_op jit(solution)/shard_map/ppermute | solution.py:665
  189.8 36.1 %collective-permute-start.30 = (bf16[2,3,64,1024]{3,2,1,0:T(8,128)(2,1)}, bf16[2,3,64,1024]{3,2,1,0:T(8,128)(2,1)S(1)}, u32[]{:S(2)}, u32[]{:S(2)}) collective-permute-start(bf16[2,3,64,1024]{3,2,1,0:T(8,128)(2,1)} %pad_maximum_fusion.2.refs_1_), channel_id=1, source_target_pairs={{0,4},{4,0},{8,12},{12,8},{16,20},{20,16},{24,28},{28,24},{1,5},{5... | collective-permute-start | bytes 2359304 | tf_op jit(solution)/shard_map/ppermute | solution.py:665
  189.8 36.1 %collective-permute-start.34 = (bf16[2,3,64,1024]{3,2,1,0:T(8,128)(2,1)S(1)}, bf16[2,3,64,1024]{3,2,1,0:T(8,128)(2,1)}, u32[]{:S(2)}, u32[]{:S(2)}) collective-permute-start(bf16[2,3,64,1024]{3,2,1,0:T(8,128)(2,1)S(1)} %copy-done.20), channel_id=1, source_target_pairs={{0,4},{4,0},{8,12},{12,8},{16,20},{20,16},{24,28},{28,24},{1,5},{5... | collective-permute-start | bytes 2359304 | tf_op jit(solution)/shard_map/ppermute | solution.py:665
  190.4 35.5 %collective-permute-start.31 = (bf16[2,3,64,1024]{3,2,1,0:T(8,128)(2,1)}, bf16[2,3,64,1024]{3,2,1,0:T(8,128)(2,1)}, u32[]{:S(2)}, u32[]{:S(2)}) collective-permute-start(bf16[2,3,64,1024]{3,2,1,0:T(8,128)(2,1)} %collective-permute-done.29.refs_2_), channel_id=1, source_target_pairs={{0,4},{4,0},{8,12},{12,8},{16,20},{20,16},{24,28},{28,24},{1,5},{5... | collective-permute-start | bytes 2359304 | tf_op jit(solution)/shard_map/ppermute | solution.py:665
  190.5 35.5 %collective-permute-start.35 = (bf16[2,3,64,1024]{3,2,1,0:T(8,128)(2,1)}, bf16[2,3,64,1024]{3,2,1,0:T(8,128)(2,1)}, u32[]{:S(2)}, u32[]{:S(2)}) collective-permute-start(bf16[2,3,64,1024]{3,2,1,0:T(8,128)(2,1)} %collective-permute-done.33.refs_6_), channel_id=1, source_target_pairs={{0,4},{4,0},{8,12},{12,8},{16,20},{20,16},{24,28},{28,24},{1,5},{5... | collective-permute-start | bytes 2359304 | tf_op jit(solution)/shard_map/ppermute | solution.py:665
  295.4 10.6 %all-to-all-start.5 = ((f32[32,1,32]{2,1,0:T(1,128)}), f32[32,1,32]{2,1,0:T(1,128)S(1)}, u32[]{:S(2)}, u32[]{:S(2)}) async-start(f32[32,1,32]{2,1,0:T(1,128)} %bitcast.58), calls=%async_computation.5 | async-start | bytes 32768 | tf_op jit(solution)/shard_map/all_to_all | solution.py:822
  299.7 52.3 %collective-permute-start.37 = (bf16[4,512,768]{2,1,0:T(8,128)(2,1)}, bf16[4,512,768]{2,1,0:T(8,128)(2,1)}, u32[]{:S(2)}, u32[]{:S(2)}) collective-permute-start(bf16[4,512,768]{2,1,0:T(8,128)(2,1)} %get-tuple-element.79.refs_2_), channel_id=1, source_target_pairs={{0,4},{4,0},{8,12},{12,8},{16,20},{20,16},{24,28},{28,24},{1,5},{5... | collective-permute-start | bytes 9437192 | tf_op jit(solution)/shard_map/ppermute | solution.py:665
  306.0 10.1 %all-to-all-start.4 = ((f32[32,1,386]{2,1,0:T(1,128)}), f32[32,1,386]{2,1,0:T(1,128)S(1)}, u32[]{:S(2)}, u32[]{:S(2)}) async-start(f32[32,1,386]{2,1,0:T(1,128)} %copy.129), calls=%async_computation.4 | async-start | bytes 131072 | tf_op jit(solution)/shard_map/all_to_all | solution.py:816
  308.5 90.1 %collective-permute-start.48 = (bf16[4,512,1024]{2,1,0:T(8,128)(2,1)}, bf16[4,512,1024]{2,1,0:T(8,128)(2,1)}, u32[]{:S(2)}, u32[]{:S(2)}) collective-permute-start(bf16[4,512,1024]{2,1,0:T(8,128)(2,1)} %get-tuple-element.85.refs_2_), channel_id=1, source_target_pairs={{0,4},{4,0},{8,12},{12,8},{16,20},{20,16},{24,28},{28,24},{1,5},{5... | collective-permute-start | bytes 12582920 | tf_op jit(solution)/shard_map/ppermute | solution.py:665
  316.0 30.2 %all-to-all-start.2 = ((bf16[4,128,1024]{2,1,0:T(8,128)(2,1)}), bf16[4,128,1024]{2,1,0:T(8,128)(2,1)}, u32[]{:S(2)}, u32[]{:S(2)}) async-start(bf16[4,128,1024]{2,1,0:T(8,128)(2,1)} %bitcast.40), calls=%async_computation.2 | async-start | bytes 2097152 | tf_op jit(solution)/shard_map/all_to_all | solution.py:675
  321.7 30.1 %collective-permute-start.39 = (bf16[4,512,256]{2,1,0:T(8,128)(2,1)S(1)}, bf16[4,512,256]{2,1,0:T(8,128)(2,1)}, u32[]{:S(2)}, u32[]{:S(2)}) collective-permute-start(bf16[4,512,256]{2,1,0:T(8,128)(2,1)S(1)} %constant_dynamic-update-slice_fusion.refs_6_), channel_id=1, source_target_pairs={{0,4},{4,0},{8,12},{12,8},{16,20},{20,16},{24,28},{28,24},{1,5},{5... | collective-permute-start | bytes 3145736 | tf_op jit(solution)/shard_map/ppermute | solution.py:665
  322.3 29.6 %collective-permute-start.38 = (bf16[512,1024]{1,0:T(8,128)(2,1)S(1)}, bf16[512,1024]{1,0:T(8,128)(2,1)}, u32[]{:S(2)}, u32[]{:S(2)}) collective-permute-start(bf16[512,1024]{1,0:T(8,128)(2,1)S(1)} %copy-done.2), channel_id=1, source_target_pairs={{0,4},{4,0},{8,12},{12,8},{16,20},{20,16},{24,28},{28,24},{1,5},{5... | collective-permute-start | bytes 3145736 | tf_op jit(solution)/shard_map/ppermute | solution.py:665
  324.1 99.2 %collective-permute-start.57 = (bf16[4,512,1024]{2,1,0:T(8,128)(2,1)}, bf16[4,512,1024]{2,1,0:T(8,128)(2,1)}, u32[]{:S(2)}, u32[]{:S(2)}) collective-permute-start(bf16[4,512,1024]{2,1,0:T(8,128)(2,1)} %get-tuple-element.58.act_ref.refs_2_), channel_id=1, source_target_pairs={{0,4},{4,0},{8,12},{12,8},{16,20},{20,16},{24,28},{28,24},{1,5},{5... | collective-permute-start | bytes 12582920 | tf_op jit(solution)/shard_map/ppermute | solution.py:665
  346.3 31.0 %all-to-all-start.3 = ((bf16[4,128,1024]{2,1,0:T(8,128)(2,1)}), bf16[4,128,1024]{2,1,0:T(8,128)(2,1)}, u32[]{:S(2)}, u32[]{:S(2)}) async-start(bf16[4,128,1024]{2,1,0:T(8,128)(2,1)} %bitcast.198), calls=%async_computation.3 | async-start | bytes 2097152 | tf_op jit(solution)/shard_map/all_to_all | solution.py:675
  351.8 45.2 %collective-permute-start.47 = (bf16[512,1024]{1,0:T(8,128)(2,1)}, bf16[512,1024]{1,0:T(8,128)(2,1)}, u32[]{:S(2)}, u32[]{:S(2)}) collective-permute-start(bf16[512,1024]{1,0:T(8,128)(2,1)} %get-tuple-element.84.refs_0_), channel_id=1, source_target_pairs={{0,4},{4,0},{8,12},{12,8},{16,20},{20,16},{24,28},{28,24},{1,5},{5... | collective-permute-start | bytes 3145736 | tf_op jit(solution)/shard_map/ppermute | solution.py:665
  360.4 25.7 %collective-permute-start.43 = (bf16[2,2,128,1024]{3,2,0,1:T(8,128)(2,1)S(1)}, bf16[2,2,128,1024]{3,2,0,1:T(8,128)(2,1)}, u32[]{:S(2)}, u32[]{:S(2)}) collective-permute-start(bf16[2,2,128,1024]{3,2,0,1:T(8,128)(2,1)S(1)} %copy.135), channel_id=1, source_target_pairs={{0,16},{4,20},{8,24},{12,28},{16,0},{20,4},{24,8},{28,12},{1,17},{... | collective-permute-start | bytes 3145736 | tf_op jit(solution)/shard_map/ppermute | solution.py:665
  370.9 25.5 %collective-permute-start.40 = (bf16[2,2,128,1024]{3,2,0,1:T(8,128)(2,1)}, bf16[2,2,128,1024]{3,2,0,1:T(8,128)(2,1)S(1)}, u32[]{:S(2)}, u32[]{:S(2)}) collective-permute-start(bf16[2,2,128,1024]{3,2,0,1:T(8,128)(2,1)} %copy.132), channel_id=1, source_target_pairs={{0,8},{4,12},{8,0},{12,4},{16,24},{20,28},{24,16},{28,20},{1,9},{5... | collective-permute-start | bytes 3145736 | tf_op jit(solution)/shard_map/ppermute | solution.py:665
  386.1 34.8 %collective-permute-start.56 = (bf16[512,1024]{1,0:T(8,128)(2,1)S(1)}, bf16[512,1024]{1,0:T(8,128)(2,1)S(1)}, u32[]{:S(2)}, u32[]{:S(2)}) collective-permute-start(bf16[512,1024]{1,0:T(8,128)(2,1)S(1)} %copy-done.7), channel_id=1, source_target_pairs={{0,4},{4,0},{8,12},{12,8},{16,20},{20,16},{24,28},{28,24},{1,5},{5... | collective-permute-start | bytes 3145736 | tf_op jit(solution)/shard_map/ppermute | solution.py:665
  396.4 19.9 %collective-permute-start.44 = (bf16[2,128,1024]{2,1,0:T(8,128)(2,1)S(1)}, bf16[2,128,1024]{2,1,0:T(8,128)(2,1)S(1)}, u32[]{:S(2)}, u32[]{:S(2)}) collective-permute-start(bf16[2,128,1024]{2,1,0:T(8,128)(2,1)S(1)} %fusion.4), channel_id=1, source_target_pairs={{0,8},{4,12},{8,0},{12,4},{16,24},{20,28},{24,16},{28,20},{1,9},{5... | collective-permute-start | bytes 1572872 | tf_op jit(solution)/shard_map/ppermute | solution.py:665
  397.1 21.5 %collective-permute-start.41 = (bf16[2,128,1024]{2,1,0:T(8,128)(2,1)S(1)}, bf16[2,128,1024]{2,1,0:T(8,128)(2,1)S(1)}, u32[]{:S(2)}, u32[]{:S(2)}) collective-permute-start(bf16[2,128,1024]{2,1,0:T(8,128)(2,1)S(1)} %fusion.3), channel_id=1, source_target_pairs={{0,16},{4,20},{8,24},{12,28},{16,0},{20,4},{24,8},{28,12},{1,17},{... | collective-permute-start | bytes 1572872 | tf_op jit(solution)/shard_map/ppermute | solution.py:665
  406.9 36.6 %collective-permute-start.49 = (bf16[2,2,128,1024]{3,2,0,1:T(8,128)(2,1)}, bf16[2,2,128,1024]{3,2,0,1:T(8,128)(2,1)}, u32[]{:S(2)}, u32[]{:S(2)}) collective-permute-start(bf16[2,2,128,1024]{3,2,0,1:T(8,128)(2,1)} %copy.139), channel_id=1, source_target_pairs={{0,8},{4,12},{8,0},{12,4},{16,24},{20,28},{24,16},{28,20},{1,9},{5... | collective-permute-start | bytes 3145736 | tf_op jit(solution)/shard_map/ppermute | solution.py:665
  416.2 29.2 %collective-permute-start.52 = (bf16[2,2,128,1024]{3,2,0,1:T(8,128)(2,1)}, bf16[2,2,128,1024]{3,2,0,1:T(8,128)(2,1)}, u32[]{:S(2)}, u32[]{:S(2)}) collective-permute-start(bf16[2,2,128,1024]{3,2,0,1:T(8,128)(2,1)} %copy.142), channel_id=1, source_target_pairs={{0,16},{4,20},{8,24},{12,28},{16,0},{20,4},{24,8},{28,12},{1,17},{... | collective-permute-start | bytes 3145736 | tf_op jit(solution)/shard_map/ppermute | solution.py:665
  418.6 12.5 %collective-permute-start.46 = (bf16[128,1024]{1,0:T(8,128)(2,1)S(1)}, bf16[128,1024]{1,0:T(8,128)(2,1)S(1)}, u32[]{:S(2)}, u32[]{:S(2)}) collective-permute-start(bf16[128,1024]{1,0:T(8,128)(2,1)S(1)} %get-tuple-element.171), channel_id=1, source_target_pairs={{0,1},{1,2},{2,3},{3,0},{4,5},{5,6},{6,7},{7,4},{8,9},{9,10},{10,1... | collective-permute-start | bytes 786440 | tf_op jit(solution)/shard_map/ppermute | solution.py:668
  420.9 19.6 %collective-permute-start.45 = (bf16[128,1024]{1,0:T(8,128)(2,1)S(1)}, bf16[128,1024]{1,0:T(8,128)(2,1)S(1)}, u32[]{:S(2)}, u32[]{:S(2)}) collective-permute-start(bf16[128,1024]{1,0:T(8,128)(2,1)S(1)} %get-tuple-element.170), channel_id=1, source_target_pairs={{0,2},{1,3},{2,0},{3,1},{4,6},{5,7},{6,4},{7,5},{8,10},{9,11},{10,... | collective-permute-start | bytes 786440 | tf_op jit(solution)/shard_map/ppermute | solution.py:668
  423.4 18.1 %collective-permute-start.42 = (bf16[128,1024]{1,0:T(8,128)(2,1)S(1)}, bf16[128,1024]{1,0:T(8,128)(2,1)S(1)}, u32[]{:S(2)}, u32[]{:S(2)}) collective-permute-start(bf16[128,1024]{1,0:T(8,128)(2,1)S(1)} %fusion.22), channel_id=1, source_target_pairs={{0,3},{1,0},{2,1},{3,2},{4,7},{5,4},{6,5},{7,6},{8,11},{9,8},{10,9... | collective-permute-start | bytes 786440 | tf_op jit(solution)/shard_map/ppermute | solution.py:668
  431.1 34.0 %collective-permute-start.61 = (bf16[2,2,128,1024]{3,2,1,0:T(8,128)(2,1)}, bf16[2,2,128,1024]{3,2,1,0:T(8,128)(2,1)}, u32[]{:S(2)}, u32[]{:S(2)}) collective-permute-start(bf16[2,2,128,1024]{3,2,1,0:T(8,128)(2,1)} %get-tuple-element.93), channel_id=1, source_target_pairs={{0,16},{4,20},{8,24},{12,28},{16,0},{20,4},{24,8},{28,12},{1,17},{... | collective-permute-start | bytes 3145736 | tf_op jit(solution)/shard_map/ppermute | solution.py:665
  440.6 26.8 %collective-permute-start.58 = (bf16[2,2,128,1024]{3,2,0,1:T(8,128)(2,1)}, bf16[2,2,128,1024]{3,2,0,1:T(8,128)(2,1)}, u32[]{:S(2)}, u32[]{:S(2)}) collective-permute-start(bf16[2,2,128,1024]{3,2,0,1:T(8,128)(2,1)} %copy.145), channel_id=1, source_target_pairs={{0,8},{4,12},{8,0},{12,4},{16,24},{20,28},{24,16},{28,20},{1,9},{5... | collective-permute-start | bytes 3145736 | tf_op jit(solution)/shard_map/ppermute | solution.py:665
  444.8 49.3 %collective-permute-start.50 = (bf16[2,128,1024]{2,1,0:T(8,128)(2,1)S(1)}, bf16[2,128,1024]{2,1,0:T(8,128)(2,1)S(1)}, u32[]{:S(2)}, u32[]{:S(2)}) collective-permute-start(bf16[2,128,1024]{2,1,0:T(8,128)(2,1)S(1)} %fusion.5), channel_id=1, source_target_pairs={{0,16},{4,20},{8,24},{12,28},{16,0},{20,4},{24,8},{28,12},{1,17},{... | collective-permute-start | bytes 1572872 | tf_op jit(solution)/shard_map/ppermute | solution.py:665
  446.9 31.2 %collective-permute-start.53 = (bf16[2,128,1024]{2,1,0:T(8,128)(2,1)S(1)}, bf16[2,128,1024]{2,1,0:T(8,128)(2,1)S(1)}, u32[]{:S(2)}, u32[]{:S(2)}) collective-permute-start(bf16[2,128,1024]{2,1,0:T(8,128)(2,1)S(1)} %fusion.6), channel_id=1, source_target_pairs={{0,8},{4,12},{8,0},{12,4},{16,24},{20,28},{24,16},{28,20},{1,9},{5... | collective-permute-start | bytes 1572872 | tf_op jit(solution)/shard_map/ppermute | solution.py:665
  466.4 19.8 %collective-permute-start.62 = (bf16[2,128,1024]{2,1,0:T(8,128)(2,1)S(1)}, bf16[2,128,1024]{2,1,0:T(8,128)(2,1)S(1)}, u32[]{:S(2)}, u32[]{:S(2)}) collective-permute-start(bf16[2,128,1024]{2,1,0:T(8,128)(2,1)S(1)} %fusion.8), channel_id=1, source_target_pairs={{0,8},{4,12},{8,0},{12,4},{16,24},{20,28},{24,16},{28,20},{1,9},{5... | collective-permute-start | bytes 1572872 | tf_op jit(solution)/shard_map/ppermute | solution.py:665
  468.6 20.8 %collective-permute-start.59 = (bf16[2,128,1024]{2,1,0:T(8,128)(2,1)S(1)}, bf16[2,128,1024]{2,1,0:T(8,128)(2,1)S(1)}, u32[]{:S(2)}, u32[]{:S(2)}) collective-permute-start(bf16[2,128,1024]{2,1,0:T(8,128)(2,1)S(1)} %fusion.7), channel_id=1, source_target_pairs={{0,16},{4,20},{8,24},{12,28},{16,0},{20,4},{24,8},{28,12},{1,17},{... | collective-permute-start | bytes 1572872 | tf_op jit(solution)/shard_map/ppermute | solution.py:665
  480.2 38.1 %collective-permute-start.55 = (bf16[128,1024]{1,0:T(8,128)(2,1)}, bf16[128,1024]{1,0:T(8,128)(2,1)}, u32[]{:S(2)}, u32[]{:S(2)}) collective-permute-start(bf16[128,1024]{1,0:T(8,128)(2,1)} %get-tuple-element.169), channel_id=1, source_target_pairs={{0,1},{1,2},{2,3},{3,0},{4,5},{5,6},{6,7},{7,4},{8,9},{9,10},{10,1... | collective-permute-start | bytes 786440 | tf_op jit(solution)/shard_map/ppermute | solution.py:668
  484.5 33.9 %collective-permute-start.54 = (bf16[128,1024]{1,0:T(8,128)(2,1)}, bf16[128,1024]{1,0:T(8,128)(2,1)}, u32[]{:S(2)}, u32[]{:S(2)}) collective-permute-start(bf16[128,1024]{1,0:T(8,128)(2,1)} %get-tuple-element.168), channel_id=1, source_target_pairs={{0,2},{1,3},{2,0},{3,1},{4,6},{5,7},{6,4},{7,5},{8,10},{9,11},{10,... | collective-permute-start | bytes 786440 | tf_op jit(solution)/shard_map/ppermute | solution.py:668
  487.5 15.2 %collective-permute-start.64 = (bf16[128,1024]{1,0:T(8,128)(2,1)S(1)}, bf16[128,1024]{1,0:T(8,128)(2,1)S(1)}, u32[]{:S(2)}, u32[]{:S(2)}) collective-permute-start(bf16[128,1024]{1,0:T(8,128)(2,1)S(1)} %get-tuple-element.167), channel_id=1, source_target_pairs={{0,1},{1,2},{2,3},{3,0},{4,5},{5,6},{6,7},{7,4},{8,9},{9,10},{10,1... | collective-permute-start | bytes 786440 | tf_op jit(solution)/shard_map/ppermute | solution.py:668
  489.4 26.0 %collective-permute-start.63 = (bf16[128,1024]{1,0:T(8,128)(2,1)S(1)}, bf16[128,1024]{1,0:T(8,128)(2,1)S(1)}, u32[]{:S(2)}, u32[]{:S(2)}) collective-permute-start(bf16[128,1024]{1,0:T(8,128)(2,1)S(1)} %get-tuple-element.166), channel_id=1, source_target_pairs={{0,2},{1,3},{2,0},{3,1},{4,6},{5,7},{6,4},{7,5},{8,10},{9,11},{10,... | collective-permute-start | bytes 786440 | tf_op jit(solution)/shard_map/ppermute | solution.py:668
  494.1 21.3 %collective-permute-start.60 = (bf16[128,1024]{1,0:T(8,128)(2,1)S(1)}, bf16[128,1024]{1,0:T(8,128)(2,1)S(1)}, u32[]{:S(2)}, u32[]{:S(2)}) collective-permute-start(bf16[128,1024]{1,0:T(8,128)(2,1)S(1)} %fusion.24), channel_id=1, source_target_pairs={{0,3},{1,0},{2,1},{3,2},{4,7},{5,4},{6,5},{7,6},{8,11},{9,8},{10,9... | collective-permute-start | bytes 786440 | tf_op jit(solution)/shard_map/ppermute | solution.py:668
  502.7 20.1 %collective-permute-start.51 = (bf16[128,1024]{1,0:T(8,128)(2,1)S(1)}, bf16[128,1024]{1,0:T(8,128)(2,1)}, u32[]{:S(2)}, u32[]{:S(2)}) collective-permute-start(bf16[128,1024]{1,0:T(8,128)(2,1)S(1)} %fusion.23), channel_id=1, source_target_pairs={{0,3},{1,0},{2,1},{3,2},{4,7},{5,4},{6,5},{7,6},{8,11},{9,8},{10,9... | collective-permute-start | bytes 786440 | tf_op jit(solution)/shard_map/ppermute | solution.py:668
  (47 other events, 828.8 us)

commit v3 on v2

v3 whole, which is shorter than its diff:
```python
import functools
import math

import jax
import jax.numpy as jnp
from jax import lax
from jax.experimental import pallas as pl
from jax.experimental.pallas import tpu as pltpu
from jax.sharding import PartitionSpec as P

HD = 64
f32 = jnp.float32
bf16 = jnp.bfloat16
VMEM_LIMIT = 56 * 2**20


def params(**more):
    return pltpu.CompilerParams(vmem_limit_bytes=VMEM_LIMIT, **more)


def dot(a, b, dims):
    return lax.dot_general(a, b, (dims, ((), ())), preferred_element_type=f32)


def sinusoid(steps, model_width):
    half_width = model_width // 2
    freqs = jnp.exp(-math.log(10000.0) * jnp.arange(half_width, dtype=f32) / half_width)
    angles = steps[:, None] * freqs[None, :]
    return jnp.concatenate([jnp.sin(angles), jnp.cos(angles)], axis=-1).astype(bf16)


def masks(place):
    first = 2 + 2 * (place & 1)
    return first, 6 - first


class Gathered:
    def __init__(self, own, pieces, lead, start):
        self.arrays = [own] + pieces
        self.lead = lead
        self.start = start
        self.dims = own.shape

    def scratch(self, shards):
        return [pltpu.VMEM((shards,) + self.dims, bf16), pltpu.SemaphoreType.DMA((shards, 8))]

    def copies_of(self, refs, place, into, sems, shard, slot):
        if isinstance(shard, int) and shard == 0:
            return [pltpu.make_async_copy(refs[0], into.at[slot], sems.at[slot, 0])]
        lead = (slice(None),) * self.lead
        first, second = masks(place)
        held = (place, place ^ first)
        far = (place ^ second, place ^ 6)
        held2 = (place ^ 1, place ^ 1 ^ second)
        far2 = (place ^ 1 ^ first, place ^ 7)
        made = []
        for ref, chunks in zip(refs[1:], (held, far, held2, far2)):
            for i, chunk in enumerate(chunks):
                at = lead + (pl.ds(self.start, self.dims[-2]),)
                made.append(
                    pltpu.make_async_copy(
                        ref.at[i, shard - 1].at[at],
                        into.at[(slot,) + lead + (chunk,)],
                        sems.at[slot, len(made)],
                    )
                )
        return made

    def start_all(self, refs, place, into, sems, shards):
        for shard in range(shards):
            for copy in self.copies_of(refs, place, into, sems, shard, shard):
                copy.start()

    def wait(self, refs, place, into, sems, shard):
        @pl.when(shard == 0)
        def _():
            for copy in self.copies_of(refs, place, into, sems, 0, 0):
                copy.wait()

        @pl.when(shard > 0)
        def _():
            for copy in self.copies_of(refs, place, into, sems, shard, shard):
                copy.wait()


HBM = pl.BlockSpec(memory_space=pl.ANY)
SMEM = pl.BlockSpec(memory_space=pltpu.SMEM)


def whole(shape):
    return pl.BlockSpec(shape, lambda *_: (0,) * len(shape))


def cost(micros):
    return pl.CostEstimate(flops=int(micros * 1.15e9), transcendentals=0, bytes_accessed=0)


def over_rows(length, step, body, init):
    def one(i, carry):
        return body(pl.ds(pl.multiple_of(i * step, step), step), carry)

    return lax.fori_loop(0, length // step, one, init)


def row_sum(v):
    return jnp.sum(v, axis=0, keepdims=True)


def pack_body(rows, n, *refs):
    out_ref = refs[n]
    for i, ref in enumerate(refs[:n]):
        out_ref[i] = ref[..., :rows, :]
        if len(refs) > n + 1:
            total = ref[..., rows : rows + 1, :].astype(f32)
            for part in range(1, 3):
                total += ref[..., rows + part : rows + part + 1, :].astype(f32)
            refs[n + 1][i] = total


def pack(covers, parts, rows=None):
    dims = parts[0].shape
    n = len(parts)
    out = [(n,) + dims[:-2] + (rows or dims[-2], dims[-1])]
    if rows:
        out.append((n,) + dims[:-2] + (1, dims[-1]))
    made = pl.pallas_call(
        functools.partial(pack_body, rows or dims[-2], n),
        out_shape=[jax.ShapeDtypeStruct(o, t) for o, t in zip(out, (bf16, f32))],
        compiler_params=params(),
        cost_estimate=cost(covers),
        name="pack",
    )(*parts)
    return made if rows else made[0]


def in_three(v):
    parts = []
    for _ in range(3):
        parts.append(lax.reduce_precision(v, 8, 7))
        v = v - parts[-1]
    return jnp.concatenate(parts + [jnp.zeros_like(v)] * 5, axis=-2).astype(bf16)


def embed_body(sinus_ref, w_ref, row_ref, out_ref):
    out_ref[...] = dot(sinus_ref[...], w_ref[...], ((1,), (0,)))[:1] + row_ref[...]


def embed(covers, sinus, w, row):
    return pl.pallas_call(
        embed_body,
        out_shape=jax.ShapeDtypeStruct(row.shape, f32),
        compiler_params=params(),
        cost_estimate=cost(covers),
        name="embed",
    )(jnp.broadcast_to(sinus, (16,) + sinus.shape[1:]), w, row)


def attend_body(shard, gathered, place_ref, x_ref, bias_ref, *refs):
    n = len(gathered.arrays)
    w_refs = refs[:n]
    qkv_ref, p_ref, c_ref, w, sems = refs[-5:]
    pair = pl.program_id(0)
    place = place_ref[0]
    cols = w.shape[-1]

    @pl.when(pair == 0)
    def _():
        copies = gathered.copies_of(w_refs, place, w, sems, shard, 0)
        for copy in copies:
            copy.start()
        for copy in copies:
            copy.wait()
        for c in range(3):
            wide = w[0, c].reshape(x_ref.shape[1], cols)
            out = dot(x_ref[...], wide, ((1,), (0,))) + bias_ref[0, c]
            qkv_ref[0, :, c * cols : (c + 1) * cols] = out.astype(bf16)

    at = pl.multiple_of(pair * 2 * HD, 2 * HD)
    q = qkv_ref[0, :, pl.ds(at, 2 * HD)]
    k = qkv_ref[0, :, pl.ds(cols + at, 2 * HD)]
    v = qkv_ref[0, :, pl.ds(2 * cols + at, 2 * HD)]
    lane = lax.broadcasted_iota(jnp.int32, q.shape, 1)
    joined = None
    for hh in range(2):
        mine = (lane // HD) == hh
        kh = jnp.where(mine, k, jnp.zeros_like(k))
        st = dot(kh, q, ((1,), (1,))) * 0.125
        top = jnp.max(st, axis=0, keepdims=True)
        e = jnp.exp(st - top)
        p = (e * (1.0 / jnp.sum(e, axis=0, keepdims=True))).astype(bf16)
        p_ref[0, hh] = p
        c = dot(p, v, ((0,), (0,)))
        joined = c if joined is None else jnp.where(mine, c, joined)
    c_ref[0] = joined.astype(bf16)


def attend(covers, shard, shards, gathered, place, x, bias, old):
    length, width = x.shape
    cols = gathered.dims[-1]
    pairs = cols // (2 * HD)
    n_w = len(gathered.arrays)
    return pl.pallas_call(
        functools.partial(attend_body, shard, gathered),
        grid=(pairs,),
        out_shape=[
            jax.ShapeDtypeStruct((shards, length, 3 * cols), bf16),
            jax.ShapeDtypeStruct((shards, 2 * pairs, length, length), bf16),
            jax.ShapeDtypeStruct((shards, length, cols), bf16),
        ],
        in_specs=[SMEM, whole(x.shape), pl.BlockSpec((1, 3, 1, cols), lambda i: (max(shard - 1, 0), 0, 0, 0))]
        + [HBM] * (n_w + len(old)),
        out_specs=[
            pl.BlockSpec((1, length, 3 * cols), lambda i: (shard, 0, 0)),
            pl.BlockSpec((1, 2, length, length), lambda i: (shard, i, 0, 0)),
            pl.BlockSpec((1, length, 2 * HD), lambda i: (shard, 0, i)),
        ],
        input_output_aliases={3 + n_w + i: i for i in range(len(old))},
        scratch_shapes=gathered.scratch(1),
        compiler_params=params(),
        cost_estimate=cost(covers),
        name="attend",
    )(place, x, bias, *gathered.arrays, *old)


def norm_stats(values):
    center = values - jnp.mean(values, axis=-1, keepdims=True)
    inv = lax.rsqrt(jnp.mean(center * center, axis=-1, keepdims=True) + 1e-05)
    return center * inv, inv


def norm_back(grad, n, inv, gain):
    gn = grad * gain
    return (gn - jnp.mean(gn, -1, keepdims=True) - n * jnp.mean(gn * n, -1, keepdims=True)) * inv


def up_body(
    shards, g_out, g_up, place_ref, ctx_ref, x_ref, te_ref, b_ref, gain_ref, shift_ref, bias_ref, *refs
):
    n_out = len(g_out.arrays)
    out_refs = list(refs[:n_out])
    up_refs = [refs[n_out]] + list(refs[1:n_out])
    n1_ref, inv_ref, low_ref, act_ref, slope_ref, wo_full, wu_full = refs[n_out + 1 : n_out + 8]
    wo, o_sems, wu, u_sems, acc, keep_o, keep_u = refs[n_out + 8 :]
    s = pl.program_id(0)
    place = place_ref[0]
    length, width = acc.shape

    def keep_out(shard):
        return pltpu.make_async_copy(wo.at[shard], wo_full.at[shard], keep_o.at[shard])

    def keep_up(shard):
        return pltpu.make_async_copy(wu.at[shard], wu_full.at[shard], keep_u.at[shard])

    @pl.when(s == 0)
    def _():
        g_out.start_all(out_refs, place, wo, o_sems, shards)
        g_up.start_all(up_refs, place, wu, u_sems, shards)
        for shard in range(shards):
            g_out.wait(out_refs, place, wo, o_sems, shard)
            keep_out(shard).start()
            part = dot(ctx_ref[shard], wo[shard].reshape(-1, width), ((1,), (0,)))
            if shard == 0:
                acc[...] = part
            else:
                acc[...] += part

        def rows(at, _):
            start = x_ref[at, :].astype(f32) + te_ref[...]
            n1, inv = norm_stats(start + (acc[at, :] + b_ref[...]))
            n1_ref[at, :] = n1
            inv_ref[at, :] = jnp.broadcast_to(inv, (64, inv_ref.shape[1]))
            low_ref[at, :] = (n1 * gain_ref[...] + shift_ref[...]).astype(bf16)
            return 0

        over_rows(length, 64, rows, 0)

    g_up.wait(up_refs, place, wu, u_sems, s)
    keep_up(s).start()
    units = wu.shape[-1]
    for n in range(units // 256):
        span = slice(n * 256, (n + 1) * 256)
        u = dot(low_ref[...], wu[s, :, :, span].reshape(width, 256), ((1,), (0,)))
        u = u + bias_ref[0, :, span]
        phi = 0.5 + 0.5 * lax.erf(u * (2.0**-0.5))
        act_ref[0, :, span] = (u * phi).astype(bf16)
        slope_ref[0, :, span] = (
            phi + u * jnp.exp(-0.5 * u * u) * (2.0 * math.pi) ** -0.5
        ).astype(bf16)

    @pl.when(s == shards - 1)
    def _():
        for shard in range(shards):
            keep_out(shard).wait()
            keep_up(shard).wait()


def up_project(g_out, g_up, place, ctx, x, time_embed, b_out, gain, shift, bias):
    length, width = x.shape
    shards = ctx.shape[0]
    units = g_up.dims[-1]
    block = pl.BlockSpec((1, length, units), lambda s: (s, 0, 0))
    row = whole((1, width))
    return pl.pallas_call(
        functools.partial(up_body, shards, g_out, g_up),
        grid=(shards,),
        out_shape=[
            jax.ShapeDtypeStruct((length, width), f32),
            jax.ShapeDtypeStruct((length, 128), f32),
            jax.ShapeDtypeStruct((length, width), bf16),
            jax.ShapeDtypeStruct((shards, length, units), bf16),
            jax.ShapeDtypeStruct((shards, length, units), bf16),
            jax.ShapeDtypeStruct((shards,) + g_out.dims, bf16),
            jax.ShapeDtypeStruct((shards,) + g_up.dims, bf16),
        ],
        in_specs=[
            SMEM,
            whole(ctx.shape),
            whole(x.shape),
            row,
            row,
            row,
            row,
            pl.BlockSpec((1, 1, units), lambda s: (s, 0, 0)),
        ]
        + [HBM] * (len(g_out.arrays) + 1),
        out_specs=[
            whole((length, width)),
            whole((length, 128)),
            whole((length, width)),
            block,
            block,
            HBM,
            HBM,
        ],
        scratch_shapes=g_out.scratch(shards)
        + g_up.scratch(shards)
        + [pltpu.VMEM((length, width), f32)]
        + [pltpu.SemaphoreType.DMA((shards,))] * 2,
        compiler_params=params(),
        cost_estimate=cost(40),
        name="up_project",
    )(place, ctx, x, time_embed, b_out, gain, shift, bias, *g_out.arrays, g_up.arrays[0])


def down_body(
    shards, gathered, place_ref, live_ref, act_ref, b_ref, gain1_ref, shift1_ref, gain2_ref, shift2_ref,
    n1_hbm, cot_hbm, *refs
):
    n = len(gathered.arrays)
    w_refs, (out_ref, gs_ref, bg_ref, sums_ref, w_full) = refs[:n], refs[n : n + 5]
    w, sems, acc, n1_ref, cot_ref, late, keep_sems = refs[n + 5 :]
    s = pl.program_id(0)
    place = place_ref[0]
    length, width = acc.shape

    def fetch(i):
        return pltpu.make_async_copy((n1_hbm, cot_hbm)[i], (n1_ref, cot_ref)[i], late.at[i])

    def keep(shard):
        return pltpu.make_async_copy(w.at[shard], w_full.at[shard], keep_sems.at[shard])

    @pl.when(s == 0)
    def _():
        gathered.start_all(w_refs, place, w, sems, shards)
        fetch(0).start()
        fetch(1).start()

    gathered.wait(w_refs, place, w, sems, s)
    keep(s).start()
    part = dot(act_ref[0], w[s].reshape(-1, width), ((1,), (0,)))

    @pl.when(s == 0)
    def _():
        acc[...] = part

    @pl.when(s > 0)
    def _():
        acc[...] += part

    @pl.when(s == shards - 1)
    def _():
        live = live_ref[0]
        fetch(0).wait()
        fetch(1).wait()

        def rows(at, sums):
            normed = n1_ref[at, :] * gain1_ref[...] + shift1_ref[...]
            n2, inv = norm_stats(normed + (acc[at, :] + b_ref[...]))
            out_ref[at, :] = (n2 * gain2_ref[...] + shift2_ref[...]).astype(bf16)
            grad = cot_ref[at, :].astype(f32) * live
            second = norm_back(grad, n2, inv, gain2_ref[...])
            gs_ref[at, :] = second
            low = second.astype(bf16)
            bg_ref[at, :] = low
            add = (low.astype(f32), grad * n2, grad)
            return tuple(a + row_sum(b) for a, b in zip(sums, add))

        zero = jnp.zeros((1, width), f32)
        sums = over_rows(length, 64, rows, (zero, zero, zero))
        for i, v in enumerate(sums):
            sums_ref[i : i + 1, :] = v
        for shard in range(shards):
            keep(shard).wait()


def down_project(gathered, place, live, act, n1, cot, b_down, gain1, shift1, gain2, shift2):
    shards, length, units = act.shape
    width = n1.shape[1]
    row = whole((1, width))
    return pl.pallas_call(
        functools.partial(down_body, shards, gathered),
        grid=(shards,),
        out_shape=[
            jax.ShapeDtypeStruct((length, width), bf16),
            jax.ShapeDtypeStruct((length, width), f32),
            jax.ShapeDtypeStruct((length, width), bf16),
            jax.ShapeDtypeStruct((3, width), f32),
            jax.ShapeDtypeStruct((shards,) + gathered.dims, bf16),
        ],
        in_specs=[SMEM, SMEM, pl.BlockSpec((1, length, units), lambda s: (s, 0, 0))]
        + [row] * 5
        + [HBM] * (2 + len(gathered.arrays)),
        out_specs=[whole((length, width))] * 3 + [whole((3, width)), HBM],
        scratch_shapes=gathered.scratch(shards)
        + [
            pltpu.VMEM((length, width), f32),
            pltpu.VMEM((length, width), f32),
            pltpu.VMEM((length, width), bf16),
            pltpu.SemaphoreType.DMA((2,)),
            pltpu.SemaphoreType.DMA((shards,)),
        ],
        compiler_params=params(),
        cost_estimate=cost(40),
        name="down_project",
    )(place, live, act, b_down, gain1, shift1, gain2, shift2, n1, cot, *gathered.arrays)


def up_back_body(
    shards, bg_ref, slope_ref, wd_ref, wu_ref, inv_ref, gain_ref, gs_hbm, n1_hbm,
    ug_ref, bias_ref, gf_ref, mg_ref, sums_ref, acc, gs_ref, n1_ref, late
):
    s = pl.program_id(0)
    length, width = acc.shape

    def fetch(i):
        return pltpu.make_async_copy((gs_hbm, n1_hbm)[i], (gs_ref, n1_ref)[i], late.at[i])

    @pl.when(s == 0)
    def _():
        fetch(0).start()
        fetch(1).start()

    units = ug_ref.shape[2]
    for n in range(units // 256):
        span = slice(n * 256, (n + 1) * 256)
        grad = dot(bg_ref[...], wd_ref[0, span, :], ((1,), (1,)))
        low = (grad * slope_ref[0, :, span].astype(f32)).astype(bf16)
        ug_ref[0, :, span] = low
        bias_ref[0, :, span] = row_sum(low.astype(f32))
    part = dot(ug_ref[0], wu_ref[0], ((1,), (1,)))

    @pl.when(s == 0)
    def _():
        acc[...] = part

    @pl.when(s > 0)
    def _():
        acc[...] += part

    @pl.when(s == shards - 1)
    def _():
        fetch(0).wait()
        fetch(1).wait()

        def rows(at, sums):
            n1, grad = n1_ref[at, :], acc[at, :] + gs_ref[at, :]
            first = norm_back(grad, n1, inv_ref[at, 0:1], gain_ref[...])
            gf_ref[at, :] = first
            low = first.astype(bf16)
            mg_ref[at, :] = low
            add = (low.astype(f32), grad * n1, grad)
            return tuple(a + row_sum(b) for a, b in zip(sums, add))

        zero = jnp.zeros((1, width), f32)
        sums = over_rows(length, 64, rows, (zero, zero, zero))
        for i, v in enumerate(sums):
            sums_ref[i : i + 1, :] = v


def up_back(w_down, w_up, bg, slope, gs, n1, inv, gain):
    shards, length, units = slope.shape
    width = n1.shape[1]
    block = pl.BlockSpec((1, length, units), lambda s: (s, 0, 0))
    return pl.pallas_call(
        functools.partial(up_back_body, shards),
        grid=(shards,),
        out_shape=[
            jax.ShapeDtypeStruct((shards, length, units), bf16),
            jax.ShapeDtypeStruct((shards, 1, units), f32),
            jax.ShapeDtypeStruct((length, width), f32),
            jax.ShapeDtypeStruct((length, width), bf16),
            jax.ShapeDtypeStruct((3, width), f32),
        ],
        in_specs=[
            whole(bg.shape),
            block,
            pl.BlockSpec((1, units, width), lambda s: (s, 0, 0)),
            pl.BlockSpec((1, width, units), lambda s: (s, 0, 0)),
            whole(inv.shape),
            whole((1, width)),
            HBM,
            HBM,
        ],
        out_specs=[
            block,
            pl.BlockSpec((1, 1, units), lambda s: (s, 0, 0)),
            whole((length, width)),
            whole((length, width)),
            whole((3, width)),
        ],
        scratch_shapes=[pltpu.VMEM((length, width), f32)] * 3 + [pltpu.SemaphoreType.DMA((2,))],
        compiler_params=params(),
        cost_estimate=cost(40),
        name="up_back",
    )(bg, slope, w_down, w_up, inv, gain, gs, n1)


def attend_back_body(mg_ref, wo_ref, qkv, p_of, *refs):
    pg_ref, bias_ref, cg = refs[-3:]
    pair = pl.program_id(1)
    cols = cg.shape[1]

    @pl.when(pair == 0)
    def _():
        cg[...] = dot(mg_ref[...], wo_ref[0], ((1,), (1,))).astype(bf16)

    at = pl.multiple_of(pair * 2 * HD, 2 * HD)
    q = qkv[0, :, pl.ds(at, 2 * HD)]
    k = qkv[0, :, pl.ds(cols + at, 2 * HD)]
    v = qkv[0, :, pl.ds(2 * cols + at, 2 * HD)]
    g = cg[:, pl.ds(at, 2 * HD)]
    lane = lax.broadcasted_iota(jnp.int32, q.shape, 1)
    dq = dk = dv = None
    for hh in range(2):
        mine = (lane // HD) == hh
        zero = jnp.zeros_like(q)
        gh = jnp.where(mine, g, zero)
        kh = jnp.where(mine, k, zero)
        qh = jnp.where(mine, q, zero)
        p = p_of[0, hh]
        dpt = dot(v, gh, ((1,), (1,)))
        pf = p.astype(f32)
        row = row_sum(pf * dpt)
        ds = (pf * (dpt - row)).astype(bf16)
        a = dot(p, gh, ((1,), (0,)))
        b = dot(ds, qh, ((1,), (0,)))
        c = dot(ds, kh, ((0,), (0,)))
        dv = a if dv is None else dv + a
        dk = b if dk is None else dk + b
        dq = c if dq is None else dq + c
    for c, g in enumerate((dq * 0.125, dk * 0.125, dv)):
        low = g.astype(bf16)
        pg_ref[0, :, pl.ds(c * cols + at, 2 * HD)] = low
        bias_ref[0, :, pl.ds(c * cols + at, 2 * HD)] = row_sum(low.astype(f32))


def attend_back(covers, base, count, w_out, mg, qkv, p, pg):
    length, width = mg.shape
    shards, cols = w_out.shape[:2]
    pairs = cols // (2 * HD)
    old = [] if pg is None else [pg]
    return pl.pallas_call(
        attend_back_body,
        grid=(count, pairs),
        out_shape=[
            jax.ShapeDtypeStruct((shards, length, 3 * cols), bf16),
            jax.ShapeDtypeStruct((count, 1, 3 * cols), f32),
        ],
        in_specs=[
            whole(mg.shape),
            pl.BlockSpec((1, cols, width), lambda s, i: (s + base, 0, 0)),
            pl.BlockSpec((1, length, 3 * cols), lambda s, i: (s + base, 0, 0)),
            pl.BlockSpec((1, 2, length, length), lambda s, i: (s + base, i, 0, 0)),
        ]
        + [HBM] * len(old),
        out_specs=[
            pl.BlockSpec((1, length, 3 * cols), lambda s, i: (s + base, 0, 0)),
            pl.BlockSpec((1, 1, 3 * cols), lambda s, i: (s, 0, 0)),
        ],
        input_output_aliases={4: 0} if old else {},
        scratch_shapes=[pltpu.VMEM((length, cols), bf16)],
        compiler_params=params(),
        cost_estimate=cost(covers),
        name="attend_back",
    )(mg, w_out, qkv, p, *old)


def input_back_body(shards, gathered, place_ref, pg_ref, gf_hbm, *refs):
    n = len(gathered.arrays)
    w_refs, (gt_ref, tg_ref, w, sems, acc, gf_ref, late) = refs[:n], refs[n:]
    s = pl.program_id(0)
    place = place_ref[0]
    cols = w.shape[-1]
    length, width = acc.shape
    fetch = pltpu.make_async_copy(gf_hbm, gf_ref, late.at[0])

    @pl.when(s == 0)
    def _():
        gathered.start_all(w_refs, place, w, sems, shards)
        fetch.start()
        acc[...] = jnp.zeros_like(acc)

    gathered.wait(w_refs, place, w, sems, s)
    part = None
    for c in range(3):
        new = dot(pg_ref[0, :, c * cols : (c + 1) * cols], w[s, c].reshape(width, cols), ((1,), (1,)))
        part = new if part is None else part + new
    acc[...] += part

    @pl.when(s == shards - 1)
    def _():
        fetch.wait()

        def rows(at, total):
            grad = acc[at, :] + gf_ref[at, :]
            gt_ref[at, :] = grad.astype(bf16)
            return total + row_sum(grad)

        tg_ref[...] = over_rows(length, 64, rows, jnp.zeros((1, width), f32))


def input_back(gathered, place, pg, gf):
    shards, length, cols3 = pg.shape
    width = gf.shape[1]
    return pl.pallas_call(
        functools.partial(input_back_body, shards, gathered),
        grid=(shards,),
        out_shape=[
            jax.ShapeDtypeStruct((length, width), bf16),
            jax.ShapeDtypeStruct((1, width), f32),
        ],
        in_specs=[SMEM, pl.BlockSpec((1, length, cols3), lambda s: (s, 0, 0)), HBM]
        + [HBM] * len(gathered.arrays),
        out_specs=[whole((length, width)), whole((1, width))],
        scratch_shapes=gathered.scratch(shards)
        + [pltpu.VMEM((length, width), f32)] * 2
        + [pltpu.SemaphoreType.DMA((1,))],
        compiler_params=params(),
        cost_estimate=cost(5),
        name="input_back",
    )(place, pg, gf, *gathered.arrays)


def weight_grad_body(n_pairs, place_ref, *refs):
    ins = refs[: 4 * n_pairs]
    keep_ref, send_ref = refs[4 * n_pairs : 4 * n_pairs + 2]
    turned = refs[4 * n_pairs + 2 :]
    place = place_ref[0]
    rows = keep_ref.shape[2]
    first, second = masks(place)

    @pl.when(pl.program_id(0) == 0)
    def _():
        for p in range(n_pairs):
            for core in range(2):
                feature_ref = ins[4 * p + core]
                length = feature_ref.shape[0]
                for j, mask in enumerate((0, second, first, 6)):
                    at = pl.multiple_of((place ^ mask) * rows, rows)
                    block = feature_ref[:, pl.ds(at, rows)]
                    turned[p][j * rows : (j + 1) * rows, core * length : (core + 1) * length] = block.T

    at = 0
    for p in range(n_pairs):
        b_ref, b2_ref = ins[4 * p + 2 : 4 * p + 4]
        length, cols = b_ref.shape[1:]
        for n in range(cols // 256):
            span = slice(n * 256, (n + 1) * 256)
            g = dot(turned[p][:, :length], b_ref[0, :, span], ((1,), (0,)))
            g += dot(turned[p][:, length:], b2_ref[0, :, span], ((1,), (0,)))
            g = g.astype(bf16)
            for i in range(2):
                keep_ref[i, 0, :, at : at + 256] = g[i * rows : (i + 1) * rows]
                send_ref[i, 0, :, at : at + 256] = g[(i + 2) * rows : (i + 3) * rows]
            at += 256


def weight_grad(covers, place, groups):
    shards, length, _ = groups[0][2].shape
    rows = groups[0][0].shape[1] // 8
    cols = sum(g[2].shape[2] for g in groups)
    specs, args, scratch = [], [], []
    for feature, feature2, b, b2 in groups:
        block = pl.BlockSpec((1,) + b.shape[1:], lambda s: (s, 0, 0))
        specs += [whole(feature.shape)] * 2 + [block] * 2
        args += [feature, feature2, b, b2]
        scratch.append(pltpu.VMEM((4 * rows, 2 * length), bf16))
    out = jax.ShapeDtypeStruct((2, shards, rows, cols), bf16)
    return pl.pallas_call(
        functools.partial(weight_grad_body, len(groups)),
        grid=(shards,),
        out_shape=[out] * 2,
        in_specs=[SMEM] + specs,
        out_specs=[pl.BlockSpec((2, 1, rows, cols), lambda s: (0, s, 0, 0))] * 2,
        scratch_shapes=scratch,
        compiler_params=params(),
        cost_estimate=cost(covers),
        name="weight_grad",
    )(place, *args)


def after(x, *deps):
    return lax.optimization_barrier((x, deps))[0]


def on_device(
    tokens,
    timesteps,
    buckets,
    counts,
    w_time,
    table,
    w_qkv,
    b_qv,
    w_out,
    b_out,
    gain1,
    shift1,
    w_up,
    b_up,
    w_down,
    b_down,
    gain2,
    shift2,
    cotangent,
):
    mpn = lax.axis_size("mp")
    dpn = lax.axis_size("dp")
    extra = dpn.bit_length() - 4
    me = lax.axis_index("dp")
    z = lax.axis_index("mp")
    q8 = me >> extra
    width = w_time.shape[0]
    positions, slots = tokens.shape[:2]
    length = positions * mpn
    head_cols = w_qkv.shape[2]
    units = w_up.shape[1]

    def exchange(x, partner):
        low = (1 << extra) - 1
        pairs = [(i, (partner(i >> extra) << extra) | (i & low)) for i in range(dpn)]
        return lax.ppermute(x, "dp", pairs)

    def cores(x):
        return exchange(x, lambda p: p ^ 1)

    def first_link(x):
        return exchange(x, lambda p: p ^ masks(p)[0])

    def second_link(x):
        return exchange(x, lambda p: p ^ masks(p)[1])

    def shift(x, s):
        return lax.ppermute(x, "mp", [(i, (i + s) % mpn) for i in range(mpn)])

    def at_item(x, s):
        return lax.dynamic_index_in_dim(x, lax.rem(z + s, mpn), 1, False)

    def to_items(x):
        return [at_item(x, 0)] + [shift(at_item(x, s), s) for s in range(1, mpn)]

    def to_positions(x):
        blocks = x.reshape(mpn, positions, width)
        return [blocks[0]] + [shift(blocks[s], -s) for s in range(1, mpn)]

    def in_item_order(parts):
        turned = jnp.concatenate([p[:, None] for p in parts] * 2, axis=1)
        return lax.dynamic_slice_in_dim(turned, lax.rem(mpn - z, mpn), mpn, 1)

    def split(shard, axis):
        dims = shard.shape
        return shard.reshape(dims[:axis] + (8, dims[axis] // 8) + dims[axis + 1 :])

    def eighth(shaped, axis):
        return lax.dynamic_index_in_dim(shaped, q8, axis, False)

    def along_z(part):
        return [shift(part, s) for s in range(1, mpn)]

    place = q8.astype(jnp.int32)[None]
    own_qkv, own_out, own_up, own_down = split(w_qkv, 1), split(w_out, 0), split(w_up, 0), split(w_down, 0)
    b_out, gain1, shift1, b_down, gain2, shift2 = [
        v[None] for v in (b_out, gain1, shift1, b_down, gain2, shift2)
    ]

    own_bias = jnp.stack([b_qv[0], jnp.zeros_like(b_qv[0]), b_qv[1]])[:, None]
    z_qkv = along_z(jnp.concatenate([eighth(own_qkv, 1), in_three(own_bias)], axis=1))
    part_up = jnp.concatenate([eighth(own_out, 0), eighth(own_up, 0), in_three(b_up[None])])
    part_down = eighth(own_down, 0)
    mine_qkv, far_bias = pack(1, after(z_qkv, part_up, part_down), own_qkv.shape[2])
    came_qkv = first_link(mine_qkv)
    z_up = along_z(after(part_up, mine_qkv))

    timesteps, buckets, counts = after((timesteps, buckets, counts), mine_qkv)
    total_live = jnp.sum(counts).astype(f32)
    weighting = 1.0 / total_live
    live = (z < lax.dynamic_index_in_dim(counts, me, 0, True)).astype(f32)
    my_step = lax.dynamic_index_in_dim(timesteps, z, 0, True)
    my_bucket = lax.dynamic_index_in_dim(buckets, z, 0, False)
    time_embed = embed(
        40,
        sinusoid(my_step.astype(f32), width), w_time, lax.dynamic_index_in_dim(table, my_bucket, 0, True)
    )
    held_qkv = pack(1, [mine_qkv, after(came_qkv, time_embed)])
    far_qkv = second_link(held_qkv)
    mine_up, far_up_bias = pack(1, after(z_up, held_qkv), own_out.shape[1] + own_up.shape[1])
    came_up = first_link(mine_up)
    x = to_items(after(tokens, mine_up))
    held2_qkv, far2_qkv = cores(held_qkv), cores(after(far_qkv, mine_up))
    g_qkv = Gathered(own_qkv, [held_qkv, far_qkv, held2_qkv, far2_qkv], 1, 0)
    held_up = pack(1, [mine_up, after(came_up, held2_qkv, far2_qkv)])
    far_up = second_link(held_up)
    x = jnp.concatenate(after(x, held_up))
    hidden = (x.astype(f32) + time_embed).astype(bf16)
    z_down = along_z(after(part_down, hidden))

    done = attend(10, 0, mpn, Gathered(own_qkv, [], 1, 0), place, hidden, own_bias[None], [])
    done = attend(10, 1, mpn, g_qkv, place, hidden, far_bias, done)
    held2_up, far2_up = cores(held_up), cores(after(far_up, done))
    done = attend(10, 2, mpn, g_qkv, place, after(hidden, held2_up, far2_up), far_bias, done)
    mine_down = pack(1, after(z_down, done))
    came_down = first_link(mine_down)
    cot = to_items(after(cotangent, mine_down))
    qkv, probs, ctx = attend(20, 3, mpn, g_qkv, place, after(hidden, mine_down), far_bias, done)
    held_down = pack(1, [mine_down, after(came_down, ctx)])
    far_down = second_link(held_down)
    ctx2, hidden2 = cores(after(ctx, held_down)), cores(after(hidden, held_down))
    up_pieces = [held_up, far_up, held2_up, far2_up]
    g_out = Gathered(own_out, up_pieces, 0, 0)
    g_up = Gathered(own_up, up_pieces, 0, own_out.shape[1])
    n1, inv1, normed_low, active, slope, full_out, full_up = up_project(
        g_out,
        g_up,
        place,
        after(ctx, held_down, ctx2, hidden2),
        x,
        time_embed,
        b_out,
        gain1,
        shift1,
        jnp.concatenate([b_up[None, None], far_up_bias]),
    )
    full_out = full_out.reshape(mpn, head_cols, width)
    full_up = full_up.reshape(mpn, width, units)
    held2_down, far2_down = cores(held_down), cores(after(far_down, normed_low))
    g_down = Gathered(own_down, [held_down, far_down, held2_down, far2_down], 0, 0)
    cot = jnp.concatenate(after(cot, normed_low))
    active2, low2 = cores(active), cores(normed_low)
    output, grad_second, branch_grad, sums2, full_down = down_project(
        g_down, place, live, active, n1, cot, b_down, gain1, shift1, gain2, shift2
    )
    full_down = full_down.reshape(mpn, units, width)

    def pass_on(keep, came):
        return (keep[1].astype(f32) + came[1].astype(f32)).astype(bf16)

    def send_home(keep, came, last):
        part = keep[0].astype(f32) + came[0].astype(f32) + last.astype(f32)
        sent = [part[s].astype(bf16) for s in range(1, mpn)]
        return [part[0]] + [shift(v, -s - 1) for s, v in enumerate(sent)], sent

    def finish(arrived):
        total = sum(a.astype(f32) for a in arrived)
        for t in reversed(range(extra)):
            half = total.shape[0] // 2
            bit = (me >> t) & 1
            keep = lax.dynamic_slice_in_dim(total, bit * half, half, 0)
            sent = lax.dynamic_slice_in_dim(total, (1 - bit) * half, half, 0)
            total = keep + lax.ppermute(sent, "dp", [(i, i ^ (1 << t)) for i in range(dpn)])
        return total * weighting

    devices = dpn * mpn
    both = ("dp", "mp")

    def in_order(parts):
        turned = jnp.stack([parts[-i % mpn] for i in range(mpn)] * 2)
        return lax.dynamic_slice_in_dim(turned, (mpn - z) % mpn, mpn, 0).reshape(-1)

    keep_d, send_d = weight_grad(20, place, [(branch_grad, cores(branch_grad), active, active2)])
    came_d = first_link(send_d)
    out_items = to_positions(after(output, keep_d))
    up_grad, bias_up, grad_first, mixing_grad, sums1 = up_back(
        full_down, full_up, after(branch_grad, keep_d, low2), slope, grad_second, n1, inv1, gain1
    )
    up_grad2, mixing_grad2 = cores(up_grad), cores(mixing_grad)
    pass_d = pass_on(keep_d, after(came_d, mixing_grad))
    last_d = second_link(pass_d)
    output = in_item_order(after(out_items, pass_d))
    pg, bias_near = attend_back(
        80, 0, mpn // 2, full_out, after(mixing_grad, pass_d, output), qkv, probs, None
    )
    keep_u, send_u = weight_grad(
        30, place, after([(normed_low, low2, up_grad, up_grad2), (mixing_grad, mixing_grad2, ctx, ctx2)], pg)
    )
    came_u = first_link(send_u)
    home_d, sent_d = send_home(keep_d, came_d, after(last_d, keep_u))
    pg, bias_far = attend_back(
        30, mpn // 2, mpn - mpn // 2, full_out, after(mixing_grad, sent_d), qkv, probs, pg
    )
    pg2 = cores(pg)
    grad_tokens, time_grad = input_back(g_qkv, place, pg, grad_first)
    grad_w_down = finish(after(home_d, grad_tokens)).T
    pass_u = pass_on(keep_u, after(came_u, grad_w_down))
    last_u = second_link(pass_u)
    back_items = to_positions(grad_tokens)
    bias_proj = jnp.concatenate([bias_near, bias_far])
    vectors = [
        in_order(bias_proj[:, 0, :head_cols]),
        in_order(bias_proj[:, 0, 2 * head_cols :]),
        sums1[0],
        sums1[1],
        sums1[2],
        sums2[0],
        sums2[1],
        sums2[2],
        in_order(bias_up[:, 0]),
        time_grad,
    ]
    facts = jnp.stack([my_step[0].astype(f32), my_bucket.astype(f32)])
    facts = jnp.broadcast_to(facts[None], (devices, 2))
    vectors = jnp.concatenate([facts] + [v.reshape(devices, -1) for v in vectors], axis=1)
    keep_q, send_q = weight_grad(20, place, after([(hidden, hidden2, pg, pg2)], pass_u))
    came_q = first_link(send_q)
    home_u, sent_u = send_home(keep_u, came_u, after(last_u, keep_q))
    gathered = lax.all_to_all(after(vectors, sent_u), both, 0, 0, tiled=True)
    per = width // devices
    grad_tokens = in_item_order(after(back_items, sent_u)).astype(f32)
    pass_q = pass_on(keep_q, after(came_q, grad_tokens))
    last_q = second_link(pass_q)
    up_and_out = finish(after(home_u, pass_q))
    grad_w_up = up_and_out[:, :units]
    grad_w_out = up_and_out[:, units:].T
    home_q, sent_q = send_home(keep_q, came_q, after(last_q, up_and_out))
    grad_w_qkv = finish(home_q).reshape(-1, 3, head_cols)
    grad_w_qkv = jnp.moveaxis(grad_w_qkv, 1, 0)

    gathered = after(gathered, pass_q)
    grads = gathered[:, -per:]
    summed = jnp.sum(gathered[:, 2:-per], axis=0) * weighting
    steps, rows_of = gathered[:, 0], gathered[:, 1]
    small = [summed[i * per : (i + 1) * per] for i in range(8)]
    grad_b_up = summed[8 * per :]
    high = lax.Precision.HIGHEST
    grad_w_time = (
        jnp.einsum("nd,ne->de", sinusoid(steps, width).astype(f32), grads, precision=high)
        * weighting
    )
    onehot = (rows_of[:, None] == jnp.arange(table.shape[0], dtype=f32)[None, :]).astype(f32)
    grad_table = jnp.einsum("nb,nd->bd", onehot, grads, precision=high) * weighting
    return (
        output,
        grad_tokens,
        grad_w_time,
        grad_table,
        grad_w_qkv,
        jnp.stack(small[:2]),
        grad_w_out,
        small[2],
        small[3],
        small[4],
        grad_w_up,
        grad_b_up,
        grad_w_down,
        small[5],
        small[6],
        small[7],
    )


def solution(mesh):
    return jax.shard_map(
        on_device,
        mesh=mesh,
        in_specs=(
            P("mp", "dp", None),
            P("dp"),
            P("dp"),
            P(),
            P(),
            P(),
            P(None, None, "mp"),
            P(None, "mp"),
            P("mp", None),
            P(),
            P(),
            P(),
            P(None, "mp"),
            P("mp"),
            P("mp", None),
            P(),
            P(),
            P(),
            P("mp", "dp", None),
        ),
        out_specs=(
            P("mp", "dp", None),
            P("mp", "dp", None),
            P(None, ("dp", "mp")),
            P(None, ("dp", "mp")),
            P(None, "dp", "mp"),
            P(None, ("dp", "mp")),
            P("mp", "dp"),
            P(("dp", "mp")),
            P(("dp", "mp")),
            P(("dp", "mp")),
            P("dp", "mp"),
            P(("dp", "mp")),
            P("mp", "dp"),
            P(("dp", "mp")),
            P(("dp", "mp")),
            P(("dp", "mp")),
        ),
        check_vma=False,
    )
```

time: 532 us -> 466 us (0.88)
  waiting for transfers between devices: 181 us -> 114 us
  Pallas kernels: 145 us -> 161 us
  other arithmetic: 35.3 us -> 22.8 us
  local copies, waits for them, and re-layouts: 53.4 us -> 47.4 us
    ppermute x44 -> x26, waiting for transfers between devices: 69.3 us -> 33.6 us  [exchange(): return lax.ppermute(x, 'dp', pairs)]
    ppermute x21 -> x30, starting transfers between devices: 48.1 us -> 82.3 us  [shift(): return lax.ppermute(x, 'mp', [(i, (i + s) % mpn) for i in range(mpn)])]
    all_to_all x6 -> x1, waiting for transfers between devices: 32.2 us -> 2.71 us  [on_device(): gathered = lax.all_to_all(after(vectors, sent_u), both, 0, 0, tiled=True)]
    all_to_all x6 -> x1, starting transfers between devices: 23 us -> 6.34 us  [on_device(): gathered = lax.all_to_all(after(vectors, sent_u), both, 0, 0, tiled=True)]
    pallas_call x10 -> x18, Pallas kernels: 112 us -> 126 us  [the longest x4 29.6 us: attend(): pl.pallas_call(functools.partial(attend_body, shard, gathered), grid=(pai...]
    ppermute x44 -> x26, starting transfers between devices: 29.5 us -> 16.5 us  [exchange(): return lax.ppermute(x, 'dp', pairs)]
    pallas_call x6 -> x1, local copies, waits for them, and re-layouts: 10.9 us -> 0.51 us  [input_back(): pl.pallas_call(functools.partial(input_back_body, shards, gathered), grid...]
    unnamed x88 -> x123, local copies, waits for them, and re-layouts: 16.8 us -> 25.5 us
  transfers between devices with their start and end apart: 71 -> 57, of which waited for: 24 -> 22; matrix products, arithmetic and copies ran while one was open for 15% -> 12% of each run, Pallas kernels for 15% -> 33%
where the time goes in v3:
time: 466 us; the launch traced here: 459 us
  Pallas kernels  161 us (35%)
  waiting for transfers between devices  114 us (24%)
  starting transfers between devices  105 us (23%)
  local copies, waits for them, and re-layouts  47.4 us (10%)
  other arithmetic  22.8 us (5%)
  between operations  6.49 us (1%)
    ppermute x30, starting transfers between devices, shift(): return lax.ppermute(x, 'mp', [(i, (i + s) % mpn) for i in range(mpn)])  82.3 us
    ppermute x30, waiting for transfers between devices, shift(): return lax.ppermute(x, 'mp', [(i, (i + s) % mpn) for i in range(mpn)])  77.4 us
    ppermute x26, waiting for transfers between devices, exchange(): return lax.ppermute(x, 'dp', pairs)  33.6 us
    pallas_call x4, Pallas kernels, attend(): pl.pallas_call(functools.partial(attend_body, shard, gathered), grid=(pai...  29.6 us
    pallas_call x3, Pallas kernels, weight_grad(): pl.pallas_call(functools.partial(weight_grad_body, len(groups)), grid=(sh...  29.4 us
    unnamed x123, local copies, waits for them, and re-layouts  25.5 us
    pallas_call x2, Pallas kernels, attend_back(): pl.pallas_call(attend_back_body, grid=(count, pairs), out_shape=[jax.Shap...  23 us
    pallas_call x1, Pallas kernels, up_project(): pl.pallas_call(functools.partial(up_body, shards, g_out, g_up), grid=(sha...  19.7 us
  transfers between devices with their start and end apart: 57, of which 22 were waited for; matrix products, arithmetic and copies ran while one was open for 12% of the time, Pallas kernels for 33%

profile of v3, /device:TPU:0, one launch (start us, length us, event | category | flops | bytes accessed | tf_op | source)
XLA Modules:
  0.0 458.7 jit_solution(15404879846353985564)
XLA Ops:
  2.7 3.1 collective-permute-start
  5.8 2.6 collective-permute-start.1
  14.0 8.1 %collective-permute-done.1.refs_1_ = bf16[3,136,256]{2,1,0:T(8,128)(2,1)S(1)} collective-permute-done((bf16[3,136,256]{2,1,0:T(8,128)(2,1)S(1)}, bf16[3,136,256]{2,1,0:T(8,128)(2,1)S(1)}, u32[]{:S(2)}, u32[]{:S(2)}) %collective-permute-start.1) | collective-permute-done | bytes 208928 | tf_op jit(solution)/shard_map/ppermute | solution.py:764
  22.8 2.0 pack.6
  31.5 2.6 embed.1.te_ref
  34.1 2.3 collective-permute-done.6.refs_1_
  37.2 2.4 pack.7.refs_1_
  41.1 4.9 %collective-permute-start.3 = (bf16[168,1024]{1,0:T(8,128)(2,1)S(1)}, bf16[168,1024]{1,0:T(8,128)(2,1)S(1)}, u32[]{:S(2)}, u32[]{:S(2)}) collective-permute-start(bf16[168,1024]{1,0:T(8,128)(2,1)S(1)} %concatenate.77), channel_id=1, source_target_pairs={{0,1},{1,2},{2,3},{3,0},{4,5},{5,6},{6,7},{7,4},{8,9},{9,10},{10,1... | collective-permute-start | bytes 1032200 | tf_op jit(solution)/shard_map/ppermute | solution.py:764
  46.0 1.7 collective-permute-start.4
  48.3 7.9 %collective-permute-done.3.refs_0_ = bf16[168,1024]{1,0:T(8,128)(2,1)S(1)} collective-permute-done((bf16[168,1024]{1,0:T(8,128)(2,1)S(1)}, bf16[168,1024]{1,0:T(8,128)(2,1)S(1)}, u32[]{:S(2)}, u32[]{:S(2)}) %collective-permute-start.3) | collective-permute-done | bytes 344096 | tf_op jit(solution)/shard_map/ppermute | solution.py:764
  56.2 11.8 %collective-permute-done.4.refs_1_ = bf16[168,1024]{1,0:T(8,128)(2,1)S(1)} collective-permute-done((bf16[168,1024]{1,0:T(8,128)(2,1)S(1)}, bf16[168,1024]{1,0:T(8,128)(2,1)S(1)}, u32[]{:S(2)}, u32[]{:S(2)}) %collective-permute-start.4) | collective-permute-done | bytes 344096 | tf_op jit(solution)/shard_map/ppermute | solution.py:764
  69.5 2.2 pack.8
  73.3 7.3 %collective-permute-start.7 = (bf16[128,1024]{1,0:T(8,128)(2,1)S(1)}, bf16[128,1024]{1,0:T(8,128)(2,1)S(1)}, u32[]{:S(2)}, u32[]{:S(2)}) collective-permute-start(bf16[128,1024]{1,0:T(8,128)(2,1)S(1)} %get-tuple-element.356), channel_id=1, source_target_pairs={{0,1},{1,2},{2,3},{3,0},{4,5},{5,6},{6,7},{7,4},{8,9},{9,10},{10,1... | collective-permute-start | bytes 786440 | tf_op jit(solution)/shard_map/ppermute | solution.py:764
  80.6 2.7 collective-permute-start.8
  83.3 2.8 collective-permute-done.10.refs_1_
  86.1 9.5 %collective-permute-start.9 = (bf16[128,1024]{1,0:T(8,128)(2,1)S(1)}, bf16[128,1024]{1,0:T(8,128)(2,1)S(1)}, u32[]{:S(2)}, u32[]{:S(2)}) collective-permute-start(bf16[128,1024]{1,0:T(8,128)(2,1)S(1)} %get-tuple-element.354), channel_id=1, source_target_pairs={{0,3},{1,0},{2,1},{3,2},{4,7},{5,4},{6,5},{7,6},{8,11},{9,8},{10,9... | collective-permute-start | bytes 786440 | tf_op jit(solution)/shard_map/ppermute | solution.py:764
  96.3 2.9 pack.9.refs_1_
  100.7 3.6 collective-permute-done.9
  105.8 7.2 %attend.4 = (bf16[4,512,768]{2,1,0:T(8,128)(2,1)}, bf16[4,4,512,512]{3,2,1,0:T(8,128)(2,1)}, bf16[4,512,256]{2,1,0:T(8,128)(2,1)}) custom-call(s32[1]{0:T(128)} %bitcast.place_ref, bf16[512,1024]{1,0:T(8,128)(2,1)} %add_convert_fusion.2.x_ref.refs_0_, f32[1,3,1,256]{3,2,1,0:T(1,128)} %broadcast_in_dim_broadcast_in_dim.3.bias_ref, ...), custom_call_target="tpu_custom_call" | custom-call | flops 11500000256 | tf_op jit(solution)/shard_map/attend/pallas_call | solution.py:202
  113.0 7.3 %attend.5 = (bf16[4,512,768]{2,1,0:T(8,128)(2,1)}, bf16[4,4,512,512]{3,2,1,0:T(8,128)(2,1)}, bf16[4,512,256]{2,1,0:T(8,128)(2,1)}) custom-call(s32[1]{0:T(128)} %bitcast.place_ref, bf16[512,1024]{1,0:T(8,128)(2,1)} %add_convert_fusion.2.x_ref.refs_0_, ...), custom_call_target="tpu_custom_call", output_to_operand_aliasing={{0}: (8, {}), {1}: (9, {}), {2}: (10, {})} | custom-call | flops 11500000256 | tf_op jit(solution)/shard_map/attend/pallas_call | solution.py:202
  120.2 3.8 collective-permute-done.18.refs_2_
  124.6 3.4 collective-permute-start.16
  128.1 7.9 %attend.6 = (bf16[4,512,768]{2,1,0:T(8,128)(2,1)}, bf16[4,4,512,512]{3,2,1,0:T(8,128)(2,1)}, bf16[4,512,256]{2,1,0:T(8,128)(2,1)}) custom-call(s32[1]{0:T(128)} %bitcast.place_ref, bf16[512,1024]{1,0:T(8,128)(2,1)} %add_convert_fusion.2.x_ref.refs_0_, ...), custom_call_target="tpu_custom_call", output_to_operand_aliasing={{0}: (8, {}), {1}: (9, {}), {2}: (10, {})} | custom-call | flops 11500000256 | tf_op jit(solution)/shard_map/attend/pallas_call | solution.py:202
  136.0 9.4 %collective-permute-done.15.refs_1_ = bf16[128,1024]{1,0:T(8,128)(2,1)S(1)} collective-permute-done((bf16[128,1024]{1,0:T(8,128)(2,1)S(1)}, bf16[128,1024]{1,0:T(8,128)(2,1)S(1)}, u32[]{:S(2)}, u32[]{:S(2)}) %collective-permute-start.15) | collective-permute-done | bytes 262176 | tf_op jit(solution)/shard_map/ppermute | solution.py:764
  146.2 2.0 pack.10.refs_0_
  148.8 7.3 %attend.7 = (bf16[4,512,768]{2,1,0:T(8,128)(2,1)}, bf16[4,4,512,512]{3,2,1,0:T(8,128)(2,1)}, bf16[4,512,256]{2,1,0:T(8,128)(2,1)}) custom-call(s32[1]{0:T(128)} %bitcast.place_ref, bf16[512,1024]{1,0:T(8,128)(2,1)} %add_convert_fusion.2.x_ref.refs_0_, ...), custom_call_target="tpu_custom_call", output_to_operand_aliasing={{0}: (8, {}), {1}: (9, {}), {2}: (10, {})} | custom-call | flops 23000000512 | tf_op jit(solution)/shard_map/attend/pallas_call | solution.py:202
  156.0 4.4 collective-permute-done.20.refs_1_
  161.3 2.8 pack.11.refs_1_
  168.3 19.7 %up_project.1 = (f32[512,1024]{1,0:T(8,128)}, f32[512,128]{1,0:T(8,128)}, bf16[512,1024]{1,0:T(8,128)(2,1)}, bf16[4,512,1024]{2,1,0:T(8,128)(2,1)}, bf16[4,512,1...) custom-call(s32[1]{0:T(128)} %bitcast.place_ref, ...), custom_call_target="tpu_custom_call" | custom-call | flops 46000001024 | tf_op jit(solution)/shard_map/up_project/pallas_call | solution.py:303
  189.1 5.6 %collective-permute-start.23 = (bf16[128,1024]{1,0:T(8,128)(2,1)S(1)}, bf16[128,1024]{1,0:T(8,128)(2,1)S(1)}, u32[]{:S(2)}, u32[]{:S(2)}) collective-permute-start(bf16[128,1024]{1,0:T(8,128)(2,1)S(1)} %get-tuple-element.352), channel_id=1, source_target_pairs={{0,1},{1,2},{2,3},{3,0},{4,5},{5,6},{6,7},{7,4},{8,9},{9,10},{10,1... | collective-permute-start | bytes 786440 | tf_op jit(solution)/shard_map/ppermute | solution.py:764
  194.7 2.4 collective-permute-start.25
  198.3 3.1 collective-permute-done.23
  201.4 9.8 %collective-permute-done.24 = bf16[128,1024]{1,0:T(8,128)(2,1)S(1)} collective-permute-done((bf16[128,1024]{1,0:T(8,128)(2,1)S(1)}, bf16[128,1024]{1,0:T(8,128)(2,1)S(1)}, u32[]{:S(2)}, u32[]{:S(2)}) %collective-permute-start.24) | collective-permute-done | bytes 262176 | tf_op jit(solution)/shard_map/ppermute | solution.py:764
  213.0 15.7 %down_project.1 = (bf16[512,1024]{1,0:T(8,128)(2,1)}, f32[512,1024]{1,0:T(8,128)}, bf16[512,1024]{1,0:T(8,128)(2,1)}, f32[3,1024]{1,0:T(4,128)}, bf16[4,8,128,1024]{3,2,1,0:T(8,128)(2,1)}) custom-call(s32[1]{0:T(128)} %bitcast.place_ref, f32[1]{0:T(128)S(6)} %convert_element_type.172.live_ref, bf16[4,512,1024]{2,1,0:T(8,128)(2,1)} %get-tuple-element.179.act_ref.refs_2_, ...), custom_call_target="tpu_custom_call" | custom-call | flops 46000001024 | tf_op jit(solution)/shard_map/down_project/pallas_call | solution.py:410
  233.5 9.4 %weight_grad.3 = (bf16[2,4,128,1024]{3,2,1,0:T(8,128)(2,1)}, bf16[2,4,128,1024]{3,2,1,0:T(8,128)(2,1)}) custom-call(s32[1]{0:T(128)} %bitcast.place_ref, bf16[512,1024]{1,0:T(8,128)(2,1)} %get-tuple-element.193.refs_0_.bg_ref, bf16[512,1024]{1,0:T(8,128)(2,1)} %copy-done.33, bf16[4,512,1024]{2,1,0:T(8,128)(2,1)} %get-tuple-element.179.act_ref.refs_2_, ...), custom_call_target="tpu_custom_call" | custom-call | flops 23000000512 | tf_op jit(solution)/shard_map/weight_grad/pallas_call | solution.py:699
  243.6 8.7 %collective-permute-start.31 = (bf16[128,1024]{1,0:T(8,128)(2,1)S(1)}, bf16[128,1024]{1,0:T(8,128)(2,1)S(1)}, u32[]{:S(2)}, u32[]{:S(2)}) collective-permute-start(bf16[128,1024]{1,0:T(8,128)(2,1)S(1)} %get-tuple-element.348), channel_id=1, source_target_pairs={{0,3},{1,0},{2,1},{3,2},{4,7},{5,4},{6,5},{7,6},{8,11},{9,8},{10,9... | collective-permute-start | bytes 786440 | tf_op jit(solution)/shard_map/ppermute | solution.py:764
  253.1 18.5 %up_back.1 = (bf16[4,512,1024]{2,1,0:T(8,128)(2,1)}, f32[4,1,1024]{2,1,0:T(1,128)}, f32[512,1024]{1,0:T(8,128)}, bf16[512,1024]{1,0:T(8,128)(2,1)}, f32[3,1024]{1,0:T(4,128)}) custom-call(bf16[512,1024]{1,0:T(8,128)(2,1)} %get-tuple-element.193.refs_0_.bg_ref, bf16[4,512,1024]{2,1,0:T(8,128)(2,1)} %get-tuple-element.194.slope_ref, ...), custom_call_target="tpu_custom_call" | custom-call | flops 46000001024 | tf_op jit(solution)/shard_map/up_back/pallas_call | solution.py:494
  276.0 11.5 %attend_back.2 = (bf16[4,512,768]{2,1,0:T(8,128)(2,1)}, f32[2,1,768]{2,1,0:T(1,128)}) custom-call(bf16[512,1024]{1,0:T(8,128)(2,1)} %get-tuple-element.221.mg_ref.refs_4_, bf16[4,256,1024]{2,1,0:T(8,128)(2,1)} %bitcast.191, bf16[4,512,768]{2,1,0:T(8,128)(2,1)} %get-tuple-element.208.qkv, bf16[4,4,512,512]{3,2,1,0:T(8,128)(2,1)} %get-tuple-element.209.p_of), custom_call_target="tpu_custom_call" | custom-call | flops 92000002048 | tf_op jit(solution)/shard_map/attend_back/pallas_call | solution.py:572
  288.5 11.9 %weight_grad.4 = (bf16[2,4,128,1280]{3,2,1,0:T(8,128)(2,1)}, bf16[2,4,128,1280]{3,2,1,0:T(8,128)(2,1)}) custom-call(s32[1]{0:T(128)} %bitcast.place_ref, bf16[512,1024]{1,0:T(8,128)(2,1)} %get-tuple-element.211.refs_0_, bf16[512,1024]{1,0:T(8,128)(2,1)} %copy-done.32, bf16[4,512,1024]{2,1,0:T(8,128)(2,1)} %get-tuple-element.213.refs_2_, ...), custom_call_target="tpu_custom_call" | custom-call | flops 34500001792 | tf_op jit(solution)/shard_map/weight_grad/pallas_call | solution.py:699
  300.4 1.9 fusion.22
  304.2 11.5 %attend_back.3 = (bf16[4,512,768]{2,1,0:T(8,128)(2,1)}, f32[2,1,768]{2,1,0:T(1,128)}) custom-call(bf16[512,1024]{1,0:T(8,128)(2,1)} %get-tuple-element.221.mg_ref.refs_4_, bf16[4,256,1024]{2,1,0:T(8,128)(2,1)} %bitcast.192, bf16[4,512,768]{2,1,0:T(8,128)(2,1)} %get-tuple-element.208.qkv, ...), custom_call_target="tpu_custom_call", output_to_operand_aliasing={{0}: (4, {})} | custom-call | flops 34500001792 | tf_op jit(solution)/shard_map/attend_back/pallas_call | solution.py:572
  317.7 1.8 copy.95
  319.5 4.7 %collective-permute-start.43 = (bf16[128,1024]{1,0:T(8,128)(2,1)}, bf16[128,1024]{1,0:T(8,128)(2,1)}, u32[]{:S(2)}, u32[]{:S(2)}) collective-permute-start(bf16[128,1024]{1,0:T(8,128)(2,1)} %get-tuple-element.345), channel_id=1, source_target_pairs={{0,3},{1,0},{2,1},{3,2},{4,7},{5,4},{6,5},{7,6},{8,11},{9,8},{10,9... | collective-permute-start | bytes 786440 | tf_op jit(solution)/shard_map/ppermute | solution.py:764
  326.1 8.6 %input_back.1 = (bf16[512,1024]{1,0:T(8,128)(2,1)}, f32[1,1024]{1,0:T(1,128)}) custom-call(s32[1]{0:T(128)} %bitcast.place_ref, bf16[4,512,768]{2,1,0:T(8,128)(2,1)} %get-tuple-element.233.pg_ref.refs_2_, f32[512,1024]{1,0:T(8,128)} %get-tuple-element.223.gf_hbm, bf16[3,8,128,256]{3,2,1,0:T(8,128)(2,1)} %bitcast.175, ...), custom_call_target="tpu_custom_call" | custom-call | flops 5750000128 | tf_op jit(solution)/shard_map/input_back/pallas_call | solution.py:635
  337.1 2.2 fusion.23
  339.3 3.0 collective-permute-start.39
  342.4 5.7 %collective-permute-done.44 = bf16[128,1024]{1,0:T(8,128)(2,1)} collective-permute-done((bf16[128,1024]{1,0:T(8,128)(2,1)}, bf16[128,1024]{1,0:T(8,128)(2,1)}, u32[]{:S(2)}, u32[]{:S(2)}) %collective-permute-start.44) | collective-permute-done | bytes 262176 | tf_op jit(solution)/shard_map/ppermute | solution.py:764
  348.1 12.0 %collective-permute-start.41 = (bf16[128,1024]{1,0:T(8,128)(2,1)}, bf16[128,1024]{1,0:T(8,128)(2,1)}, u32[]{:S(2)}, u32[]{:S(2)}) collective-permute-start(bf16[128,1024]{1,0:T(8,128)(2,1)} %get-tuple-element.339), channel_id=1, source_target_pairs={{0,1},{1,2},{2,3},{3,0},{4,5},{5,6},{6,7},{7,4},{8,9},{9,10},{10,1... | collective-permute-start | bytes 786440 | tf_op jit(solution)/shard_map/ppermute | solution.py:764
  360.1 2.0 multiply_bitcast_fusion
  362.1 2.0 copy.99
  366.8 8.1 %weight_grad.5 = (bf16[2,4,128,768]{3,2,1,0:T(8,128)(2,1)}, bf16[2,4,128,768]{3,2,1,0:T(8,128)(2,1)}) custom-call(s32[1]{0:T(128)} %bitcast.place_ref, bf16[512,1024]{1,0:T(8,128)(2,1)} %add_convert_fusion.2.x_ref.refs_0_, bf16[512,1024]{1,0:T(8,128)(2,1)} %copy-done.29, bf16[4,512,768]{2,1,0:T(8,128)(2,1)} %get-tuple-element.233.pg_ref.refs_2_, ...), custom_call_target="tpu_custom_call" | custom-call | flops 23000000512 | tf_op jit(solution)/shard_map/weight_grad/pallas_call | solution.py:699
  376.0 14.2 %collective-permute-done.46 = bf16[4,128,1280]{2,1,0:T(8,128)(2,1)} collective-permute-done((bf16[4,128,1280]{2,1,0:T(8,128)(2,1)S(1)}, bf16[4,128,1280]{2,1,0:T(8,128)(2,1)}, u32[]{:S(2)}, u32[]{:S(2)}) %collective-permute-start.46) | collective-permute-done | bytes 1310752 | tf_op jit(solution)/shard_map/ppermute | solution.py:752
  390.2 2.2 fusion.21
  393.3 3.9 collective-permute-start.51
  398.7 6.3 %all-to-all-start = ((f32[32,1,418]{2,1,0:T(1,128)}), f32[32,1,418]{2,1,0:T(1,128)S(1)}, u32[]{:S(2)}, u32[]{:S(2)}) async-start(f32[32,1,418]{2,1,0:T(1,128)} %copy.93), calls=%async_computation | async-start | bytes 131072 | tf_op jit(solution)/shard_map/all_to_all | solution.py:935
  405.1 1.7 bitcast_dynamic-update-slice_fusion.4
  406.7 1.7 bitcast_dynamic-update-slice_fusion.2
  412.5 1.7 bitcast_dynamic-update-slice_fusion.3
  417.3 2.7 copy.96
  420.0 2.7 all-to-all-done
  422.7 2.2 fusion.2
  432.6 4.6 collective-permute-done.49
  441.7 4.0 collective-permute-done.53
  445.7 11.3 %collective-permute-done.54 = bf16[128,768]{1,0:T(8,128)(2,1)S(1)} collective-permute-done((bf16[128,768]{1,0:T(8,128)(2,1)S(1)}, bf16[128,768]{1,0:T(8,128)(2,1)S(1)}, u32[]{:S(2)}, u32[]{:S(2)}) %collective-permute-start.54) | collective-permute-done | bytes 196640 | tf_op jit(solution)/shard_map/ppermute | solution.py:764
  (287 shorter events, 77.4 us)
Async XLA Ops:
  0.6 29.6 %copy-start = (f32[32,1024]{1,0:T(8,128)S(1)}, f32[32,1024]{1,0:T(8,128)}, u32[]{:S(2)}) copy-start(f32[32,1024]{1,0:T(8,128)} %param.24) | copy-start | bytes 393220
  2.7 11.2 %collective-permute-start = (bf16[3,136,256]{2,1,0:T(8,128)(2,1)S(1)}, bf16[3,136,256]{2,1,0:T(8,128)(2,1)S(1)}, u32[]{:S(2)}, u32[]{:S(2)}) collective-permute-start(bf16[3,136,256]{2,1,0:T(8,128)(2,1)S(1)} %concatenate.75), channel_id=1, source_target_pairs={{0,1},{1,2},{2,3},{3,0},{4,5},{5,6},{6,7},{7,4},{8,9},{9,10},{10,1... | collective-permute-start | bytes 626696 | tf_op jit(solution)/shard_map/ppermute | solution.py:764
  5.8 16.3 %collective-permute-start.1 = (bf16[3,136,256]{2,1,0:T(8,128)(2,1)S(1)}, bf16[3,136,256]{2,1,0:T(8,128)(2,1)S(1)}, u32[]{:S(2)}, u32[]{:S(2)}) collective-permute-start(bf16[3,136,256]{2,1,0:T(8,128)(2,1)S(1)} %concatenate.75), channel_id=1, source_target_pairs={{0,2},{1,3},{2,0},{3,1},{4,6},{5,7},{6,4},{7,5},{8,10},{9,11},{10,... | collective-permute-start | bytes 626696 | tf_op jit(solution)/shard_map/ppermute | solution.py:764
  8.4 13.7 %collective-permute-start.2 = (bf16[3,136,256]{2,1,0:T(8,128)(2,1)S(1)}, bf16[3,136,256]{2,1,0:T(8,128)(2,1)S(1)}, u32[]{:S(2)}, u32[]{:S(2)}) collective-permute-start(bf16[3,136,256]{2,1,0:T(8,128)(2,1)S(1)} %concatenate.75), channel_id=1, source_target_pairs={{0,3},{1,0},{2,1},{3,2},{4,7},{5,4},{6,5},{7,6},{8,11},{9,8},{10,9... | collective-permute-start | bytes 626696 | tf_op jit(solution)/shard_map/ppermute | solution.py:764
  26.2 10.2 %collective-permute-start.6 = (bf16[3,3,128,256]{3,2,1,0:T(8,128)(2,1)}, bf16[3,3,128,256]{3,2,1,0:T(8,128)(2,1)S(1)}, u32[]{:S(2)}, u32[]{:S(2)}) collective-permute-start(bf16[3,3,128,256]{3,2,1,0:T(8,128)(2,1)} %get-tuple-element.139.refs_0_), channel_id=1, source_target_pairs={{0,8},{4,20},{8,0},{12,28},{16,24},{20,4},{24,16},{28,12},{1,9},{5... | collective-permute-start | bytes 1769480 | tf_op jit(solution)/shard_map/ppermute | solution.py:752
  39.6 32.6 %copy-start.28 = (bf16[2,3,3,128,256]{4,3,2,1,0:T(8,128)(2,1)S(1)}, bf16[2,3,3,128,256]{4,3,2,1,0:T(8,128)(2,1)}, u32[]{:S(2)}) copy-start(bf16[2,3,3,128,256]{4,3,2,1,0:T(8,128)(2,1)} %pack.7.refs_1_) | copy-start | bytes 3538948
  39.6 33.3 %copy-start.9 = (bf16[128,4,1024]{2,1,0:T(4,128)(2,1)S(1)}, bf16[128,4,1024]{2,1,0:T(4,128)(2,1)}, u32[]{:S(2)}) copy-start(bf16[128,4,1024]{2,1,0:T(4,128)(2,1)} %param.19) | copy-start | bytes 3145732
  39.6 33.2 %collective-permute-start.12 = (bf16[2,3,3,128,256]{4,3,2,1,0:T(8,128)(2,1)}, bf16[2,3,3,128,256]{4,3,2,1,0:T(8,128)(2,1)}, u32[]{:S(2)}, u32[]{:S(2)}) collective-permute-start(bf16[2,3,3,128,256]{4,3,2,1,0:T(8,128)(2,1)} %pack.7.refs_1_), channel_id=1, source_target_pairs={{0,16},{4,12},{8,24},{12,4},{16,0},{20,28},{24,8},{28,20},{1,17},{... | collective-permute-start | bytes 3538952 | tf_op jit(solution)/shard_map/ppermute | solution.py:752
  41.1 15.1 %collective-permute-start.3 = (bf16[168,1024]{1,0:T(8,128)(2,1)S(1)}, bf16[168,1024]{1,0:T(8,128)(2,1)S(1)}, u32[]{:S(2)}, u32[]{:S(2)}) collective-permute-start(bf16[168,1024]{1,0:T(8,128)(2,1)S(1)} %concatenate.77), channel_id=1, source_target_pairs={{0,1},{1,2},{2,3},{3,0},{4,5},{5,6},{6,7},{7,4},{8,9},{9,10},{10,1... | collective-permute-start | bytes 1032200 | tf_op jit(solution)/shard_map/ppermute | solution.py:764
  46.0 22.0 %collective-permute-start.4 = (bf16[168,1024]{1,0:T(8,128)(2,1)S(1)}, bf16[168,1024]{1,0:T(8,128)(2,1)S(1)}, u32[]{:S(2)}, u32[]{:S(2)}) collective-permute-start(bf16[168,1024]{1,0:T(8,128)(2,1)S(1)} %concatenate.77), channel_id=1, source_target_pairs={{0,2},{1,3},{2,0},{3,1},{4,6},{5,7},{6,4},{7,5},{8,10},{9,11},{10,... | collective-permute-start | bytes 1032200 | tf_op jit(solution)/shard_map/ppermute | solution.py:764
  47.6 20.3 %collective-permute-start.5 = (bf16[168,1024]{1,0:T(8,128)(2,1)S(1)}, bf16[168,1024]{1,0:T(8,128)(2,1)S(1)}, u32[]{:S(2)}, u32[]{:S(2)}) collective-permute-start(bf16[168,1024]{1,0:T(8,128)(2,1)S(1)} %concatenate.77), channel_id=1, source_target_pairs={{0,3},{1,0},{2,1},{3,2},{4,7},{5,4},{6,5},{7,6},{8,11},{9,8},{10,9... | collective-permute-start | bytes 1032200 | tf_op jit(solution)/shard_map/ppermute | solution.py:764
  71.7 14.4 %collective-permute-start.10 = (bf16[3,160,1024]{2,1,0:T(8,128)(2,1)}, bf16[3,160,1024]{2,1,0:T(8,128)(2,1)}, u32[]{:S(2)}, u32[]{:S(2)}) collective-permute-start(bf16[3,160,1024]{2,1,0:T(8,128)(2,1)} %get-tuple-element.148.refs_0_), channel_id=1, source_target_pairs={{0,8},{4,20},{8,0},{12,28},{16,24},{20,4},{24,16},{28,12},{1,9},{5... | collective-permute-start | bytes 2949128 | tf_op jit(solution)/shard_map/ppermute | solution.py:752
  72.2 24.1 %collective-permute-start.11 = (bf16[2,3,3,128,256]{4,3,2,1,0:T(8,128)(2,1)S(1)}, bf16[2,3,3,128,256]{4,3,2,1,0:T(8,128)(2,1)}, u32[]{:S(2)}, u32[]{:S(2)}) collective-permute-start(bf16[2,3,3,128,256]{4,3,2,1,0:T(8,128)(2,1)S(1)} %copy-done.28), channel_id=1, source_target_pairs={{0,4},{4,0},{8,12},{12,8},{16,20},{20,16},{24,28},{28,24},{1,5},{5... | collective-permute-start | bytes 3538952 | tf_op jit(solution)/shard_map/ppermute | solution.py:752
  72.8 23.5 %collective-permute-start.13 = (bf16[2,3,3,128,256]{4,3,2,1,0:T(8,128)(2,1)}, bf16[2,3,3,128,256]{4,3,2,1,0:T(8,128)(2,1)}, u32[]{:S(2)}, u32[]{:S(2)}) collective-permute-start(bf16[2,3,3,128,256]{4,3,2,1,0:T(8,128)(2,1)} %collective-permute-done.12.refs_2_), channel_id=1, source_target_pairs={{0,4},{4,0},{8,12},{12,8},{16,20},{20,16},{24,28},{28,24},{1,5},{5... | collective-permute-start | bytes 3538952 | tf_op jit(solution)/shard_map/ppermute | solution.py:752
  73.3 27.4 %collective-permute-start.7 = (bf16[128,1024]{1,0:T(8,128)(2,1)S(1)}, bf16[128,1024]{1,0:T(8,128)(2,1)S(1)}, u32[]{:S(2)}, u32[]{:S(2)}) collective-permute-start(bf16[128,1024]{1,0:T(8,128)(2,1)S(1)} %get-tuple-element.356), channel_id=1, source_target_pairs={{0,1},{1,2},{2,3},{3,0},{4,5},{5,6},{6,7},{7,4},{8,9},{9,10},{10,1... | collective-permute-start | bytes 786440 | tf_op jit(solution)/shard_map/ppermute | solution.py:764
  80.6 20.1 %collective-permute-start.8 = (bf16[128,1024]{1,0:T(8,128)(2,1)S(1)}, bf16[128,1024]{1,0:T(8,128)(2,1)S(1)}, u32[]{:S(2)}, u32[]{:S(2)}) collective-permute-start(bf16[128,1024]{1,0:T(8,128)(2,1)S(1)} %get-tuple-element.355), channel_id=1, source_target_pairs={{0,2},{1,3},{2,0},{3,1},{4,6},{5,7},{6,4},{7,5},{8,10},{9,11},{10,... | collective-permute-start | bytes 786440 | tf_op jit(solution)/shard_map/ppermute | solution.py:764
  86.1 18.3 %collective-permute-start.9 = (bf16[128,1024]{1,0:T(8,128)(2,1)S(1)}, bf16[128,1024]{1,0:T(8,128)(2,1)S(1)}, u32[]{:S(2)}, u32[]{:S(2)}) collective-permute-start(bf16[128,1024]{1,0:T(8,128)(2,1)S(1)} %get-tuple-element.354), channel_id=1, source_target_pairs={{0,3},{1,0},{2,1},{3,2},{4,7},{5,4},{6,5},{7,6},{8,11},{9,8},{10,9... | collective-permute-start | bytes 786440 | tf_op jit(solution)/shard_map/ppermute | solution.py:764
  99.2 24.8 %collective-permute-start.18 = (bf16[2,3,160,1024]{3,2,1,0:T(8,128)(2,1)}, bf16[2,3,160,1024]{3,2,1,0:T(8,128)(2,1)S(1)}, u32[]{:S(2)}, u32[]{:S(2)}) collective-permute-start(bf16[2,3,160,1024]{3,2,1,0:T(8,128)(2,1)} %pack.9.refs_1_), channel_id=1, source_target_pairs={{0,16},{4,12},{8,24},{12,4},{16,0},{20,28},{24,8},{28,20},{1,17},{... | collective-permute-start | bytes 5898248 | tf_op jit(solution)/shard_map/ppermute | solution.py:752
  100.7 27.3 %collective-permute-start.17 = (bf16[2,3,160,1024]{3,2,1,0:T(8,128)(2,1)}, bf16[2,3,160,1024]{3,2,1,0:T(8,128)(2,1)S(1)}, u32[]{:S(2)}, u32[]{:S(2)}) collective-permute-start(bf16[2,3,160,1024]{3,2,1,0:T(8,128)(2,1)} %pack.9.refs_1_), channel_id=1, source_target_pairs={{0,4},{4,0},{8,12},{12,8},{16,20},{20,16},{24,28},{28,24},{1,5},{5... | collective-permute-start | bytes 5898248 | tf_op jit(solution)/shard_map/ppermute | solution.py:752
  124.0 4.1 collective-permute-start.19
  124.0 12.0 %collective-permute-start.14 = (bf16[128,1024]{1,0:T(8,128)(2,1)S(1)}, bf16[128,1024]{1,0:T(8,128)(2,1)S(1)}, u32[]{:S(2)}, u32[]{:S(2)}) collective-permute-start(bf16[128,1024]{1,0:T(8,128)(2,1)S(1)} %get-tuple-element.156), channel_id=1, source_target_pairs={{0,1},{1,2},{2,3},{3,0},{4,5},{5,6},{6,7},{7,4},{8,9},{9,10},{10,1... | collective-permute-start | bytes 786440 | tf_op jit(solution)/shard_map/ppermute | solution.py:764
  124.0 21.4 %collective-permute-start.15 = (bf16[128,1024]{1,0:T(8,128)(2,1)S(1)}, bf16[128,1024]{1,0:T(8,128)(2,1)S(1)}, u32[]{:S(2)}, u32[]{:S(2)}) collective-permute-start(bf16[128,1024]{1,0:T(8,128)(2,1)S(1)} %get-tuple-element.156), channel_id=1, source_target_pairs={{0,2},{1,3},{2,0},{3,1},{4,6},{5,7},{6,4},{7,5},{8,10},{9,11},{10,... | collective-permute-start | bytes 786440 | tf_op jit(solution)/shard_map/ppermute | solution.py:764
  124.6 20.8 %collective-permute-start.16 = (bf16[128,1024]{1,0:T(8,128)(2,1)S(1)}, bf16[128,1024]{1,0:T(8,128)(2,1)S(1)}, u32[]{:S(2)}, u32[]{:S(2)}) collective-permute-start(bf16[128,1024]{1,0:T(8,128)(2,1)S(1)} %get-tuple-element.156), channel_id=1, source_target_pairs={{0,3},{1,0},{2,1},{3,2},{4,7},{5,4},{6,5},{7,6},{8,11},{9,8},{10,9... | collective-permute-start | bytes 786440 | tf_op jit(solution)/shard_map/ppermute | solution.py:764
  148.2 12.2 %collective-permute-start.20 = (bf16[3,128,1024]{2,1,0:T(8,128)(2,1)}, bf16[3,128,1024]{2,1,0:T(8,128)(2,1)S(1)}, u32[]{:S(2)}, u32[]{:S(2)}) collective-permute-start(bf16[3,128,1024]{2,1,0:T(8,128)(2,1)} %pack.10.refs_0_), channel_id=1, source_target_pairs={{0,8},{4,20},{8,0},{12,28},{16,24},{20,4},{24,16},{28,12},{1,9},{5... | collective-permute-start | bytes 2359304 | tf_op jit(solution)/shard_map/ppermute | solution.py:752
  164.1 2.7 collective-permute-start.22
  164.1 4.2 collective-permute-start.21
  165.2 22.7 %collective-permute-start.26 = (bf16[2,3,128,1024]{3,2,1,0:T(8,128)(2,1)}, bf16[2,3,128,1024]{3,2,1,0:T(8,128)(2,1)S(1)}, u32[]{:S(2)}, u32[]{:S(2)}) collective-permute-start(bf16[2,3,128,1024]{3,2,1,0:T(8,128)(2,1)} %pack.11.refs_1_), channel_id=1, source_target_pairs={{0,16},{4,12},{8,24},{12,4},{16,0},{20,28},{24,8},{28,20},{1,17},{... | collective-permute-start | bytes 4718600 | tf_op jit(solution)/shard_map/ppermute | solution.py:752
  166.7 46.2 %collective-permute-start.27 = (bf16[2,3,128,1024]{3,2,1,0:T(8,128)(2,1)}, bf16[2,3,128,1024]{3,2,1,0:T(8,128)(2,1)}, u32[]{:S(2)}, u32[]{:S(2)}) collective-permute-start(bf16[2,3,128,1024]{3,2,1,0:T(8,128)(2,1)} %pack.11.refs_1_), channel_id=1, source_target_pairs={{0,4},{4,0},{8,12},{12,8},{16,20},{20,16},{24,28},{28,24},{1,5},{5... | collective-permute-start | bytes 4718600 | tf_op jit(solution)/shard_map/ppermute | solution.py:752
  166.8 21.2 %copy-start.29 = (bf16[512,1024]{1,0:T(8,128)(2,1)}, bf16[512,1024]{1,0:T(8,128)(2,1)S(1)}, u32[]{:S(2)}) copy-start(bf16[512,1024]{1,0:T(8,128)(2,1)S(1)} %collective-permute-done.22.refs_1_) | copy-start | bytes 3145732
  188.0 25.0 %collective-permute-start.28 = (bf16[2,3,128,1024]{3,2,1,0:T(8,128)(2,1)S(1)}, bf16[2,3,128,1024]{3,2,1,0:T(8,128)(2,1)}, u32[]{:S(2)}, u32[]{:S(2)}) collective-permute-start(bf16[2,3,128,1024]{3,2,1,0:T(8,128)(2,1)S(1)} %collective-permute-done.26.refs_2_), channel_id=1, source_target_pairs={{0,4},{4,0},{8,12},{12,8},{16,20},{20,16},{24,28},{28,24},{1,5},{5... | collective-permute-start | bytes 4718600 | tf_op jit(solution)/shard_map/ppermute | solution.py:752
  189.1 12.3 %collective-permute-start.23 = (bf16[128,1024]{1,0:T(8,128)(2,1)S(1)}, bf16[128,1024]{1,0:T(8,128)(2,1)S(1)}, u32[]{:S(2)}, u32[]{:S(2)}) collective-permute-start(bf16[128,1024]{1,0:T(8,128)(2,1)S(1)} %get-tuple-element.352), channel_id=1, source_target_pairs={{0,1},{1,2},{2,3},{3,0},{4,5},{5,6},{6,7},{7,4},{8,9},{9,10},{10,1... | collective-permute-start | bytes 786440 | tf_op jit(solution)/shard_map/ppermute | solution.py:764
  194.7 16.5 %collective-permute-start.24 = (bf16[128,1024]{1,0:T(8,128)(2,1)S(1)}, bf16[128,1024]{1,0:T(8,128)(2,1)S(1)}, u32[]{:S(2)}, u32[]{:S(2)}) collective-permute-start(bf16[128,1024]{1,0:T(8,128)(2,1)S(1)} %get-tuple-element.351), channel_id=1, source_target_pairs={{0,2},{1,3},{2,0},{3,1},{4,6},{5,7},{6,4},{7,5},{8,10},{9,11},{10,... | collective-permute-start | bytes 786440 | tf_op jit(solution)/shard_map/ppermute | solution.py:764
  194.7 17.1 %collective-permute-start.25 = (bf16[128,1024]{1,0:T(8,128)(2,1)S(1)}, bf16[128,1024]{1,0:T(8,128)(2,1)S(1)}, u32[]{:S(2)}, u32[]{:S(2)}) collective-permute-start(bf16[128,1024]{1,0:T(8,128)(2,1)S(1)} %get-tuple-element.350), channel_id=1, source_target_pairs={{0,3},{1,0},{2,1},{3,2},{4,7},{5,4},{6,5},{7,6},{8,11},{9,8},{10,9... | collective-permute-start | bytes 786440 | tf_op jit(solution)/shard_map/ppermute | solution.py:764
  211.9 20.6 %collective-permute-start.30 = (bf16[4,512,1024]{2,1,0:T(8,128)(2,1)}, bf16[4,512,1024]{2,1,0:T(8,128)(2,1)}, u32[]{:S(2)}, u32[]{:S(2)}) collective-permute-start(bf16[4,512,1024]{2,1,0:T(8,128)(2,1)} %get-tuple-element.179.act_ref.refs_2_), channel_id=1, source_target_pairs={{0,4},{4,0},{8,12},{12,8},{16,20},{20,16},{24,28},{28,24},{1,5},{5... | collective-permute-start | bytes 12582920 | tf_op jit(solution)/shard_map/ppermute | solution.py:752
  228.7 3.8 collective-permute-start.29
  232.5 10.4 %collective-permute-start.35 = (bf16[512,1024]{1,0:T(8,128)(2,1)S(1)}, bf16[512,1024]{1,0:T(8,128)(2,1)S(1)}, u32[]{:S(2)}, u32[]{:S(2)}) collective-permute-start(bf16[512,1024]{1,0:T(8,128)(2,1)S(1)} %copy-done.31), channel_id=1, source_target_pairs={{0,4},{4,0},{8,12},{12,8},{16,20},{20,16},{24,28},{28,24},{1,5},{5... | collective-permute-start | bytes 3145736 | tf_op jit(solution)/shard_map/ppermute | solution.py:752
  242.9 29.4 %collective-permute-start.34 = (bf16[2,4,128,1024]{3,2,1,0:T(8,128)(2,1)}, bf16[2,4,128,1024]{3,2,1,0:T(8,128)(2,1)S(1)}, u32[]{:S(2)}, u32[]{:S(2)}) collective-permute-start(bf16[2,4,128,1024]{3,2,1,0:T(8,128)(2,1)} %get-tuple-element.192), channel_id=1, source_target_pairs={{0,8},{4,20},{8,0},{12,28},{16,24},{20,4},{24,16},{28,12},{1,9},{5... | collective-permute-start | bytes 6291464 | tf_op jit(solution)/shard_map/ppermute | solution.py:752
  243.6 29.2 %collective-permute-start.31 = (bf16[128,1024]{1,0:T(8,128)(2,1)S(1)}, bf16[128,1024]{1,0:T(8,128)(2,1)S(1)}, u32[]{:S(2)}, u32[]{:S(2)}) collective-permute-start(bf16[128,1024]{1,0:T(8,128)(2,1)S(1)} %get-tuple-element.348), channel_id=1, source_target_pairs={{0,3},{1,0},{2,1},{3,2},{4,7},{5,4},{6,5},{7,6},{8,11},{9,8},{10,9... | collective-permute-start | bytes 786440 | tf_op jit(solution)/shard_map/ppermute | solution.py:764
  252.3 22.5 %collective-permute-start.32 = (bf16[128,1024]{1,0:T(8,128)(2,1)S(1)}, bf16[128,1024]{1,0:T(8,128)(2,1)S(1)}, u32[]{:S(2)}, u32[]{:S(2)}) collective-permute-start(bf16[128,1024]{1,0:T(8,128)(2,1)S(1)} %get-tuple-element.347), channel_id=1, source_target_pairs={{0,2},{1,3},{2,0},{3,1},{4,6},{5,7},{6,4},{7,5},{8,10},{9,11},{10,... | collective-permute-start | bytes 786440 | tf_op jit(solution)/shard_map/ppermute | solution.py:764
  252.3 22.5 %collective-permute-start.33 = (bf16[128,1024]{1,0:T(8,128)(2,1)S(1)}, bf16[128,1024]{1,0:T(8,128)(2,1)S(1)}, u32[]{:S(2)}, u32[]{:S(2)}) collective-permute-start(bf16[128,1024]{1,0:T(8,128)(2,1)S(1)} %get-tuple-element.346), channel_id=1, source_target_pairs={{0,1},{1,2},{2,3},{3,0},{4,5},{5,6},{6,7},{7,4},{8,9},{9,10},{10,1... | collective-permute-start | bytes 786440 | tf_op jit(solution)/shard_map/ppermute | solution.py:764
  271.6 15.9 %collective-permute-start.37 = (bf16[4,512,1024]{2,1,0:T(8,128)(2,1)}, bf16[4,512,1024]{2,1,0:T(8,128)(2,1)}, u32[]{:S(2)}, u32[]{:S(2)}) collective-permute-start(bf16[4,512,1024]{2,1,0:T(8,128)(2,1)} %get-tuple-element.213.refs_2_), channel_id=1, source_target_pairs={{0,4},{4,0},{8,12},{12,8},{16,20},{20,16},{24,28},{28,24},{1,5},{5... | collective-permute-start | bytes 12582920 | tf_op jit(solution)/shard_map/ppermute | solution.py:752
  272.3 15.2 %collective-permute-start.38 = (bf16[512,1024]{1,0:T(8,128)(2,1)}, bf16[512,1024]{1,0:T(8,128)(2,1)S(1)}, u32[]{:S(2)}, u32[]{:S(2)}) collective-permute-start(bf16[512,1024]{1,0:T(8,128)(2,1)} %get-tuple-element.221.mg_ref.refs_4_), channel_id=1, source_target_pairs={{0,4},{4,0},{8,12},{12,8},{16,20},{20,16},{24,28},{28,24},{1,5},{5... | collective-permute-start | bytes 3145736 | tf_op jit(solution)/shard_map/ppermute | solution.py:752
  272.8 27.6 %collective-permute-start.36 = (bf16[4,128,1024]{2,1,0:T(8,128)(2,1)S(1)}, bf16[4,128,1024]{2,1,0:T(8,128)(2,1)}, u32[]{:S(2)}, u32[]{:S(2)}) collective-permute-start(bf16[4,128,1024]{2,1,0:T(8,128)(2,1)S(1)} %fusion.1), channel_id=1, source_target_pairs={{0,16},{4,12},{8,24},{12,4},{16,0},{20,28},{24,8},{28,20},{1,17},{... | collective-permute-start | bytes 3145736 | tf_op jit(solution)/shard_map/ppermute | solution.py:752
  303.3 60.9 %collective-permute-start.42 = (bf16[2,4,128,1280]{3,2,1,0:T(8,128)(2,1)}, bf16[2,4,128,1280]{3,2,1,0:T(8,128)(2,1)}, u32[]{:S(2)}, u32[]{:S(2)}) collective-permute-start(bf16[2,4,128,1280]{3,2,1,0:T(8,128)(2,1)} %get-tuple-element.225), channel_id=1, source_target_pairs={{0,8},{4,20},{8,0},{12,28},{16,24},{20,4},{24,16},{28,12},{1,9},{5... | collective-permute-start | bytes 7864328 | tf_op jit(solution)/shard_map/ppermute | solution.py:752
  315.8 51.0 %collective-permute-start.47 = (bf16[4,512,768]{2,1,0:T(8,128)(2,1)}, bf16[4,512,768]{2,1,0:T(8,128)(2,1)}, u32[]{:S(2)}, u32[]{:S(2)}) collective-permute-start(bf16[4,512,768]{2,1,0:T(8,128)(2,1)} %get-tuple-element.233.pg_ref.refs_2_), channel_id=1, source_target_pairs={{0,4},{4,0},{8,12},{12,8},{16,20},{20,16},{24,28},{28,24},{1,5},{5... | collective-permute-start | bytes 9437192 | tf_op jit(solution)/shard_map/ppermute | solution.py:752
  319.5 19.8 %collective-permute-start.43 = (bf16[128,1024]{1,0:T(8,128)(2,1)}, bf16[128,1024]{1,0:T(8,128)(2,1)}, u32[]{:S(2)}, u32[]{:S(2)}) collective-permute-start(bf16[128,1024]{1,0:T(8,128)(2,1)} %get-tuple-element.345), channel_id=1, source_target_pairs={{0,3},{1,0},{2,1},{3,2},{4,7},{5,4},{6,5},{7,6},{8,11},{9,8},{10,9... | collective-permute-start | bytes 786440 | tf_op jit(solution)/shard_map/ppermute | solution.py:764
  324.2 23.9 %collective-permute-start.44 = (bf16[128,1024]{1,0:T(8,128)(2,1)}, bf16[128,1024]{1,0:T(8,128)(2,1)}, u32[]{:S(2)}, u32[]{:S(2)}) collective-permute-start(bf16[128,1024]{1,0:T(8,128)(2,1)} %get-tuple-element.344), channel_id=1, source_target_pairs={{0,2},{1,3},{2,0},{3,1},{4,6},{5,7},{6,4},{7,5},{8,10},{9,11},{10,... | collective-permute-start | bytes 786440 | tf_op jit(solution)/shard_map/ppermute | solution.py:764
  324.2 23.9 %collective-permute-start.45 = (bf16[128,1024]{1,0:T(8,128)(2,1)}, bf16[128,1024]{1,0:T(8,128)(2,1)}, u32[]{:S(2)}, u32[]{:S(2)}) collective-permute-start(bf16[128,1024]{1,0:T(8,128)(2,1)} %get-tuple-element.343), channel_id=1, source_target_pairs={{0,1},{1,2},{2,3},{3,0},{4,5},{5,6},{6,7},{7,4},{8,9},{9,10},{10,1... | collective-permute-start | bytes 786440 | tf_op jit(solution)/shard_map/ppermute | solution.py:764
  334.8 25.3 %copy-start.6 = (f32[128,1024]{1,0:T(8,128)S(1)}, f32[128,1024]{1,0:T(8,128)}, u32[]{:S(2)}) copy-start(f32[128,1024]{1,0:T(8,128)} %slice_bitcast_fusion.1) | copy-start | bytes 1572868
  337.1 27.1 %copy-start.3 = (bf16[2,4,128,1280]{3,2,1,0:T(8,128)(2,1)S(1)}, bf16[2,4,128,1280]{3,2,1,0:T(8,128)(2,1)}, u32[]{:S(2)}) copy-start(bf16[2,4,128,1280]{3,2,1,0:T(8,128)(2,1)} %get-tuple-element.219) | copy-start | bytes 7864324
  339.3 54.0 %collective-permute-start.39 = (bf16[128,1024]{1,0:T(8,128)(2,1)}, bf16[128,1024]{1,0:T(8,128)(2,1)}, u32[]{:S(2)}, u32[]{:S(2)}) collective-permute-start(bf16[128,1024]{1,0:T(8,128)(2,1)} %get-tuple-element.341), channel_id=1, source_target_pairs={{0,3},{1,0},{2,1},{3,2},{4,7},{5,4},{6,5},{7,6},{8,11},{9,8},{10,9... | collective-permute-start | bytes 786440 | tf_op jit(solution)/shard_map/ppermute | solution.py:764
  348.1 49.2 %collective-permute-start.40 = (bf16[128,1024]{1,0:T(8,128)(2,1)}, bf16[128,1024]{1,0:T(8,128)(2,1)}, u32[]{:S(2)}, u32[]{:S(2)}) collective-permute-start(bf16[128,1024]{1,0:T(8,128)(2,1)} %get-tuple-element.340), channel_id=1, source_target_pairs={{0,2},{1,3},{2,0},{3,1},{4,6},{5,7},{6,4},{7,5},{8,10},{9,11},{10,... | collective-permute-start | bytes 786440 | tf_op jit(solution)/shard_map/ppermute | solution.py:764
  348.1 49.2 %collective-permute-start.41 = (bf16[128,1024]{1,0:T(8,128)(2,1)}, bf16[128,1024]{1,0:T(8,128)(2,1)}, u32[]{:S(2)}, u32[]{:S(2)}) collective-permute-start(bf16[128,1024]{1,0:T(8,128)(2,1)} %get-tuple-element.339), channel_id=1, source_target_pairs={{0,1},{1,2},{2,3},{3,0},{4,5},{5,6},{6,7},{7,4},{8,9},{9,10},{10,1... | collective-permute-start | bytes 786440 | tf_op jit(solution)/shard_map/ppermute | solution.py:764
  365.8 24.4 %copy-start.4 = (bf16[2,4,128,1280]{3,2,1,0:T(8,128)(2,1)S(1)}, bf16[2,4,128,1280]{3,2,1,0:T(8,128)(2,1)}, u32[]{:S(2)}) copy-start(bf16[2,4,128,1280]{3,2,1,0:T(8,128)(2,1)} %get-tuple-element.219) | copy-start | bytes 7864324
  365.8 24.4 %collective-permute-start.46 = (bf16[4,128,1280]{2,1,0:T(8,128)(2,1)S(1)}, bf16[4,128,1280]{2,1,0:T(8,128)(2,1)}, u32[]{:S(2)}, u32[]{:S(2)}) collective-permute-start(bf16[4,128,1280]{2,1,0:T(8,128)(2,1)S(1)} %fusion), channel_id=1, source_target_pairs={{0,16},{4,12},{8,24},{12,4},{16,0},{20,28},{24,8},{28,20},{1,17},{... | collective-permute-start | bytes 3932168 | tf_op jit(solution)/shard_map/ppermute | solution.py:752
  374.9 47.8 %collective-permute-start.48 = (bf16[2,4,128,768]{3,2,1,0:T(8,128)(2,1)}, bf16[2,4,128,768]{3,2,1,0:T(8,128)(2,1)}, u32[]{:S(2)}, u32[]{:S(2)}) collective-permute-start(bf16[2,4,128,768]{3,2,1,0:T(8,128)(2,1)} %get-tuple-element.248), channel_id=1, source_target_pairs={{0,8},{4,20},{8,0},{12,28},{16,24},{20,4},{24,16},{28,12},{1,9},{5... | collective-permute-start | bytes 4718600 | tf_op jit(solution)/shard_map/ppermute | solution.py:752
  393.3 33.1 %collective-permute-start.50 = (bf16[128,1280]{1,0:T(8,128)(2,1)}, bf16[128,1280]{1,0:T(8,128)(2,1)}, u32[]{:S(2)}, u32[]{:S(2)}) collective-permute-start(bf16[128,1280]{1,0:T(8,128)(2,1)} %get-tuple-element.338), channel_id=1, source_target_pairs={{0,3},{1,0},{2,1},{3,2},{4,7},{5,4},{6,5},{7,6},{8,11},{9,8},{10,9... | collective-permute-start | bytes 983048 | tf_op jit(solution)/shard_map/ppermute | solution.py:764
  393.3 33.1 %collective-permute-start.51 = (bf16[128,1280]{1,0:T(8,128)(2,1)}, bf16[128,1280]{1,0:T(8,128)(2,1)}, u32[]{:S(2)}, u32[]{:S(2)}) collective-permute-start(bf16[128,1280]{1,0:T(8,128)(2,1)} %get-tuple-element.337), channel_id=1, source_target_pairs={{0,2},{1,3},{2,0},{3,1},{4,6},{5,7},{6,4},{7,5},{8,10},{9,11},{10,... | collective-permute-start | bytes 983048 | tf_op jit(solution)/shard_map/ppermute | solution.py:764
  397.3 29.2 %collective-permute-start.52 = (bf16[128,1280]{1,0:T(8,128)(2,1)}, bf16[128,1280]{1,0:T(8,128)(2,1)}, u32[]{:S(2)}, u32[]{:S(2)}) collective-permute-start(bf16[128,1280]{1,0:T(8,128)(2,1)} %get-tuple-element.336), channel_id=1, source_target_pairs={{0,1},{1,2},{2,3},{3,0},{4,5},{5,6},{6,7},{7,4},{8,9},{9,10},{10,1... | collective-permute-start | bytes 983048 | tf_op jit(solution)/shard_map/ppermute | solution.py:764
  398.7 24.0 %all-to-all-start = ((f32[32,1,418]{2,1,0:T(1,128)}), f32[32,1,418]{2,1,0:T(1,128)S(1)}, u32[]{:S(2)}, u32[]{:S(2)}) async-start(f32[32,1,418]{2,1,0:T(1,128)} %copy.93), calls=%async_computation | async-start | bytes 131072 | tf_op jit(solution)/shard_map/all_to_all | solution.py:935
  424.9 12.2 %collective-permute-start.49 = (bf16[4,128,768]{2,1,0:T(8,128)(2,1)}, bf16[4,128,768]{2,1,0:T(8,128)(2,1)S(1)}, u32[]{:S(2)}, u32[]{:S(2)}) collective-permute-start(bf16[4,128,768]{2,1,0:T(8,128)(2,1)} %fusion.2), channel_id=1, source_target_pairs={{0,16},{4,12},{8,24},{12,4},{16,0},{20,28},{24,8},{28,20},{1,17},{... | collective-permute-start | bytes 2359304 | tf_op jit(solution)/shard_map/ppermute | solution.py:752
  438.6 7.1 %collective-permute-start.53 = (bf16[128,768]{1,0:T(8,128)(2,1)S(1)}, bf16[128,768]{1,0:T(8,128)(2,1)S(1)}, u32[]{:S(2)}, u32[]{:S(2)}) collective-permute-start(bf16[128,768]{1,0:T(8,128)(2,1)S(1)} %get-tuple-element.358), channel_id=1, source_target_pairs={{0,3},{1,0},{2,1},{3,2},{4,7},{5,4},{6,5},{7,6},{8,11},{9,8},{10,9... | collective-permute-start | bytes 589832 | tf_op jit(solution)/shard_map/ppermute | solution.py:764
  439.6 17.5 %collective-permute-start.54 = (bf16[128,768]{1,0:T(8,128)(2,1)S(1)}, bf16[128,768]{1,0:T(8,128)(2,1)S(1)}, u32[]{:S(2)}, u32[]{:S(2)}) collective-permute-start(bf16[128,768]{1,0:T(8,128)(2,1)S(1)} %get-tuple-element.360), channel_id=1, source_target_pairs={{0,2},{1,3},{2,0},{3,1},{4,6},{5,7},{6,4},{7,5},{8,10},{9,11},{10,... | collective-permute-start | bytes 589832 | tf_op jit(solution)/shard_map/ppermute | solution.py:764
  440.8 16.2 %collective-permute-start.55 = (bf16[128,768]{1,0:T(8,128)(2,1)S(1)}, bf16[128,768]{1,0:T(8,128)(2,1)S(1)}, u32[]{:S(2)}, u32[]{:S(2)}) collective-permute-start(bf16[128,768]{1,0:T(8,128)(2,1)S(1)} %get-tuple-element.359), channel_id=1, source_target_pairs={{0,1},{1,2},{2,3},{3,0},{4,5},{5,6},{6,7},{7,4},{8,9},{9,10},{10,1... | collective-permute-start | bytes 589832 | tf_op jit(solution)/shard_map/ppermute | solution.py:764
  (43 other events, 330.7 us)
